TPU v7x, 32 devices: a whole 2x2x4 slice. The times are simulated.
32 devices in a mesh: seq: 4 (over y, x), fsdp: 4 (over z), tensor: 2 (over core).
Axes of the slice: x: 2, y: 2, z: 4, core: 2. Of those that a mesh axis runs over, the one named last changes fastest.
Arguments:
- inputs: bfloat16 [8192, 2560], P(('seq', 'fsdp')), may hold values from -6 to 6
- cotangent: bfloat16 [8192, 2560], P(('seq', 'fsdp')), may hold values from -6 to 6
- gain_attn: bfloat16 [2560], P('fsdp'), may hold values from 0.099609375 to 1.8984375
- gain_ffn: bfloat16 [2560], P('fsdp'), may hold values from 0.099609375 to 1.8984375
- w_query: bfloat16 [2560, 2560], P('fsdp', 'tensor'), may hold values from -0.125 to 0.125
- w_key: bfloat16 [2560, 256], P('fsdp'), may hold values from -0.125 to 0.125
- w_value: bfloat16 [2560, 256], P('fsdp'), may hold values from -0.125 to 0.125
- w_out: bfloat16 [2560, 2560], P('tensor', 'fsdp'), may hold values from -3.5 to 3.5
- w_gate: bfloat16 [2560, 7680], P('fsdp', 'tensor'), may hold values from -0.125 to 0.125
- w_up: bfloat16 [2560, 7680], P('fsdp', 'tensor'), may hold values from -0.125 to 0.125
- w_down: bfloat16 [7680, 2560], P('tensor', 'fsdp'), may hold values from -0.0625 to 0.0625
Outputs:
- layer_out: bfloat16 [8192, 2560], P(('seq', 'fsdp'))
- grad_input: float32 [8192, 2560], P(('seq', 'fsdp'))
- grad_gain_attn: float32 [2560], P('fsdp')
- grad_gain_ffn: float32 [2560], P('fsdp')
- grad_w_query: float32 [2560, 2560], P('fsdp', 'tensor')
- grad_w_key: float32 [2560, 256], P('fsdp')
- grad_w_value: float32 [2560, 256], P('fsdp')
- grad_w_out: float32 [2560, 2560], P('tensor', 'fsdp')
- grad_w_gate: float32 [2560, 7680], P('fsdp', 'tensor')
- grad_w_up: float32 [2560, 7680], P('fsdp', 'tensor')
- grad_w_down: float32 [7680, 2560], P('tensor', 'fsdp')
All inputs are finite; a program needn't handle non-finite values.
Results may differ from a plain program's by a relative error of at most 0.014.
Values may be sent and summed in bfloat16 or wider, within the bound.
A program may use at most 320 MiB of HBM per device.

v0:
```python
import jax
import jax.numpy as jnp
from jax import lax
from jax.sharding import PartitionSpec as P

WINDOW = 2048


EPSILON = 1e-06


def from_behind(value, axis, steps):
    count = lax.axis_size(axis)
    leading, last = (max(0, -steps), min(count, count - steps))
    return lax.ppermute(value, axis, [(source, source + steps) for source in range(leading, last)])


def rms_norm(values, gain):
    return values * lax.rsqrt(jnp.mean(values * values, axis=-1, keepdims=True) + EPSILON) * gain


def rotate(values, angles, sign):
    half = angles.shape[-1]
    cosine = jnp.cos(angles)
    sine = sign * jnp.sin(angles)
    first_part = values[..., :half]
    second_part = values[..., half : 2 * half]
    return jnp.concatenate(
        [
            first_part * cosine - second_part * sine,
            second_part * cosine + first_part * sine,
            values[..., 2 * half :],
        ],
        axis=-1,
    )


def tensor_total(values):
    return lax.psum(values, "tensor")


def times_transpose(left, right):
    return lax.dot_general(
        left, right, (((1,), (1,)), ((), ())), preferred_element_type=jnp.float32
    )


def rows_product(left, right):
    return lax.dot_general(
        left, right, (((0,), (0,)), ((), ())), preferred_element_type=jnp.float32
    )


def gated_unit(gate_pre, up_proj):
    return jax.nn.gelu(gate_pre) * up_proj


def local(
    inputs, cotangent, gain_attn, gain_ffn, w_query, w_key, w_value, w_out, w_gate, w_up, w_down
):
    token_rows, width = inputs.shape
    head_size = w_key.shape[1]
    heads_here = w_query.shape[1] // head_size
    fsdp_count = lax.axis_size("fsdp")
    block_len = token_rows * fsdp_count
    window = WINDOW
    key_span = token_rows + window
    fsdp_at = lax.axis_index("fsdp")
    first_pos = lax.axis_index("seq") * block_len + fsdp_at * token_rows
    scale = head_size ** (-0.5)
    rot_half = head_size // 4
    frequency = 10000.0 ** (-(jnp.arange(rot_half, dtype=jnp.float32) * 2.0) / (2 * rot_half))
    angles = (first_pos + jnp.arange(token_rows, dtype=jnp.int32)).astype(jnp.float32)[
        :, None
    ] * frequency[None, :]
    gathered_gain_attn, gathered_gain_ffn, query_weight, key_weight, value_weight, out_weight = (
        lax.all_gather(gain_attn, "fsdp", axis=0, tiled=True),
        lax.all_gather(gain_ffn, "fsdp", axis=0, tiled=True),
        lax.all_gather(w_query, "fsdp", axis=0, tiled=True),
        lax.all_gather(w_key, "fsdp", axis=0, tiled=True),
        lax.all_gather(w_value, "fsdp", axis=0, tiled=True),
        lax.all_gather(w_out, "fsdp", axis=1, tiled=True),
    )
    source = inputs.astype(jnp.float32)
    gain_one = gathered_gain_attn.astype(jnp.float32)
    normed_attn = rms_norm(source, gain_one).astype(jnp.bfloat16)
    query_proj = jnp.dot(normed_attn, query_weight, preferred_element_type=jnp.float32).reshape(
        token_rows, heads_here, head_size
    )
    queries = (rotate(query_proj, angles[:, None, :], 1.0) * scale).astype(jnp.bfloat16)
    key_rot = rotate(
        jnp.dot(normed_attn, key_weight, preferred_element_type=jnp.float32), angles, 1.0
    )
    value_proj = jnp.dot(normed_attn, value_weight, preferred_element_type=jnp.float32)
    local_pairs = jnp.concatenate([key_rot, value_proj], axis=1).astype(jnp.bfloat16)
    block_pairs = lax.all_gather(local_pairs, "fsdp", axis=0, tiled=True)
    earlier = from_behind(block_pairs, "seq", 1)
    window_pairs = lax.dynamic_slice_in_dim(
        jnp.concatenate([earlier, block_pairs], axis=0), fsdp_at * token_rows, key_span, 0
    )
    key_rows = window_pairs[:, :head_size]
    value_rows = window_pairs[:, head_size:]
    query_at = jnp.arange(token_rows, dtype=jnp.int32)[:, None]
    key_at = jnp.arange(key_span, dtype=jnp.int32)[None, :]
    allowed = (
        (key_at > query_at) & (key_at <= query_at + window) & (first_pos - window + key_at >= 0)
    )

    def score_all():
        raw_scores = jnp.einsum(
            "rhd,kd->hrk", queries, key_rows, preferred_element_type=jnp.float32
        )
        return jnp.where(allowed[None], raw_scores, -1e30)

    scores = score_all()
    row_max = jnp.max(scores, axis=-1, keepdims=True)
    expon = jnp.exp(scores - row_max)
    denominator = jnp.sum(expon, axis=-1, keepdims=True)
    probability = expon / denominator
    log_total = row_max + jnp.log(denominator)
    attended = jnp.einsum(
        "hrk,kd->rhd",
        probability.astype(jnp.bfloat16),
        value_rows,
        preferred_element_type=jnp.float32,
    )
    head_outputs = attended.reshape(token_rows, heads_here * head_size).astype(jnp.bfloat16)
    hidden_in = source + tensor_total(
        jnp.dot(head_outputs, out_weight, preferred_element_type=jnp.float32)
    )
    gain_two = gathered_gain_ffn.astype(jnp.float32)
    normed_ffn = rms_norm(hidden_in, gain_two).astype(jnp.bfloat16)
    gate_weight, up_weight, down_weight = (
        lax.all_gather(w_gate, "fsdp", axis=0, tiled=True),
        lax.all_gather(w_up, "fsdp", axis=0, tiled=True),
        lax.all_gather(w_down, "fsdp", axis=1, tiled=True),
    )
    gate_pre = jnp.dot(normed_ffn, gate_weight, preferred_element_type=jnp.float32)
    up_proj = jnp.dot(normed_ffn, up_weight, preferred_element_type=jnp.float32)
    activation = gated_unit(gate_pre, up_proj).astype(jnp.bfloat16)
    ffn_out = tensor_total(jnp.dot(activation, down_weight, preferred_element_type=jnp.float32))
    layer_out = (hidden_in + ffn_out).astype(jnp.bfloat16)
    grad_out = cotangent.astype(jnp.float32)
    grad_activation = times_transpose(cotangent, down_weight)
    gated_pull = jax.vjp(gated_unit, gate_pre, up_proj)[1]
    grad_gate_full, grad_up_full = gated_pull(grad_activation)
    grad_gate = grad_gate_full.astype(jnp.bfloat16)
    grad_up = grad_up_full.astype(jnp.bfloat16)
    grad_normed_ffn = tensor_total(
        times_transpose(grad_gate, gate_weight) + times_transpose(grad_up, up_weight)
    )
    paired_grads = jnp.concatenate([grad_gate, grad_up], axis=1)
    hidden_here = gate_weight.shape[1]
    normed_cols, cotangent_cols = (
        lax.all_to_all(normed_ffn, "fsdp", split_axis=1, concat_axis=0, tiled=True),
        lax.all_to_all(cotangent, "fsdp", split_axis=1, concat_axis=0, tiled=True),
    )
    ffn_shard = jnp.concatenate(
        [
            rows_product(normed_cols, lax.all_gather(paired_grads, "fsdp", axis=0, tiled=True)),
            rows_product(cotangent_cols, lax.all_gather(activation, "fsdp", axis=0, tiled=True)),
        ],
        axis=1,
    )
    norm_pull_two = jax.vjp(rms_norm, hidden_in, gain_two)[1]
    grad_hidden_ffn, grad_gain_two = norm_pull_two(grad_normed_ffn)
    grad_hidden = grad_out + grad_hidden_ffn
    grad_attn_out = grad_hidden.astype(jnp.bfloat16)
    grad_heads = (
        times_transpose(grad_attn_out, out_weight)
        .reshape(token_rows, heads_here, head_size)
        .astype(jnp.bfloat16)
    )
    out_term = rows_product(head_outputs, grad_attn_out)
    probability_again = jnp.exp(score_all() - log_total)
    grad_probability = jnp.einsum(
        "rhd,kd->hrk", grad_heads, value_rows, preferred_element_type=jnp.float32
    )
    inner = jnp.sum(probability_again * grad_probability, axis=-1, keepdims=True)
    grad_scores = (probability_again * (grad_probability - inner)).astype(jnp.bfloat16)
    grad_queries = jnp.einsum(
        "hrk,kd->rhd", grad_scores, key_rows, preferred_element_type=jnp.float32
    )
    grad_query_proj = (
        rotate(grad_queries * scale, angles[:, None, :], -1.0)
        .astype(jnp.bfloat16)
        .reshape(token_rows, heads_here * head_size)
    )
    grad_keys = jnp.einsum("hrk,rhd->kd", grad_scores, queries, preferred_element_type=jnp.float32)
    grad_values = jnp.einsum(
        "hrk,rhd->kd",
        probability_again.astype(jnp.bfloat16),
        grad_heads,
        preferred_element_type=jnp.float32,
    )
    grad_pairs = jnp.concatenate([grad_keys, grad_values], axis=1)
    placed = lax.dynamic_update_slice_in_dim(
        jnp.zeros((window + block_len, 2 * head_size), jnp.float32),
        grad_pairs,
        fsdp_at * token_rows,
        0,
    )
    returned = from_behind(placed[:window], "seq", -1)
    own_block = placed[window:].at[block_len - window :].add(returned)
    pair_grads = tensor_total(lax.psum_scatter(own_block, "fsdp", scatter_dimension=0, tiled=True))
    grad_key_proj = rotate(pair_grads[:, :head_size], angles, -1.0).astype(jnp.bfloat16)
    grad_value_proj = pair_grads[:, head_size:].astype(jnp.bfloat16)
    grad_normed_attn = (
        tensor_total(times_transpose(grad_query_proj, query_weight))
        + times_transpose(grad_key_proj, key_weight)
        + times_transpose(grad_value_proj, value_weight)
    )
    norm_pull_one = jax.vjp(rms_norm, source, gain_one)[1]
    grad_source_attn, grad_gain_one = norm_pull_one(grad_normed_attn)
    grad_input = grad_hidden + grad_source_attn
    query_term = rows_product(normed_attn, grad_query_proj)
    key_term = rows_product(normed_attn, grad_key_proj)
    value_term = rows_product(normed_attn, grad_value_proj)
    gain_one_shard, gain_two_shard, query_shard, key_shard, value_shard, out_shard = (
        lax.psum_scatter(grad_gain_one, "fsdp", scatter_dimension=0, tiled=True),
        lax.psum_scatter(grad_gain_two, "fsdp", scatter_dimension=0, tiled=True),
        lax.psum_scatter(query_term, "fsdp", scatter_dimension=0, tiled=True),
        lax.psum_scatter(key_term, "fsdp", scatter_dimension=0, tiled=True),
        lax.psum_scatter(value_term, "fsdp", scatter_dimension=0, tiled=True),
        lax.psum_scatter(out_term, "fsdp", scatter_dimension=1, tiled=True),
    )
    gain_one_sum, gain_two_sum, query_sum, key_sum, value_sum, out_sum, ffn_sum = lax.psum(
        (gain_one_shard, gain_two_shard, query_shard, key_shard, value_shard, out_shard, ffn_shard),
        "seq",
    )
    gate_grad = ffn_sum[:, :hidden_here]
    up_grad = ffn_sum[:, hidden_here : 2 * hidden_here]
    down_grad = ffn_sum[:, 2 * hidden_here :].T
    return (
        layer_out,
        grad_input,
        gain_one_sum,
        gain_two_sum,
        query_sum,
        key_sum,
        value_sum,
        out_sum,
        gate_grad,
        up_grad,
        down_grad,
    )


def solution(mesh):
    in_specs = (
        P(("seq", "fsdp"), None),
        P(("seq", "fsdp"), None),
        P("fsdp"),
        P("fsdp"),
        P("fsdp", "tensor"),
        P("fsdp", None),
        P("fsdp", None),
        P("tensor", "fsdp"),
        P("fsdp", "tensor"),
        P("fsdp", "tensor"),
        P("tensor", "fsdp"),
    )
    out_specs = (
        P(("seq", "fsdp"), None),
        P(("seq", "fsdp"), None),
        P("fsdp"),
        P("fsdp"),
        P("fsdp", "tensor"),
        P("fsdp", None),
        P("fsdp", None),
        P("tensor", "fsdp"),
        P("fsdp", "tensor"),
        P("fsdp", "tensor"),
        P("tensor", "fsdp"),
    )
    return jax.shard_map(local, mesh=mesh, in_specs=in_specs, out_specs=out_specs, check_vma=False)
```

profile of v0, /device:TPU:9, one launch (start us, length us, event | category | flops | bytes accessed | tf_op | source)
XLA Modules:
  0.0 3948.4 jit_solution(4363243627819187403)
XLA Ops:
  47.0 28.9 all-gather.15.cloned.1.call-done
  79.8 43.5 %all-gather.17.cloned.1.call-done = bf16[2048,512]{0,1:T(8,128)(2,1)} async-done(((bf16[512,512]{0,1:T(8,128)(2,1)}), bf16[2048,512]{0,1:T(8,128)(2,1)}) %all-gather.17.cloned.1.call-update) | async-done | bytes 2097168 | tf_op jit(solution)/shard_map/all_gather | solution.py:96
  131.7 39.0 collective-permute-done
  174.7 67.5 %all-gather.19.cloned.1.call-done = bf16[2560,1280]{1,0:T(8,128)(2,1)} async-done(((bf16[640,1280]{1,0:T(8,128)(2,1)}), bf16[2560,1280]{1,0:T(8,128)(2,1)}) %all-gather.19.cloned.1.call-update) | async-done | bytes 6553616 | tf_op jit(solution)/shard_map/all_gather | solution.py:79
  300.2 61.3 %all-gather.21.cloned.1.call-done = bf16[1280,2560]{1,0:T(8,128)(2,1)} async-done(((bf16[1280,640]{1,0:T(8,128)(2,1)}), bf16[1280,2560]{1,0:T(8,128)(2,1)}) %all-gather.21.cloned.1.call-update) | async-done | bytes 6553616 | tf_op jit(solution)/shard_map/all_gather | solution.py:82
  408.9 329.2 %all-gather.23.cloned.1.call-done = bf16[2560,3840]{1,0:T(8,128)(2,1)} async-done(((bf16[640,3840]{1,0:T(8,128)(2,1)}), bf16[2560,3840]{1,0:T(8,128)(2,1)}) %all-gather.23.cloned.1.call-update) | async-done | bytes 19660816 | tf_op jit(solution)/shard_map/all_gather | solution.py:134
  755.0 318.9 %all-gather.25.cloned.1.call-done = bf16[2560,3840]{1,0:T(8,128)(2,1)} async-done(((bf16[640,3840]{1,0:T(8,128)(2,1)}), bf16[2560,3840]{1,0:T(8,128)(2,1)}) %all-gather.25.cloned.1.call-update) | async-done | bytes 19660816 | tf_op jit(solution)/shard_map/all_gather | solution.py:135
  1090.9 318.9 %all-gather.27.cloned.1.call-done = bf16[3840,2560]{1,0:T(8,128)(2,1)} async-done(((bf16[3840,640]{1,0:T(8,128)(2,1)}), bf16[3840,2560]{1,0:T(8,128)(2,1)}) %all-gather.27.cloned.1.call-update) | async-done | bytes 19660816 | tf_op jit(solution)/shard_map/all_gather | solution.py:136
  1409.8 23.1 multiply_convert_fusion
  1468.0 31.9 all-reduce.13.cloned.1.call-done
  1550.7 23.3 fusion.2
  1586.1 92.2 %collective-permute-done.1 = f32[2048,512]{0,1:T(8,128)S(1)} collective-permute-done((f32[2048,512]{0,1:T(8,128)S(1)}, f32[2048,512]{0,1:T(8,128)S(1)}, u32[]{:S(2)}, u32[]{:S(2)}) %collective-permute-start.1) | collective-permute-done | bytes 4194336 | tf_op jit(solution)/shard_map/ppermute | solution.py:15
  1717.6 41.8 %reduce-scatter.6.cloned.1.call-done = f32[512,512]{0,1:T(8,128)} async-done(((f32[2048,512]{0,1:T(8,128)}), f32[512,512]{0,1:T(8,128)}) %reduce-scatter.6.cloned.1.call-update) | async-done | bytes 1048592 | tf_op jit(solution)/shard_map/reduce_scatter | solution.py:205
  1817.7 85.2 %all-to-all-done.1 = bf16[512,4,640]{0,2,1:T(8,128)(2,1)} async-done(((bf16[512,4,640]{0,2,1:T(8,128)(2,1)}), bf16[512,4,640]{0,2,1:T(8,128)(2,1)}, u32[]{:S(2)}, u32[]{:S(2)}) %all-to-all-start.1) | async-done | bytes 2621472 | tf_op jit(solution)/shard_map/all_to_all | solution.py:156
  1921.3 246.7 %all-gather.31.cloned.1.call-done = bf16[2048,3840]{1,0:T(8,128)(2,1)} async-done(((bf16[512,3840]{1,0:T(8,128)(2,1)}), bf16[2048,3840]{1,0:T(8,128)(2,1)}) %all-gather.31.cloned.1.call-update) | async-done | bytes 15728656 | tf_op jit(solution)/shard_map/all_gather | solution.py:161
  2189.3 506.5 %all-gather.29.cloned.1.call-done = bf16[2048,7680]{1,0:T(8,128)(2,1)} async-done(((bf16[512,7680]{1,0:T(8,128)(2,1)}), bf16[2048,7680]{1,0:T(8,128)(2,1)}) %all-gather.29.cloned.1.call-update) | async-done | bytes 31457296 | tf_op jit(solution)/shard_map/all_gather | solution.py:160
  2695.9 28.5 fusion.84
  2724.4 20.8 pad_maximum_fusion
  2745.2 174.4 %reduce-scatter.8.cloned.1.call-done = f32[640,1280]{1,0:T(8,128)} async-done(((f32[2560,1280]{1,0:T(8,128)}), f32[640,1280]{1,0:T(8,128)}) %reduce-scatter.8.cloned.1.call-update) | async-done | bytes 3276816 | tf_op jit(solution)/shard_map/reduce_scatter | solution.py:222
  2919.6 223.7 %reduce-scatter.14.cloned.1.call-done = f32[1280,640]{1,0:T(8,128)} async-done(((f32[1280,2560]{1,0:T(8,128)}), f32[1280,640]{1,0:T(8,128)}) %reduce-scatter.14.cloned.1.call-update) | async-done | bytes 3276816 | tf_op jit(solution)/shard_map/reduce_scatter | solution.py:225
  3143.3 55.0 %reduce-scatter.10.cloned.1.call-done = f32[640,256]{1,0:T(8,128)} async-done(((f32[2560,256]{1,0:T(8,128)}), f32[640,256]{1,0:T(8,128)}) %reduce-scatter.10.cloned.1.call-update) | async-done | bytes 655376 | tf_op jit(solution)/shard_map/reduce_scatter | solution.py:223
  3198.4 54.7 %reduce-scatter.12.cloned.1.call-done = f32[640,256]{1,0:T(8,128)} async-done(((f32[2560,256]{1,0:T(8,128)}), f32[640,256]{1,0:T(8,128)}) %reduce-scatter.12.cloned.1.call-update) | async-done | bytes 655376 | tf_op jit(solution)/shard_map/reduce_scatter | solution.py:224
  3298.9 605.3 %all-reduce.15.cloned.1.call-done = (f32[640,1280]{1,0:T(8,128)}, f32[640,256]{1,0:T(8,128)}, f32[640,256]{1,0:T(8,128)}, f32[1280,640]{1,0:T(8,128)}, f32[640,11520]{1,0:T(8,128)}) async-done(((f32[640,1280]{1,0:T(8,128)}, f32[640,256]{1,0:T(8,128)}, f32[640,256]{1,0:T(8,128)}, f32[1280,640]{1,0:T(8,128)}, f32[640,11520]{1,0:T(8,128)}), (f32[640,1280]{1,0:T(8,128)}, f32[640,256]{1,0:T(8,128)}, ...) | async-done | bytes 37355536 | tf_op jit(solution)/shard_map/psum | solution.py:227
  3904.2 20.5 slice_bitcast_fusion
  (215 shorter events, 492.0 us)
Async XLA Ops:
  7.2 35.4 all-gather.13.cloned.1.call-start
  7.9 67.9 %all-gather.15.cloned.1.call-start = ((), (), s32[]{:S(2)}) async-start(), calls=%async_computation.8 | async-start | bytes 1638400 | tf_op jit(solution)/shard_map/all_gather | solution.py:81
  8.7 114.6 %all-gather.17.cloned.1.call-start = ((), (), s32[]{:S(2)}) async-start(), calls=%async_computation.9 | async-start | bytes 2621440 | tf_op jit(solution)/shard_map/all_gather | solution.py:96
  79.1 163.0 %all-gather.19.cloned.1.call-start = ((), (), s32[]{:S(2)}) async-start(), calls=%async_computation.10 | async-start | bytes 8192000 | tf_op jit(solution)/shard_map/all_gather | solution.py:79
  79.7 281.7 %all-gather.21.cloned.1.call-start = ((), (), s32[]{:S(2)}) async-start(), calls=%async_computation.11 | async-start | bytes 8192000 | tf_op jit(solution)/shard_map/all_gather | solution.py:82
  123.3 47.4 %collective-permute-start = (bf16[2048,512]{0,1:T(8,128)(2,1)}, bf16[2048,512]{0,1:T(8,128)(2,1)}, u32[]{:S(2)}, u32[]{:S(2)}) collective-permute-start(bf16[2048,512]{0,1:T(8,128)(2,1)} %all-gather.17.cloned.1.call-done), channel_id=1, source_target_pairs={{0,8},{8,16},{16,24},{1,9},{9,17},{17,25},{2,10},{10,18},{18,26},{... | collective-permute-start | bytes 6291464 | tf_op jit(solution)/shard_map/ppermute | solution.py:15
  127.7 275.0 %all-reduce.11.cloned.1.call-start = ((), (), s32[]{:S(2)}) async-start(), calls=%async_computation.12 | async-start | bytes 10485760 | tf_op jit(solution)/shard_map/psum | solution.py:39
  370.7 367.3 %all-gather.23.cloned.1.call-start = ((), (), s32[]{:S(2)}) async-start(), calls=%async_computation.13 | async-start | bytes 24576000 | tf_op jit(solution)/shard_map/all_gather | solution.py:134
  371.5 702.5 %all-gather.25.cloned.1.call-start = ((), (), s32[]{:S(2)}) async-start(), calls=%async_computation.14 | async-start | bytes 24576000 | tf_op jit(solution)/shard_map/all_gather | solution.py:135
  372.2 1037.6 %all-gather.27.cloned.1.call-start = ((), (), s32[]{:S(2)}) async-start(), calls=%async_computation.15 | async-start | bytes 24576000 | tf_op jit(solution)/shard_map/all_gather | solution.py:136
  373.0 1127.0 %all-reduce.13.cloned.1.call-start = ((), (), s32[]{:S(2)}) async-start(), calls=%async_computation.16 | async-start | bytes 10485760 | tf_op jit(solution)/shard_map/psum | solution.py:39
  408.8 665.1 %copy-start.8 = (bf16[512,2560]{1,0:T(8,128)(2,1)}, bf16[512,2560]{1,0:T(8,128)(2,1)S(1)}, u32[]{:S(2)}) copy-start(bf16[512,2560]{1,0:T(8,128)(2,1)S(1)} %multiply_convert_fusion.2) | copy-start | bytes 7864324
  1467.9 291.4 %reduce-scatter.6.cloned.1.call-start = ((), (), s32[]{:S(2)}) async-start(), calls=%async_computation.17 | async-start | bytes 5242880 | tf_op jit(solution)/shard_map/reduce_scatter | solution.py:205
  1584.2 94.0 %collective-permute-start.1 = (f32[2048,512]{0,1:T(8,128)S(1)}, f32[2048,512]{0,1:T(8,128)S(1)}, u32[]{:S(2)}, u32[]{:S(2)}) collective-permute-start(f32[2048,512]{0,1:T(8,128)S(1)} %slice.114), channel_id=1, source_target_pairs={{8,0},{16,8},{24,16},{9,1},{17,9},{25,17},{10,2},{18,10},{26,18},{... | collective-permute-start | bytes 12582920 | tf_op jit(solution)/shard_map/ppermute | solution.py:15
  1681.1 127.7 %all-reduce.17.cloned.1.call-start = ((), (), s32[]{:S(2)}) async-start(), calls=%async_computation.25 | async-start | bytes 23068672 | tf_op jit(solution)/shard_map/psum | solution.py:39
  1759.3 408.7 %all-gather.31.cloned.1.call-start = ((), (), s32[]{:S(2)}) async-start(), calls=%async_computation.23 | async-start | bytes 19660800 | tf_op jit(solution)/shard_map/all_gather | solution.py:161
  1760.1 935.8 %all-gather.29.cloned.1.call-start = ((), (), s32[]{:S(2)}) async-start(), calls=%async_computation.22 | async-start | bytes 39321600 | tf_op jit(solution)/shard_map/all_gather | solution.py:160
  1767.2 1152.4 %reduce-scatter.8.cloned.1.call-start = ((), (), s32[]{:S(2)}) async-start(), calls=%async_computation.18 | async-start | bytes 16384000 | tf_op jit(solution)/shard_map/reduce_scatter | solution.py:222
  1780.2 1363.2 %reduce-scatter.14.cloned.1.call-start = ((), (), s32[]{:S(2)}) async-start(), calls=%async_computation.21 | async-start | bytes 16384000 | tf_op jit(solution)/shard_map/reduce_scatter | solution.py:225
  1796.5 106.5 %all-to-all-start.1 = ((bf16[512,4,640]{0,2,1:T(8,128)(2,1)}), bf16[512,4,640]{0,2,1:T(8,128)(2,1)}, u32[]{:S(2)}, u32[]{:S(2)}) async-start(bf16[512,4,640]{0,2,1:T(8,128)(2,1)} %bitcast.105), calls=%async_computation.6 | async-start | bytes 5242880 | tf_op jit(solution)/shard_map/all_to_all | solution.py:156
  1801.9 1396.5 %reduce-scatter.10.cloned.1.call-start = ((), (), s32[]{:S(2)}) async-start(), calls=%async_computation.19 | async-start | bytes 3276800 | tf_op jit(solution)/shard_map/reduce_scatter | solution.py:223
  1902.9 286.4 %all-to-all-start = ((bf16[512,4,640]{2,0,1:T(8,128)(2,1)}), bf16[512,4,640]{2,0,1:T(8,128)(2,1)}, u32[]{:S(2)}, u32[]{:S(2)}) async-start(bf16[512,4,640]{2,0,1:T(8,128)(2,1)} %bitcast.106), calls=%async_computation.5 | async-start | bytes 5242880 | tf_op jit(solution)/shard_map/all_to_all | solution.py:155
  1916.7 1336.3 %reduce-scatter.12.cloned.1.call-start = ((), (), s32[]{:S(2)}) async-start(), calls=%async_computation.20 | async-start | bytes 3276800 | tf_op jit(solution)/shard_map/reduce_scatter | solution.py:224
  2189.0 1715.2 %all-reduce.15.cloned.1.call-start = ((), (), s32[]{:S(2)}) async-start(), calls=%async_computation.24 | async-start | bytes 74711040 | tf_op jit(solution)/shard_map/psum | solution.py:227
  (39 other events, 1150.9 us)
Sparse Core Ops, SparseCore 0:
  9.6 32.9 all-gather.12
  44.1 31.7 all-gather.14
  79.3 43.9 all-gather.16
  124.7 117.3 all-gather.18
  243.6 117.8 all-gather.20
  370.8 31.8 all-reduce.10
  404.4 333.6 all-gather.22
  739.7 334.1 all-gather.24
  1075.6 334.1 all-gather.26
  1468.0 31.8 all-reduce.12
  1681.2 78.0 reduce-scatter.5
  1762.7 46.0 all-reduce.16
  1810.4 357.5 all-gather.30
  2170.2 525.6 all-gather.28
  2698.2 221.3 reduce-scatter.7
  2921.9 221.3 reduce-scatter.13
  3146.2 52.1 reduce-scatter.9
  3201.2 51.7 reduce-scatter.11
  3257.9 646.2 all-reduce.14
where the time goes:
time: 3950 us
  waiting for transfers between devices  3380 us (86%)
  matrix products  300 us (8%)
  other arithmetic  111 us (3%)
  local copies, waits for them, and re-layouts  77 us (2%)
  blocking collectives  42.4 us (1%)
    psum x1, waiting for transfers between devices, local(): lax.psum((gain_one_shard, gain_two_shard, query_shard, key_shard, value_s...  605 us
    all_gather x1, waiting for transfers between devices, local(): lax.all_gather(paired_grads, 'fsdp', axis=0, tiled=True)  507 us
    all_gather x1, waiting for transfers between devices, local(): lax.all_gather(w_gate, 'fsdp', axis=0, tiled=True)  329 us
    all_gather x1, waiting for transfers between devices, local(): lax.all_gather(w_up, 'fsdp', axis=0, tiled=True)  319 us
    all_gather x1, waiting for transfers between devices, local(): lax.all_gather(w_down, 'fsdp', axis=1, tiled=True)  319 us
    all_gather x1, waiting for transfers between devices, local(): lax.all_gather(activation, 'fsdp', axis=0, tiled=True)  247 us
    reduce_scatter x1, waiting for transfers between devices, local(): lax.psum_scatter(out_term, 'fsdp', scatter_dimension=1, tiled=True)  224 us
    reduce_scatter x1, waiting for transfers between devices, local(): lax.psum_scatter(query_term, 'fsdp', scatter_dimension=0, tiled=True)  174 us
  transfers between devices with their start and end apart: 23, of which 22 were waited for; matrix products, arithmetic and copies ran while one was open for 7% of the time, Pallas kernels for 0%

commit v1 on v0

v1 whole, which is shorter than its diff:
```python
import jax
import jax.numpy as jnp
from jax import lax
from jax.sharding import PartitionSpec as P

WINDOW = 2048
EPSILON = 1e-06
F32 = jnp.float32
BF16 = jnp.bfloat16


def exchange(value, step):
    count = lax.axis_size("seq")
    return lax.ppermute(value, "seq", [(at, at ^ step) for at in range(count)])


def swap(value):
    return lax.ppermute(value, "tensor", [(0, 1), (1, 0)])


def seq_shift(value, steps):
    count = lax.axis_size("seq")
    leading, last = (max(0, -steps), min(count, count - steps))
    return lax.ppermute(value, "seq", [(at, at + steps) for at in range(leading, last)])


def plane_gather(value):
    count = lax.axis_size("seq")
    if count != 4:
        return [value] + [exchange(value, step) for step in range(1, count)]
    half = value.shape[0] // 2
    near_one, near_two = exchange(value, 1), exchange(value, 2)
    far = jnp.concatenate([exchange(near_two[:half], 1), exchange(near_one[half:], 2)], axis=0)
    return [value, near_one, near_two, far]


def plane_scatter(own, others):
    total = own.astype(F32)
    for step, part in enumerate(others, 1):
        total = total + exchange(part.astype(BF16), step).astype(F32)
    return total


def times_transpose(left, right):
    return lax.dot_general(left, right, (((1,), (1,)), ((), ())), preferred_element_type=F32)


def rows_product(left, right):
    return lax.dot_general(left, right, (((0,), (0,)), ((), ())), preferred_element_type=F32)


def rotate(values, cosine, sine):
    half = cosine.shape[-1]
    first_part = values[..., :half]
    second_part = values[..., half : 2 * half]
    return jnp.concatenate(
        [
            first_part * cosine - second_part * sine,
            second_part * cosine + first_part * sine,
            values[..., 2 * half :],
        ],
        axis=-1,
    )


def inverse_rms(values):
    return lax.rsqrt(jnp.mean(values * values, axis=-1, keepdims=True) + EPSILON)


def norm_pull(values, inverse, grad):
    unit = values * inverse
    return inverse * (grad - unit * jnp.mean(grad * unit, axis=-1, keepdims=True))


def gated_unit(gate_pre, up_proj):
    return jax.nn.gelu(gate_pre) * up_proj


def pick(stacked, at):
    return lax.dynamic_index_in_dim(stacked, at, 0, keepdims=False)


def after(value, *others):
    return lax.optimization_barrier((value, *others))[0]


def part_of(value, at, size, axis):
    return lax.dynamic_slice_in_dim(value, at * size, size, axis)


def local(
    inputs, cotangent, gain_attn, gain_ffn, w_query, w_key, w_value, w_out, w_gate, w_up, w_down
):
    rows, width = inputs.shape
    half = rows // 2
    head_size = w_key.shape[1]
    head_cols = w_query.shape[1]
    heads_here = head_cols // head_size
    seqs, shards = lax.axis_size("seq"), lax.axis_size("fsdp")
    assert rows * shards == WINDOW and lax.axis_size("tensor") == 2
    seq_at, shard_at, core = (lax.axis_index(name) for name in ("seq", "fsdp", "tensor"))
    first = core == 0
    key_span = rows + WINDOW
    first_pos = (seq_at * shards + shard_at) * rows
    scale = head_size ** (-0.5)
    rot_half = head_size // 4
    frequency = 10000.0 ** (-(jnp.arange(rot_half, dtype=F32) * 2.0) / (2 * rot_half))
    angles = (first_pos + jnp.arange(rows, dtype=jnp.int32)).astype(F32)[:, None] * frequency[None]
    cosine, sine = jnp.cos(angles), jnp.sin(angles)

    def my_half(value):
        return part_of(value, core, half, 0)

    def other_half(value):
        return part_of(value, 1 - core, half, 0)

    def whole_rows(own):
        other = swap(own)
        return jnp.where(first, jnp.stack([own, other]), jnp.stack([other, own])).reshape(
            rows, own.shape[1]
        )

    def plane_rows(own, other=None):
        near = plane_gather(own)
        far = [swap(piece) if at or other is None else other for at, piece in enumerate(near)]
        return jnp.concatenate(near + far, axis=0)

    def plane_sum(partial):
        count = seqs * half
        cores = partial[:count].astype(F32) + swap(partial[count:].astype(BF16)).astype(F32)
        return plane_scatter(cores[:half], [cores[j * half : (j + 1) * half] for j in range(1, seqs)])

    def order_cols(pieces):
        stacked = jnp.stack(pieces)
        return [pick(stacked, seq_at ^ at) for at in range(seqs)]

    gain_one, gain_two = gain_attn.astype(F32)[:, None], gain_ffn.astype(F32)[:, None]
    gains = jnp.stack([gain_attn, gain_ffn])
    gains = jnp.stack(
        [gains]
        + [
            lax.ppermute(gains, "fsdp", [((at + by) % shards, at) for at in range(shards)])
            for by in range(1, shards)
        ]
    )
    gains = jnp.concatenate(
        [pick(gains, (at - shard_at) % shards) for at in range(shards)], axis=1
    ).astype(F32)
    pair_shard = jnp.where(first, w_key, w_value)
    proj_shard = jnp.concatenate([w_query, pair_shard], axis=1)
    proj_cols = proj_shard.shape[1] // seqs
    proj_weight = lax.all_gather(
        part_of(proj_shard, seq_at, proj_cols, 1), "fsdp", axis=0, tiled=True
    )
    out_rows = head_cols // seqs
    out_quarter = lax.all_gather(
        part_of(w_out, seq_at, out_rows, 0), "fsdp", axis=1, tiled=True
    )
    hidden = w_gate.shape[1] // seqs
    pair_in = jnp.concatenate(
        [part_of(w_gate, seq_at, hidden, 1), part_of(w_up, seq_at, hidden, 1)], axis=1
    )
    in_weight = lax.all_gather(pair_in, "fsdp", axis=0, tiled=True)
    down_weight = lax.all_gather(
        part_of(w_down, seq_at, hidden, 0), "fsdp", axis=1, tiled=True
    )

    source = inputs.astype(F32)
    inverse_one = inverse_rms(source)
    unit_one = (source * inverse_one * gains[0]).astype(BF16)
    rows_one = plane_rows(my_half(unit_one), other_half(unit_one))
    proj = jnp.dot(rows_one, proj_weight, preferred_element_type=F32)
    rotate_first = proj_cols % (2 * rot_half) == 0
    if rotate_first:
        halves_at = jnp.where(first, jnp.arange(2), 1 - jnp.arange(2))[:, None, None]
        seqs_at = (seq_at ^ jnp.arange(seqs))[None, :, None]
        row_pos = (
            (seqs_at * shards + shard_at) * rows + halves_at * half + jnp.arange(half)[None, None]
        ).reshape(-1)
        row_angles = row_pos.astype(F32)[:, None] * frequency[None]
        units = proj_cols // (2 * rot_half)
        unit_at = seq_at * units + jnp.arange(units)
        head_units = head_cols // (2 * rot_half)
        turned = (unit_at % 2 == 0) & (first | (unit_at < head_units))
        unit_scale = jnp.where(unit_at < head_units, scale, 1.0)[None, :, None]
        turned = turned[None, :, None]
        row_cos = jnp.where(turned, jnp.cos(row_angles)[:, None], 1.0) * unit_scale
        row_sin = jnp.where(turned, jnp.sin(row_angles)[:, None], 0.0) * unit_scale
        proj = rotate(proj.reshape(-1, units, 2 * rot_half), row_cos, row_sin)
    proj = proj.astype(BF16).reshape(2, seqs, half, proj_cols)
    proj = jnp.where(first, proj, proj[::-1])
    proj_parts = [proj[:, 0].reshape(rows, proj_cols)] + [
        exchange(proj[:, at].reshape(rows, proj_cols), at) for at in range(1, seqs)
    ]
    proj_here = jnp.concatenate(order_cols(proj_parts), axis=1)
    queries = proj_here[:, :head_cols].reshape(rows, heads_here, head_size)
    pair_here = proj_here[:, head_cols:]
    if not rotate_first:
        queries = (rotate(queries.astype(F32), cosine[:, None], sine[:, None]) * scale).astype(BF16)
        pair_here = jnp.where(first, rotate(pair_here.astype(F32), cosine, sine), pair_here)
        pair_here = pair_here.astype(BF16)

    earlier = seq_shift(pair_here, 1)
    slots = [
        lax.ppermute(
            jnp.where(shard_at >= at, earlier, pair_here),
            "fsdp", [(source_at, (source_at - at) % shards) for source_at in range(shards)],
        )
        for at in range(1, shards)
    ]
    window_here = jnp.concatenate([earlier] + slots + [pair_here], axis=0)
    window_other = swap(window_here)
    key_rows = jnp.where(first, window_here, window_other)
    value_rows = jnp.where(first, window_other, window_here)

    query_at = jnp.arange(rows, dtype=jnp.int32)[:, None]
    key_at = jnp.arange(key_span, dtype=jnp.int32)[None, :]
    allowed = (
        (key_at > query_at) & (key_at <= query_at + WINDOW) & (first_pos - WINDOW + key_at >= 0)
    )

    def score_all():
        raw_scores = jnp.einsum("rhd,kd->hrk", queries, key_rows, preferred_element_type=F32)
        return jnp.where(allowed[None], raw_scores, -1e30)

    scores = score_all()
    row_max = jnp.max(scores, axis=-1, keepdims=True)
    expon = jnp.exp(scores - row_max)
    denominator = jnp.sum(expon, axis=-1, keepdims=True)
    probability = expon / denominator
    log_total = row_max + jnp.log(denominator)
    attended = jnp.einsum(
        "hrk,kd->rhd", probability.astype(BF16), value_rows, preferred_element_type=F32
    )
    head_outputs = attended.reshape(rows, head_cols).astype(BF16)

    out_weight = jnp.zeros((head_cols, width), BF16)
    for at, piece in enumerate(plane_gather(out_quarter)):
        out_weight = lax.dynamic_update_slice_in_dim(
            out_weight, piece, (seq_at ^ at) * out_rows, 0
        )
    out_part = jnp.dot(head_outputs, out_weight, preferred_element_type=F32)
    hidden_in = my_half(source) + my_half(out_part) + swap(other_half(out_part))
    inverse_two = inverse_rms(hidden_in)
    unit_two = (hidden_in * inverse_two * gains[1]).astype(BF16)
    rows_two = plane_rows(unit_two)
    cot_later = after(cotangent, window_here)
    rows_cot = plane_rows(my_half(cot_later), other_half(cot_later))

    in_proj = jnp.dot(rows_two, in_weight, preferred_element_type=F32)
    gate_pre, up_proj = in_proj[:, :hidden], in_proj[:, hidden:]
    activation = gated_unit(gate_pre, up_proj).astype(BF16)
    grad_activation = times_transpose(rows_cot, down_weight)
    grad_gate, grad_up = jax.vjp(gated_unit, gate_pre, up_proj)[1](grad_activation)
    grad_in = jnp.concatenate([grad_gate.astype(BF16), grad_up.astype(BF16)], axis=1)
    grad_unit_two = plane_sum(times_transpose(grad_in, in_weight))
    grad_hidden = my_half(cotangent).astype(F32) + norm_pull(
        hidden_in, inverse_two, grad_unit_two * gains[1]
    )
    ffn_out = plane_sum(
        jnp.dot(after(activation, grad_unit_two), down_weight, preferred_element_type=F32)
    )
    layer_out = whole_rows((hidden_in + ffn_out).astype(BF16))

    in_term = rows_product(rows_two, grad_in).astype(BF16)
    down_term = rows_product(activation, rows_cot).astype(BF16)
    in_shard = lax.psum_scatter(in_term, "fsdp", scatter_dimension=0, tiled=True)
    down_shard = lax.psum_scatter(down_term, "fsdp", scatter_dimension=1, tiled=True)
    in_parts = order_cols(plane_gather(in_shard))
    gate_grad = jnp.concatenate([piece[:, :hidden] for piece in in_parts], axis=1).astype(F32)
    up_grad = jnp.concatenate([piece[:, hidden:] for piece in in_parts], axis=1).astype(F32)
    down_grad = jnp.concatenate(order_cols(plane_gather(down_shard)), axis=0).astype(F32)
    gain_two_half = jnp.sum(
        gate_grad * w_gate.astype(F32) + up_grad * w_up.astype(F32), axis=1
    ) / gain_two[:, 0]

    grad_attn_out = after(whole_rows(grad_hidden.astype(BF16)), in_term, down_term)
    grad_heads = (
        times_transpose(grad_attn_out, out_weight)
        .reshape(rows, heads_here, head_size)
        .astype(BF16)
    )
    out_term = rows_product(head_outputs, grad_attn_out).astype(BF16)
    out_sum = plane_scatter(
        part_of(out_term, seq_at, out_rows, 0),
        [part_of(out_term, seq_at ^ at, out_rows, 0) for at in range(1, seqs)],
    ).astype(BF16)
    out_shard = lax.psum_scatter(out_sum, "fsdp", scatter_dimension=1, tiled=True)
    out_grad = jnp.concatenate(order_cols(plane_gather(out_shard)), axis=0).astype(F32)

    probability_again = jnp.exp(score_all() - log_total)
    grad_probability = jnp.einsum(
        "rhd,kd->hrk", grad_heads, value_rows, preferred_element_type=F32
    )
    inner = jnp.sum(probability_again * grad_probability, axis=-1, keepdims=True)
    grad_scores = (probability_again * (grad_probability - inner)).astype(BF16)
    grad_queries = jnp.einsum("hrk,kd->rhd", grad_scores, key_rows, preferred_element_type=F32)
    grad_query_proj = (
        rotate(grad_queries * scale, cosine[:, None], -sine[:, None])
        .astype(BF16)
        .reshape(rows, head_cols)
    )
    grad_keys = jnp.einsum("hrk,rhd->kd", grad_scores, queries, preferred_element_type=F32)
    grad_values = jnp.einsum(
        "hrk,rhd->kd", probability_again.astype(BF16), grad_heads, preferred_element_type=F32
    )
    pair_grads = jnp.where(first, grad_keys, grad_values) + swap(
        jnp.where(first, grad_values, grad_keys)
    )
    returned = [
        lax.ppermute(
            pair_grads[at * rows : (at + 1) * rows].astype(BF16),
            "fsdp", [((source_at - at) % shards, source_at) for source_at in range(shards)],
        ).astype(F32)
        for at in range(1, shards)
    ]
    own_total = pair_grads[shards * rows :]
    earlier_total = pair_grads[:rows]
    for at, piece in enumerate(returned, 1):
        own_total = own_total + jnp.where(shard_at >= at, 0.0, piece)
        earlier_total = earlier_total + jnp.where(shard_at >= at, piece, 0.0)
    own_total = own_total + seq_shift(earlier_total.astype(BF16), -1).astype(F32)
    grad_pair = jnp.where(first, rotate(own_total, cosine, -sine), own_total).astype(BF16)
    grad_proj = jnp.concatenate([grad_query_proj, grad_pair], axis=1)
    grad_parts = [part_of(grad_proj, seq_at, proj_cols, 1)] + [
        exchange(part_of(grad_proj, seq_at ^ at, proj_cols, 1), at) for at in range(1, seqs)
    ]
    grad_rows = jnp.stack(grad_parts).reshape(seqs, 2, half, proj_cols).swapaxes(0, 1)
    grad_rows = jnp.where(first, grad_rows, grad_rows[::-1]).reshape(2 * seqs * half, proj_cols)

    proj_term = rows_product(rows_one, grad_rows).astype(BF16)
    grad_unit_one = plane_sum(times_transpose(grad_rows, proj_weight))
    grad_input = whole_rows(
        grad_hidden + norm_pull(my_half(source), my_half(inverse_one), grad_unit_one * gains[0])
    )
    proj_sum = lax.psum_scatter(proj_term, "fsdp", scatter_dimension=0, tiled=True)
    proj_grad = jnp.concatenate(order_cols(plane_gather(proj_sum)), axis=1).astype(F32)
    gain_one_half = jnp.sum(proj_grad * proj_shard.astype(F32), axis=1) / gain_one[:, 0]
    query_grad = proj_grad[:, :head_cols]
    pair_grad = proj_grad[:, head_cols:]
    pair_other = swap(pair_grad)
    gain_grads = jnp.stack([gain_one_half, gain_two_half])
    gain_grads = gain_grads + swap(gain_grads)
    return (
        layer_out,
        grad_input,
        gain_grads[0],
        gain_grads[1],
        query_grad,
        jnp.where(first, pair_grad, pair_other),
        jnp.where(first, pair_other, pair_grad),
        out_grad,
        gate_grad,
        up_grad,
        down_grad,
    )


def solution(mesh):
    rows = P(("seq", "fsdp"), None)
    specs = (
        P("fsdp"),
        P("fsdp"),
        P("fsdp", "tensor"),
        P("fsdp", None),
        P("fsdp", None),
        P("tensor", "fsdp"),
        P("fsdp", "tensor"),
        P("fsdp", "tensor"),
        P("tensor", "fsdp"),
    )
    return jax.shard_map(
        local, mesh=mesh, in_specs=(rows, rows) + specs, out_specs=(rows, rows) + specs,
        check_vma=False,
    )
```

time: 3950 us -> 1170 us (0.30)
  waiting for transfers between devices: 3380 us -> 401 us
  local copies, waits for them, and re-layouts: 77 us -> 186 us
  starting transfers between devices: 27 us -> 112 us
  other arithmetic: 111 us -> 189 us
  matrix products: 300 us -> 255 us
  blocking collectives: 42.4 us -> 0 us
    all_gather x10 -> x4, waiting for transfers between devices: 1940 us -> 11.5 us  [the longest x1 10.2 us: local(): lax.all_gather(part_of(w_down, seq_at, hidden, 0), 'fsdp', axis=1, tiled=...]
    psum x4 -> x0, waiting for transfers between devices: 664 us -> none  [the longest x1 605 us: local(): lax.psum((gain_one_shard, gain_two_shard, query_shard, key_shard, value_s...]
    reduce_scatter x5 -> x2, waiting for transfers between devices: 550 us -> 33.3 us  [the longest x1 33.3 us: local(): lax.psum_scatter(in_term, 'fsdp', scatter_dimension=0, tiled=True)]
    ppermute x2 -> x82, waiting for transfers between devices: 131 us -> 355 us  [the longest x50 290 us: exchange(): return lax.ppermute(value, 'seq', [(at, at ^ step) for at in range(count)])]
    ppermute x2 -> x82, starting transfers between devices: 6.26 us -> 112 us  [the longest x21 49.2 us: swap(): return lax.ppermute(value, 'tensor', [(0, 1), (1, 0)])]
    all_to_all x2 -> x0, waiting for transfers between devices: 85.2 us -> none  [the longest x1 85.2 us: local(): lax.all_to_all(cotangent, 'fsdp', split_axis=1, concat_axis=0, tiled=True)]
    slice x2 -> x37, local copies, waits for them, and re-layouts: 2.66 us -> 63.9 us  [the longest x3 18.5 us: plane_sum(): partial[count:].astype(BF16)]
    another operation x3 -> x19, other arithmetic: 3.34 us -> 53.2 us
  transfers between devices with their start and end apart: 23 -> 90, of which waited for: 22 -> 36; matrix products, arithmetic and copies ran while one was open for 7% -> 46% of each run, Pallas kernels for 0% -> 0%
where the time goes in v1:
time: 1170 us; the launch traced here: 1160 us
  waiting for transfers between devices  401 us (34%)
  matrix products  255 us (22%)
  other arithmetic  189 us (16%)
  local copies, waits for them, and re-layouts  186 us (16%)
  starting transfers between devices  112 us (10%)
  between operations  16 us (1%)
    ppermute x50, waiting for transfers between devices, exchange(): return lax.ppermute(value, 'seq', [(at, at ^ step) for at in range(count)])  290 us
    dot_general x4, matrix products, times_transpose(): lax.dot_general(left, right, (((1,), (1,)), ((), ())), preferred_element_...  74.2 us
    unnamed x181, local copies, waits for them, and re-layouts  57.3 us
    dot_general x4, matrix products, rows_product(): lax.dot_general(left, right, (((0,), (0,)), ((), ())), preferred_element_...  55.8 us
    ppermute x21, starting transfers between devices, swap(): return lax.ppermute(value, 'tensor', [(0, 1), (1, 0)])  49.2 us
    another operation x6, other arithmetic  45 us
    ppermute x50, starting transfers between devices, exchange(): return lax.ppermute(value, 'seq', [(at, at ^ step) for at in range(count)])  41.5 us
    ppermute x3, waiting for transfers between devices, local(): lax.ppermute(jnp.where(shard_at >= at, earlier, pair_here), 'fsdp', [(sou...  41 us
  transfers between devices with their start and end apart: 90, of which 36 were waited for; matrix products, arithmetic and copies ran while one was open for 46% of the time, Pallas kernels for 0%

profile of v1, /device:TPU:9, one launch (start us, length us, event | category | flops | bytes accessed | tf_op | source)
XLA Modules:
  0.0 1159.0 jit_solution(11105447640795320773)
XLA Ops:
  35.6 24.3 %collective-permute-done.4 = bf16[256,2560]{1,0:T(8,128)(2,1)S(1)} collective-permute-done((bf16[256,2560]{1,0:T(8,128)(2,1)}, bf16[256,2560]{1,0:T(8,128)(2,1)S(1)}, u32[]{:S(2)}, u32[]{:S(2)}) %collective-permute-start.4) | collective-permute-done | bytes 1310752 | tf_op jit(solution)/shard_map/ppermute | solution.py:14
  181.1 17.8 %collective-permute-done.16 = bf16[512,256]{0,1:T(8,128)(2,1)S(1)} collective-permute-done((bf16[512,256]{0,1:T(8,128)(2,1)S(1)}, bf16[512,256]{0,1:T(8,128)(2,1)S(1)}, u32[]{:S(2)}, u32[]{:S(2)}) %collective-permute-start.16) | collective-permute-done | bytes 262176 | tf_op jit(solution)/shard_map/ppermute | solution.py:205
  293.3 24.1 %collective-permute-done.24 = bf16[256,2560]{1,0:T(8,128)(2,1)S(1)} collective-permute-done((bf16[256,2560]{1,0:T(8,128)(2,1)S(1)}, bf16[256,2560]{1,0:T(8,128)(2,1)S(1)}, u32[]{:S(2)}, u32[]{:S(2)}) %collective-permute-start.24) | collective-permute-done | bytes 1310752 | tf_op jit(solution)/shard_map/ppermute | solution.py:14
  342.2 27.9 %fusion.84 = f32[2048,1920]{0,1:T(8,128)} fusion(bf16[2048,2560]{1,0:T(8,128)(2,1)} %constant_dynamic-update-slice_fusion.13, bf16[2560,1920]{1,0:T(8,128)(2,1)} %all-gather.9.cloned.1.call-done), kind=kOutput, calls=%fused_computation.289 | convolution fusion | flops 20132659200 | bytes 36044800 | tf_op jit(solution)/shard_map/dot_general | solution.py:250
  380.4 25.1 %fusion.18 = (bf16[2048,960]{0,1:T(8,128)(2,1)S(1)}, bf16[2048,960]{0,1:T(8,128)(2,1)}, bf16[2048,960]{0,1:T(8,128)(2,1)}) fusion(f32[2048,1920]{0,1:T(8,128)} %fusion.84, bf16[2048,2560]{1,0:T(8,128)(2,1)} %constant_dynamic-update-slice_fusion.22, bf16[960,2560]{1,0:T(8,128)(2,1)} %all-gather.11.cloned.1.call-done), kind=kOutput, calls=%fused_computation.35 | convolution fusion | flops 10117447680 | bytes 42926080 | tf_op jit(solution)/shard_map/dot_general | solution.py:45
  405.5 29.6 %fusion.21 = f32[2048,2560]{1,0:T(8,128)} fusion(bf16[2560,1920]{1,0:T(8,128)(2,1)} %all-gather.9.cloned.1.call-done, bf16[2048,960]{0,1:T(8,128)(2,1)} %get-tuple-element.43, bf16[2048,960]{0,1:T(8,128)(2,1)S(1)} %get-tuple-element.42), kind=kOutput, calls=%fused_computation.48 | convolution fusion | flops 20148387840 | bytes 38666240 | tf_op jit(solution)/shard_map/dot_general | solution.py:45
  448.7 13.3 %fusion.72 = (bf16[1024,2560]{1,0:T(8,128)(2,1)}, f32[1024,2560]{1,0:T(8,128)}) fusion(bf16[1024,2560]{1,0:T(8,128)(2,1)} %collective-permute-done.38, f32[2048,2560]{1,0:T(8,128)} %fusion.21), kind=kLoop, calls=%fused_computation.277 | loop fusion | flops 7864320 | bytes 31457280 | tf_op jit(solution)/shard_map/convert.17
  468.9 14.4 %convolution_convert_fusion.2 = bf16[960,2560]{1,0:T(8,128)(2,1)} fusion(bf16[2048,960]{0,1:T(8,128)(2,1)S(1)} %copy-done.65, bf16[2048,2560]{1,0:T(8,128)(2,1)} %constant_dynamic-update-slice_fusion.22), kind=kOutput, calls=%fused_computation.40 | convolution fusion | flops 10068787200 | bytes 19333120 | tf_op jit(solution)/shard_map/dot_general | solution.py:49
  497.6 28.3 %collective-permute-done.41 = bf16[256,2560]{1,0:T(8,128)(2,1)} collective-permute-done((bf16[256,2560]{1,0:T(8,128)(2,1)}, bf16[256,2560]{1,0:T(8,128)(2,1)}, u32[]{:S(2)}, u32[]{:S(2)}) %collective-permute-start.41) | collective-permute-done | bytes 1310752 | tf_op jit(solution)/shard_map/ppermute | solution.py:14
  534.1 26.2 %convolution_convert_fusion = bf16[2560,1920]{1,0:T(8,128)(2,1)} fusion(bf16[2048,2560]{1,0:T(8,128)(2,1)} %constant_dynamic-update-slice_fusion.13, bf16[2048,960]{0,1:T(8,128)(2,1)S(1)} %copy-done.68, bf16[2048,960]{0,1:T(8,128)(2,1)S(1)} %copy-done.67), kind=kOutput, calls=%fused_computation.17 | convolution fusion | flops 20153303040 | bytes 28180480 | tf_op jit(solution)/shard_map/dot_general | solution.py:49
  571.6 17.5 %fusion = (f32[5,512]{1,0:T(8,128)S(1)}, f32[2560,512,5]{1,0,2:T(8,128)}) fusion(f32[2560,512,5]{1,0,2:T(8,128)} %get-tuple-element.119, f32[5,512]{1,0:T(8,128)S(1)} %log_add_fusion, pred[512,2560]{0,1:T(8,128)(4,1)S(1)} %copy-done.6, bf16[512,5,256]{0,2,1:T(8,128)(2,1)S(1)} %bitcast.197, bf16[2560,256]{0,1:T(8,128)(2,1)} %copy-done.39, ...), kind=kOutput, calls=%fused_computation.2 | convolution fusion | flops 3382310400 | bytes 57692160 | tf_op jit(solution)/shard_map/rhd,kd->hrk/dot_general | solution.py:292
  589.1 23.3 %fusion.2 = bf16[5,512,2560]{1,2,0:T(8,128)(2,1)} fusion(f32[2560,512,5]{1,0,2:T(8,128)} %get-tuple-element.121, f32[2560,512,5]{1,0,2:T(8,128)} %get-tuple-element.119, f32[5,512]{1,0:T(8,128)S(1)} %get-tuple-element.120, f32[5,512]{1,0:T(8,128)S(1)} %log_add_fusion, pred[512,2560]{0,1:T(8,128)(4,1)S(1)} %copy-done.6), kind=kLoop, calls=%fused_computation.4 | loop fusion | flops 32768000 | bytes 66867200 | tf_op jit(solution)/shard_map/convert_element_type | solution.py:296
  619.2 14.0 %broadcast_select_fusion = (f32[2560,256]{0,1:T(8,128)}, f32[2560,256]{0,1:T(8,128)}) fusion(f32[2560,256]{0,1:T(8,128)S(1)} %convolution_bitcast_fusion, pred[]{:T(512)S(6)} %eq.17, bf16[512,5,256]{0,2,1:T(8,128)(2,1)S(1)} %bitcast.198, f32[2560,512,5]{1,0,2:T(8,128)} %get-tuple-element.119, f32[5,512]{1,0:T(8,128)S(1)} %log_add_fusion, ...), kind=kOutput, calls=%fused_computation.128 | convolution fusion | flops 3375759360 | bytes 36710400 | tf_op jit(solution)/shard_map/hrk,rhd->kd/dot_general | solution.py:304
  667.1 12.5 %collective-permute-done.50 = bf16[512,256]{0,1:T(8,128)(2,1)S(1)} collective-permute-done((bf16[512,256]{0,1:T(8,128)(2,1)}, bf16[512,256]{0,1:T(8,128)(2,1)S(1)}, u32[]{:S(2)}, u32[]{:S(2)}) %collective-permute-start.50) | collective-permute-done | bytes 262176 | tf_op jit(solution)/shard_map/ppermute | solution.py:311
  686.2 34.2 %collective-permute-done.73 = bf16[320,2560]{1,0:T(8,128)(2,1)} collective-permute-done((bf16[320,2560]{1,0:T(8,128)(2,1)}, bf16[320,2560]{1,0:T(8,128)(2,1)}, u32[]{:S(2)}, u32[]{:S(2)}) %collective-permute-start.73) | collective-permute-done | bytes 1638432 | tf_op jit(solution)/shard_map/ppermute | solution.py:14
  794.4 18.3 %fusion.85 = f32[2048,2560]{1,0:T(8,128)} fusion(bf16[2048,960]{0,1:T(8,128)(2,1)} %get-tuple-element.15, bf16[960,2560]{1,0:T(8,128)(2,1)} %all-gather.11.cloned.1.call-done), kind=kOutput, calls=%fused_computation.290 | convolution fusion | flops 10066329600 | bytes 29818880 | tf_op jit(solution)/shard_map/dot_general | solution.py:261
  824.1 13.5 %collective-permute-done.80 = bf16[480,640]{1,0:T(8,128)(2,1)S(1)} collective-permute-done((bf16[480,640]{1,0:T(8,128)(2,1)S(1)}, bf16[480,640]{1,0:T(8,128)(2,1)S(1)}, u32[]{:S(2)}, u32[]{:S(2)}) %collective-permute-start.80) | collective-permute-done | bytes 614432 | tf_op jit(solution)/shard_map/ppermute | solution.py:14
  859.4 13.3 %fusion.68 = (bf16[1024,2560]{1,0:T(8,128)(2,1)}, f32[1024,2560]{1,0:T(8,128)}) fusion(bf16[1024,2560]{1,0:T(8,128)(2,1)} %collective-permute-done.56, f32[2048,2560]{1,0:T(8,128)} %fusion.86), kind=kLoop, calls=%fused_computation.274 | loop fusion | flops 7864320 | bytes 31457280 | tf_op jit(solution)/shard_map/convert.2
  877.5 13.4 %fusion.71 = (bf16[1024,2560]{1,0:T(8,128)(2,1)}, f32[1024,2560]{1,0:T(8,128)}) fusion(bf16[1024,2560]{1,0:T(8,128)(2,1)} %collective-permute-done.42, f32[2048,2560]{1,0:T(8,128)} %fusion.85), kind=kLoop, calls=%fused_computation.276 | loop fusion | flops 7864320 | bytes 31457280 | tf_op jit(solution)/shard_map/convert.13
  915.5 37.7 %collective-permute-done.58 = bf16[256,2560]{1,0:T(8,128)(2,1)} collective-permute-done((bf16[256,2560]{1,0:T(8,128)(2,1)}, bf16[256,2560]{1,0:T(8,128)(2,1)}, u32[]{:S(2)}, u32[]{:S(2)}) %collective-permute-start.58) | collective-permute-done | bytes 1310752 | tf_op jit(solution)/shard_map/ppermute | solution.py:14
  953.2 33.3 %reduce-scatter.11.cloned.1.call-done = bf16[640,1920]{1,0:T(8,128)(2,1)} async-done(((bf16[2560,1920]{1,0:T(8,128)(2,1)}), bf16[640,1920]{1,0:T(8,128)(2,1)}) %reduce-scatter.11.cloned.1.call-update) | async-done | bytes 2457616 | tf_op jit(solution)/shard_map/reduce_scatter | solution.py:267
  995.1 14.3 %collective-permute-done.44 = bf16[256,2560]{1,0:T(8,128)(2,1)} collective-permute-done((bf16[256,2560]{1,0:T(8,128)(2,1)}, bf16[256,2560]{1,0:T(8,128)(2,1)}, u32[]{:S(2)}, u32[]{:S(2)}) %collective-permute-start.44) | collective-permute-done | bytes 1310752 | tf_op jit(solution)/shard_map/ppermute | solution.py:14
  1027.8 34.2 %collective-permute-done.66 = bf16[640,1920]{1,0:T(8,128)(2,1)S(1)} collective-permute-done((bf16[640,1920]{1,0:T(8,128)(2,1)}, bf16[640,1920]{1,0:T(8,128)(2,1)S(1)}, u32[]{:S(2)}, u32[]{:S(2)}) %collective-permute-start.66) | collective-permute-done | bytes 2457632 | tf_op jit(solution)/shard_map/ppermute | solution.py:14
  1119.7 17.6 %add_reduce_fusion = (f32[640]{0:T(1024)S(1)}, f32[640,3840]{1,0:T(8,128)}, f32[640,3840]{1,0:T(8,128)}) fusion(bf16[640,3840]{1,0:T(8,128)(2,1)} %param.20, bf16[640,3840]{1,0:T(8,128)(2,1)} %param.19, bf16[640,3840]{1,0:T(8,128)(2,1)} %concatenate.104, bf16[640,3840]{1,0:T(8,128)(2,1)} %concatenate.105), kind=kLoop, calls=%fused_computation.28 | loop fusion | flops 19660160 | bytes 39324160 | tf_op jit(solution)/shard_map/reduce_sum | solution.py:273
  (524 shorter events, 614.9 us)
Async XLA Ops:
  7.2 74.4 %all-gather.7.cloned.1.call-start = ((), (), s32[]{:S(2)}) async-start(), calls=%async_computation.5 | async-start | bytes 2048000 | tf_op jit(solution)/shard_map/all_gather | solution.py:156
  9.4 83.3 %all-gather.5.cloned.1.call-start = ((), (), s32[]{:S(2)}) async-start(), calls=%async_computation.4 | async-start | bytes 2457600 | tf_op jit(solution)/shard_map/all_gather | solution.py:152
  11.5 330.7 %all-gather.9.cloned.1.call-start = ((), (), s32[]{:S(2)}) async-start(), calls=%async_computation.6 | async-start | bytes 12288000 | tf_op jit(solution)/shard_map/all_gather | solution.py:163
  21.8 358.7 %all-gather.11.cloned.1.call-start = ((), (), s32[]{:S(2)}) async-start(), calls=%async_computation.7 | async-start | bytes 6144000 | tf_op jit(solution)/shard_map/all_gather | solution.py:164
  81.6 74.5 %collective-permute-start.18 = (bf16[320,2560]{1,0:T(8,128)(2,1)}, bf16[320,2560]{1,0:T(8,128)(2,1)}, u32[]{:S(2)}, u32[]{:S(2)}) collective-permute-start(bf16[320,2560]{1,0:T(8,128)(2,1)} %all-gather.7.cloned.1.call-done), channel_id=1, source_target_pairs={{0,8},{8,0},{16,24},{24,16},{1,9},{9,1},{17,25},{25,17},{2,10},{10... | collective-permute-start | bytes 4915208 | tf_op jit(solution)/shard_map/ppermute | solution.py:14
  82.8 70.4 %collective-permute-start.19 = (bf16[320,2560]{1,0:T(8,128)(2,1)}, bf16[320,2560]{1,0:T(8,128)(2,1)}, u32[]{:S(2)}, u32[]{:S(2)}) collective-permute-start(bf16[320,2560]{1,0:T(8,128)(2,1)} %all-gather.7.cloned.1.call-done), channel_id=1, source_target_pairs={{0,16},{8,24},{16,0},{24,8},{1,17},{9,25},{17,1},{25,9},{2,18},{10... | collective-permute-start | bytes 4915208 | tf_op jit(solution)/shard_map/ppermute | solution.py:14
  154.9 55.1 %collective-permute-start.20 = (bf16[160,2560]{1,0:T(8,128)(2,1)S(1)}, bf16[160,2560]{1,0:T(8,128)(2,1)S(1)}, u32[]{:S(2)}, u32[]{:S(2)}) collective-permute-start(bf16[160,2560]{1,0:T(8,128)(2,1)S(1)} %slice.304), channel_id=1, source_target_pairs={{0,8},{8,0},{16,24},{24,16},{1,9},{9,1},{17,25},{25,17},{2,10},{10... | collective-permute-start | bytes 2457608 | tf_op jit(solution)/shard_map/ppermute | solution.py:14
  258.6 533.3 %reduce-scatter.15.cloned.1.call-start = ((), (), s32[]{:S(2)}) async-start(), calls=%async_computation.11 | async-start | bytes 6553600
  468.9 57.0 %collective-permute-start.41 = (bf16[256,2560]{1,0:T(8,128)(2,1)}, bf16[256,2560]{1,0:T(8,128)(2,1)}, u32[]{:S(2)}, u32[]{:S(2)}) collective-permute-start(bf16[256,2560]{1,0:T(8,128)(2,1)} %get-tuple-element.59), channel_id=1, source_target_pairs={{0,24},{8,16},{16,8},{24,0},{1,25},{9,17},{17,9},{25,1},{2,26},{10... | collective-permute-start | bytes 3932168 | tf_op jit(solution)/shard_map/ppermute | solution.py:14
  491.3 349.1 %reduce-scatter.13.cloned.1.call-start = ((), (), s32[]{:S(2)}) async-start(), calls=%async_computation.10 | async-start | bytes 2457600
  648.1 72.3 %collective-permute-start.73 = (bf16[320,2560]{1,0:T(8,128)(2,1)}, bf16[320,2560]{1,0:T(8,128)(2,1)}, u32[]{:S(2)}, u32[]{:S(2)}) collective-permute-start(bf16[320,2560]{1,0:T(8,128)(2,1)} %get-tuple-element.50), channel_id=1, source_target_pairs={{0,24},{8,16},{16,8},{24,0},{1,25},{9,17},{17,9},{25,1},{2,26},{10... | collective-permute-start | bytes 4915208 | tf_op jit(solution)/shard_map/ppermute | solution.py:14
  726.5 131.5 %reduce-scatter.9.cloned.1.call-start = ((), (), s32[]{:S(2)}) async-start(), calls=%async_computation.8 | async-start | bytes 2457600 | tf_op jit(solution)/shard_map/reduce_scatter | solution.py:336
  763.1 223.4 %reduce-scatter.11.cloned.1.call-start = ((), (), s32[]{:S(2)}) async-start(), calls=%async_computation.9 | async-start | bytes 12288000 | tf_op jit(solution)/shard_map/reduce_scatter | solution.py:267
  782.8 76.1 %collective-permute-start.56 = (bf16[1024,2560]{1,0:T(8,128)(2,1)}, bf16[1024,2560]{1,0:T(8,128)(2,1)}, u32[]{:S(2)}, u32[]{:S(2)}) collective-permute-start(bf16[1024,2560]{1,0:T(8,128)(2,1)} %slice.431), channel_id=1, source_target_pairs={{0,1},{1,0},{2,3},{3,2},{4,5},{5,4},{6,7},{7,6},{8,9},{9,8},{10,11... | collective-permute-start | bytes 15728648 | tf_op jit(solution)/shard_map/ppermute | solution.py:18
  819.7 56.9 %collective-permute-start.42 = (bf16[1024,2560]{1,0:T(8,128)(2,1)}, bf16[1024,2560]{1,0:T(8,128)(2,1)}, u32[]{:S(2)}, u32[]{:S(2)}) collective-permute-start(bf16[1024,2560]{1,0:T(8,128)(2,1)} %slice.432), channel_id=1, source_target_pairs={{0,1},{1,0},{2,3},{3,2},{4,5},{5,4},{6,7},{7,6},{8,9},{9,8},{10,11... | collective-permute-start | bytes 15728648 | tf_op jit(solution)/shard_map/ppermute | solution.py:18
  894.9 58.3 %collective-permute-start.58 = (bf16[256,2560]{1,0:T(8,128)(2,1)}, bf16[256,2560]{1,0:T(8,128)(2,1)}, u32[]{:S(2)}, u32[]{:S(2)}) collective-permute-start(bf16[256,2560]{1,0:T(8,128)(2,1)} %get-tuple-element.54), channel_id=1, source_target_pairs={{0,16},{8,24},{16,0},{24,8},{1,17},{9,25},{17,1},{25,9},{2,18},{10... | collective-permute-start | bytes 3932168 | tf_op jit(solution)/shard_map/ppermute | solution.py:14
  895.0 92.7 %collective-permute-start.59 = (bf16[256,2560]{1,0:T(8,128)(2,1)}, bf16[256,2560]{1,0:T(8,128)(2,1)}, u32[]{:S(2)}, u32[]{:S(2)}) collective-permute-start(bf16[256,2560]{1,0:T(8,128)(2,1)} %get-tuple-element.53), channel_id=1, source_target_pairs={{0,24},{8,16},{16,8},{24,0},{1,25},{9,17},{17,9},{25,1},{2,26},{10... | collective-permute-start | bytes 3932168 | tf_op jit(solution)/shard_map/ppermute | solution.py:14
  908.7 86.5 %collective-permute-start.43 = (bf16[256,2560]{1,0:T(8,128)(2,1)}, bf16[256,2560]{1,0:T(8,128)(2,1)}, u32[]{:S(2)}, u32[]{:S(2)}) collective-permute-start(bf16[256,2560]{1,0:T(8,128)(2,1)} %get-tuple-element.55), channel_id=1, source_target_pairs={{0,8},{8,0},{16,24},{24,16},{1,9},{9,1},{17,25},{25,17},{2,10},{10... | collective-permute-start | bytes 3932168 | tf_op jit(solution)/shard_map/ppermute | solution.py:14
  909.4 100.0 %collective-permute-start.44 = (bf16[256,2560]{1,0:T(8,128)(2,1)}, bf16[256,2560]{1,0:T(8,128)(2,1)}, u32[]{:S(2)}, u32[]{:S(2)}) collective-permute-start(bf16[256,2560]{1,0:T(8,128)(2,1)} %get-tuple-element.57), channel_id=1, source_target_pairs={{0,16},{8,24},{16,0},{24,8},{1,17},{9,25},{17,1},{25,9},{2,18},{10... | collective-permute-start | bytes 3932168 | tf_op jit(solution)/shard_map/ppermute | solution.py:14
  910.3 99.1 %collective-permute-start.45 = (bf16[256,2560]{1,0:T(8,128)(2,1)}, bf16[256,2560]{1,0:T(8,128)(2,1)}, u32[]{:S(2)}, u32[]{:S(2)}) collective-permute-start(bf16[256,2560]{1,0:T(8,128)(2,1)} %get-tuple-element.56), channel_id=1, source_target_pairs={{0,24},{8,16},{16,8},{24,0},{1,25},{9,17},{17,9},{25,1},{2,26},{10... | collective-permute-start | bytes 3932168 | tf_op jit(solution)/shard_map/ppermute | solution.py:14
  986.5 75.4 %collective-permute-start.66 = (bf16[640,1920]{1,0:T(8,128)(2,1)}, bf16[640,1920]{1,0:T(8,128)(2,1)S(1)}, u32[]{:S(2)}, u32[]{:S(2)}) collective-permute-start(bf16[640,1920]{1,0:T(8,128)(2,1)} %reduce-scatter.11.cloned.1.call-done), channel_id=1, source_target_pairs={{0,16},{8,24},{16,0},{24,8},{1,17},{9,25},{17,1},{25,9},{2,18},{10... | collective-permute-start | bytes 7372808 | tf_op jit(solution)/shard_map/ppermute | solution.py:14
  987.7 75.1 %collective-permute-start.65 = (bf16[640,1920]{1,0:T(8,128)(2,1)}, bf16[640,1920]{1,0:T(8,128)(2,1)S(1)}, u32[]{:S(2)}, u32[]{:S(2)}) collective-permute-start(bf16[640,1920]{1,0:T(8,128)(2,1)} %reduce-scatter.11.cloned.1.call-done), channel_id=1, source_target_pairs={{0,8},{8,0},{16,24},{24,16},{1,9},{9,1},{17,25},{25,17},{2,10},{10... | collective-permute-start | bytes 7372808 | tf_op jit(solution)/shard_map/ppermute | solution.py:14
  1017.5 60.4 %collective-permute-start.46 = (bf16[256,2560]{1,0:T(8,128)(2,1)S(1)}, bf16[256,2560]{1,0:T(8,128)(2,1)S(1)}, u32[]{:S(2)}, u32[]{:S(2)}) collective-permute-start(bf16[256,2560]{1,0:T(8,128)(2,1)S(1)} %get-tuple-element.72), channel_id=1, source_target_pairs={{0,1},{1,0},{2,3},{3,2},{4,5},{5,4},{6,7},{7,6},{8,9},{9,8},{10,11... | collective-permute-start | bytes 3932168 | tf_op jit(solution)/shard_map/ppermute | solution.py:18
  1071.7 72.1 %collective-permute-start.60 = (f32[256,2560]{1,0:T(8,128)}, f32[256,2560]{1,0:T(8,128)}, u32[]{:S(2)}, u32[]{:S(2)}) collective-permute-start(f32[256,2560]{1,0:T(8,128)} %get-tuple-element.71), channel_id=1, source_target_pairs={{0,1},{1,0},{2,3},{3,2},{4,5},{5,4},{6,7},{7,6},{8,9},{9,8},{10,11... | collective-permute-start | bytes 7864328 | tf_op jit(solution)/shard_map/ppermute | solution.py:18
  (141 other events, 2913.3 us)
Sparse Core Ops, SparseCore 0:
  10.2 38.2 all-gather.6
  50.7 41.9 all-gather.4
  94.8 191.8 all-gather.8
  288.2 92.1 all-gather.10
  491.4 95.5 reduce-scatter.14
  726.6 45.7 reduce-scatter.12
  775.3 40.6 reduce-scatter.8
  819.0 167.5 reduce-scatter.10

commit v2 on v1

--- a/solution.py
+++ b/solution.py
@@ -1,6 +1,8 @@
 import jax
 import jax.numpy as jnp
 from jax import lax
+from jax.experimental import pallas as pl
+from jax.experimental.pallas import tpu as pltpu
 from jax.sharding import PartitionSpec as P
 
 WINDOW = 2048
@@ -34,10 +36,13 @@
     return [value, near_one, near_two, far]
 
 
-def plane_scatter(own, others):
+def plane_scatter(own, others, gate=None):
     total = own.astype(F32)
-    for step, part in enumerate(others, 1):
-        total = total + exchange(part.astype(BF16), step).astype(F32)
+    parts = [exchange(part.astype(BF16), step) for step, part in enumerate(others, 1)]
+    if gate is not None:
+        parts = lax.optimization_barrier((*parts, gate))[:-1]
+    for part in parts:
+        total = total + part.astype(F32)
     return total
 
 
@@ -86,6 +91,418 @@
 
 def part_of(value, at, size, axis):
     return lax.dynamic_slice_in_dim(value, at * size, size, axis)
+
+
+MESH = pl.DeviceIdType.MESH
+
+
+def greet(partners):
+    barrier = pltpu.get_barrier_semaphore()
+    for partner in partners:
+        pl.semaphore_signal(barrier, inc=1, device_id=partner, device_id_type=MESH)
+    pl.semaphore_wait(barrier, len(partners))
+
+
+def plane_partners():
+    seq_at, core = lax.axis_index("seq"), lax.axis_index("tensor")
+    return {"seq": seq_at ^ 1}, {"seq": seq_at ^ 2}, {"tensor": 1 - core}
+
+
+def send(source, target, sems, at, partner):
+    copy = pltpu.make_async_remote_copy(
+        src_ref=source, dst_ref=target, send_sem=sems.at[0, at], recv_sem=sems.at[1, at],
+        device_id=partner, device_id_type=MESH,
+    )
+    copy.start()
+    return copy
+
+
+def rows_kernel(own_ref, out_ref, sems, local_sem):
+    half = own_ref.shape[0]
+    one, two, core = plane_partners()
+    greet((one, two, core))
+
+    def block(at, first=0, count=half):
+        return out_ref.at[pl.ds(at * half + first, count), :]
+
+    here = pltpu.make_async_copy(own_ref, block(0), local_sem)
+    here.start()
+    from_one = send(own_ref, block(1), sems, 0, one)
+    from_two = send(own_ref, block(2), sems, 1, two)
+    copies = [from_one, from_two, send(own_ref, block(4), sems, 2, core)]
+    cut = half // 2
+    from_one.wait_recv()
+    far_low = send(block(1, cut, cut), block(3, cut, cut), sems, 3, two)
+    copies.append(send(block(1), block(5), sems, 4, core))
+    from_two.wait_recv()
+    far_top = send(block(2, 0, cut), block(3, 0, cut), sems, 5, one)
+    copies.append(send(block(2), block(6), sems, 6, core))
+    far_low.wait_recv()
+    far_top.wait_recv()
+    copies.append(send(block(3), block(7), sems, 7, core))
+    for copy in copies[2:]:
+        copy.wait_recv()
+    for copy in copies + [far_low, far_top]:
+        copy.wait_send()
+    here.wait()
+
+
+def gather_rows(own, collective_id):
+    half, width = own.shape
+    return pl.pallas_call(
+        rows_kernel,
+        out_shape=jax.ShapeDtypeStruct((8 * half, width), own.dtype),
+        in_specs=[pl.BlockSpec(memory_space=pl.ANY)],
+        out_specs=pl.BlockSpec(memory_space=pl.ANY),
+        scratch_shapes=[pltpu.SemaphoreType.DMA((2, 8)), pltpu.SemaphoreType.DMA],
+        compiler_params=pltpu.CompilerParams(collective_id=collective_id, has_side_effects=True),
+        cost_estimate=pl.CostEstimate(flops=1000, bytes_accessed=1000, transcendentals=0),
+        name="gather_rows",
+    )(own)
+
+
+def sum_kernel(
+    part_ref, out_ref, own_ref, land_ref, total_ref, near_ref, sems, local_sems
+):
+    half = out_ref.shape[0]
+    cut = half // 2
+    chunk = 32
+    one, two, core = plane_partners()
+    greet((one, two, core))
+    order = (3, 1, 2, 0)
+    loads, lands = {}, {}
+    for at in order:
+        loads[at] = pltpu.make_async_copy(
+            part_ref.at[pl.ds(at * half, half), :], own_ref.at[at], local_sems.at[at]
+        )
+        loads[at].start()
+        lands[at] = send(
+            part_ref.at[pl.ds((4 + at) * half, half), :], land_ref.at[at], sems, at, core
+        )
+    sent = []
+    for at in order:
+        loads[at].wait()
+        lands[at].wait_recv()
+
+        @pl.loop(0, half // chunk)
+        def _(step):
+            rows = pl.ds(pl.multiple_of(step * chunk, chunk), chunk)
+            value = own_ref[at, rows, :].astype(F32) + land_ref[at, rows, :].astype(F32)
+            if at:
+                total_ref[at - 1, rows, :] = value.astype(BF16)
+            else:
+                out_ref[rows, :] = value
+
+        top, low = (total_ref.at[at - 1, pl.ds(first, cut), :] for first in (0, cut))
+        if at == 3:
+            far_top = send(top, near_ref.at[1], sems, 4, one)
+            far_low = send(low, near_ref.at[3], sems, 5, two)
+        if at == 1:
+            near_top = send(top, near_ref.at[0], sems, 6, one)
+        if at == 2:
+            near_low = send(low, near_ref.at[2], sems, 7, two)
+
+    def add_in(at, first, from_at):
+        @pl.loop(0, cut // chunk)
+        def _(step):
+            rows = pl.ds(pl.multiple_of(step * chunk, chunk), chunk)
+            there = pl.ds(pl.multiple_of(first + step * chunk, chunk), chunk)
+            value = total_ref[at, there, :].astype(F32) + near_ref[from_at, rows, :].astype(F32)
+            total_ref[at, there, :] = value.astype(BF16)
+
+    far_top.wait_recv()
+    add_in(1, 0, 1)
+    last_top = send(total_ref.at[1, pl.ds(0, cut), :], near_ref.at[4], sems, 8, two)
+    far_low.wait_recv()
+    add_in(0, cut, 3)
+    last_low = send(total_ref.at[0, pl.ds(cut, cut), :], near_ref.at[5], sems, 9, one)
+
+    for first, near, last, near_at, last_at in (
+        (0, near_top, last_top, 0, 4), (cut, near_low, last_low, 2, 5),
+    ):
+        near.wait_recv()
+        last.wait_recv()
+
+        @pl.loop(0, cut // chunk)
+        def _(step):
+            rows = pl.ds(pl.multiple_of(step * chunk, chunk), chunk)
+            there = pl.ds(pl.multiple_of(first + step * chunk, chunk), chunk)
+            out_ref[there, :] += near_ref[near_at, rows, :].astype(F32) + near_ref[
+                last_at, rows, :
+            ].astype(F32)
+
+    for copy in (*lands.values(), far_top, far_low, near_top, near_low, last_top, last_low):
+        copy.wait_send()
+
+
+def scatter_rows(part, collective_id):
+    count, width = part.shape
+    half = count // 8
+    return pl.pallas_call(
+        sum_kernel,
+        out_shape=jax.ShapeDtypeStruct((half, width), F32),
+        in_specs=[pl.BlockSpec(memory_space=pl.ANY)],
+        out_specs=pl.BlockSpec(memory_space=pltpu.VMEM),
+        scratch_shapes=[
+            pltpu.VMEM((4, half, width), BF16),
+            pltpu.VMEM((4, half, width), BF16),
+            pltpu.VMEM((3, half, width), BF16),
+            pltpu.VMEM((6, half // 2, width), BF16),
+            pltpu.SemaphoreType.DMA((2, 10)),
+            pltpu.SemaphoreType.DMA((4,)),
+        ],
+        compiler_params=pltpu.CompilerParams(
+            collective_id=collective_id, has_side_effects=True, vmem_limit_bytes=40 * 2**20
+        ),
+        cost_estimate=pl.CostEstimate(flops=1000, bytes_accessed=1000, transcendentals=0),
+        name="scatter_rows",
+    )(part)
+
+
+TILE = 256
+NT = (((1,), (1,)), ((), ()))
+LOWEST = -1e30
+
+
+def masked_tile(scores, at, tiles, shift):
+    scores = scores + shift
+    if at in (0, tiles - 1):
+        key_at = lax.broadcasted_iota(jnp.int32, scores.shape, 0)
+        query_at = lax.broadcasted_iota(jnp.int32, scores.shape, 1)
+        allowed = key_at > query_at if at == 0 else key_at <= query_at
+        scores = jnp.where(allowed, scores, LOWEST)
+    return scores
+
+def tile_shifts(pos_ref, start, tiles):
+    return [
+        jnp.where(pos_ref[0] - WINDOW + start + at * TILE >= 0, 0.0, LOWEST).astype(F32)
+        for at in range(tiles)
+    ]
+
+def attend_kernel(pos_ref, q_ref, k_ref, v_ref, out_ref, log_ref, turned_ref, score_ref):
+    tiles = WINDOW // TILE + 1
+
+    @pl.when(pl.program_id(0) == 0)
+    def _():
+        turned_ref[...] = v_ref[...].T
+
+    for start in range(0, q_ref.shape[0], TILE):
+        shifts = tile_shifts(pos_ref, start, tiles)
+        queries = q_ref[start : start + TILE, :]
+        top = jnp.full((1, TILE), LOWEST, F32)
+        for at in range(tiles):
+            keys = k_ref[start + at * TILE : start + (at + 1) * TILE, :]
+            scores = lax.dot_general(keys, queries, NT, preferred_element_type=F32)
+            scores = masked_tile(scores, at, tiles, shifts[at])
+            score_ref[at] = scores
+            top = jnp.maximum(top, jnp.max(scores, axis=0, keepdims=True))
+        total = jnp.zeros((1, TILE), F32)
+        for at in range(tiles):
+            expon = jnp.exp(score_ref[at] - top)
+            score_ref[at] = expon
+            total = total + jnp.sum(expon, axis=0, keepdims=True)
+        inverse = 1.0 / total
+        attended = jnp.zeros((v_ref.shape[1], TILE), F32)
+        for at in range(tiles):
+            probability = (score_ref[at] * inverse).astype(BF16)
+            values = turned_ref[:, start + at * TILE : start + (at + 1) * TILE]
+            attended = attended + jnp.dot(values, probability, preferred_element_type=F32)
+        out_ref[start : start + TILE, :] = attended.T.astype(BF16)
+        log_ref[0, :, start : start + TILE] = top + jnp.log(total)
+
+def attend(first_pos, queries, key_rows, value_rows):
+    rows, cols = queries.shape
+    span, size = key_rows.shape
+    heads = cols // size
+    return pl.pallas_call(
+        attend_kernel,
+        out_shape=(
+            jax.ShapeDtypeStruct((rows, cols), BF16),
+            jax.ShapeDtypeStruct((heads, 1, rows), F32),
+        ),
+        grid=(heads,),
+        in_specs=[
+            pl.BlockSpec(memory_space=pltpu.SMEM),
+            pl.BlockSpec((rows, size), lambda head: (0, head)),
+            pl.BlockSpec((span, size), lambda head: (0, 0)),
+            pl.BlockSpec((span, size), lambda head: (0, 0)),
+        ],
+        out_specs=(
+            pl.BlockSpec((rows, size), lambda head: (0, head)),
+            pl.BlockSpec((1, 1, rows), lambda head: (head, 0, 0)),
+        ),
+        scratch_shapes=[
+            pltpu.VMEM((size, span), BF16),
+            pltpu.VMEM((WINDOW // TILE + 1, TILE, TILE), F32),
+        ],
+        compiler_params=pltpu.CompilerParams(vmem_limit_bytes=40 * 2**20),
+        cost_estimate=pl.CostEstimate(flops=1000, bytes_accessed=1000, transcendentals=0),
+        name="attend",
+    )(first_pos.reshape(1), queries, key_rows, value_rows)
+
+def attend_back_kernel(
+    pos_ref, q_ref, g_ref, k_ref, v_ref, log_ref, cos_ref, sin_ref,
+    q_grad_ref, k_grad_ref, v_grad_ref, turned_ref, p_ref, gp_ref,
+):
+    tiles = WINDOW // TILE + 1
+    size = k_ref.shape[1]
+
+    @pl.when(pl.program_id(0) == 0)
+    def _():
+        turned_ref[...] = k_ref[...].T
+        k_grad_ref[...] = jnp.zeros_like(k_grad_ref)
+        v_grad_ref[...] = jnp.zeros_like(v_grad_ref)
+
+    for start in range(0, q_ref.shape[0], TILE):
+        shifts = tile_shifts(pos_ref, start, tiles)
+        block = slice(start, start + TILE)
+        queries, grads = q_ref[block, :], g_ref[block, :]
+        log_total = log_ref[0, :, block]
+        inner = jnp.zeros((1, TILE), F32)
+        for at in range(tiles):
+            span = slice(start + at * TILE, start + (at + 1) * TILE)
+            scores = lax.dot_general(k_ref[span, :], queries, NT, preferred_element_type=F32)
+            scores = masked_tile(scores, at, tiles, shifts[at])
+            probability = jnp.exp(scores - log_total)
+            grad = lax.dot_general(v_ref[span, :], grads, NT, preferred_element_type=F32)
+            inner = inner + jnp.sum(probability * grad, axis=0, keepdims=True)
+            p_ref[at] = probability
+            gp_ref[at] = grad
+        query_grad = jnp.zeros((size, TILE), F32)
+        for at in range(tiles):
+            span = slice(start + at * TILE, start + (at + 1) * TILE)
+            probability = p_ref[at]
+            score_grad = (probability * (gp_ref[at] - inner)).astype(BF16)
+            k_grad_ref[span, :] += jnp.dot(score_grad, queries, preferred_element_type=F32)
+            v_grad_ref[span, :] += jnp.dot(
+                probability.astype(BF16), grads, preferred_element_type=F32
+            )
+            query_grad = query_grad + jnp.dot(
+                turned_ref[:, span], score_grad, preferred_element_type=F32
+            )
+        query_grad = query_grad.T * size ** (-0.5)
+        turn = cos_ref.shape[1]
+        rotated = query_grad[:, :turn]
+        rotated = (
+            rotated * cos_ref[block, :] + pltpu.roll(rotated, turn // 2, 1) * sin_ref[block, :]
+        )
+        q_grad_ref[block, :turn] = rotated.astype(BF16)
+        q_grad_ref[block, turn:] = query_grad[:, turn:].astype(BF16)
+
+def attend_back(first_pos, queries, grads, key_rows, value_rows, log_total, cosine, sine):
+    rows, cols = queries.shape
+    span, size = key_rows.shape
+    heads = cols // size
+    by_head = pl.BlockSpec((rows, size), lambda head: (0, head))
+    whole = pl.BlockSpec((span, size), lambda head: (0, 0))
+    tile_shape = (WINDOW // TILE + 1, TILE, TILE)
+    return pl.pallas_call(
+        attend_back_kernel,
+        out_shape=(
+            jax.ShapeDtypeStruct((rows, cols), BF16),
+            jax.ShapeDtypeStruct((span, size), F32),
+            jax.ShapeDtypeStruct((span, size), F32),
+        ),
+        grid=(heads,),
+        in_specs=[
+            pl.BlockSpec(memory_space=pltpu.SMEM), by_head, by_head, whole, whole,
+            pl.BlockSpec((1, 1, rows), lambda head: (head, 0, 0)),
+            pl.BlockSpec(cosine.shape, lambda head: (0, 0)),
+            pl.BlockSpec(sine.shape, lambda head: (0, 0)),
+        ],
+        out_specs=(by_head, whole, whole),
+        scratch_shapes=[
+            pltpu.VMEM((size, span), BF16),
+            pltpu.VMEM(tile_shape, F32),
+            pltpu.VMEM(tile_shape, F32),
+        ],
+        compiler_params=pltpu.CompilerParams(vmem_limit_bytes=48 * 2**20),
+        cost_estimate=pl.CostEstimate(flops=1000, bytes_accessed=1000, transcendentals=0),
+        name="attend_back",
+    )(first_pos.reshape(1), queries, grads, key_rows, value_rows, log_total, cosine, sine)
+
+def gelu_parts(gate):
+    root = 0.7978845608028654
+    square = gate * gate
+    tanh = jnp.tanh(root * gate * (1.0 + 0.044715 * square))
+    half = 0.5 * (1.0 + tanh)
+    slope = half + 0.5 * gate * (1.0 - tanh * tanh) * root * (1.0 + 3 * 0.044715 * square)
+    return gate * half, slope
+
+def ffn_kernel(x_ref, w_ref, act_ref, a_ref, b_ref, total_ref):
+    steps = 5
+    depth = w_ref.shape[0] // steps
+    total_ref[...] = jnp.dot(x_ref[:, :depth], w_ref[:depth, :], preferred_element_type=F32)
+    for step in range(1, steps):
+        part = slice(step * depth, (step + 1) * depth)
+        total_ref[...] += jnp.dot(x_ref[:, part], w_ref[part, :], preferred_element_type=F32)
+    hidden = act_ref.shape[1]
+    main = hidden // 128 * 128
+    for start in range(0, main, 128):
+        cols = slice(start, start + 128)
+        gate, up = total_ref[:, cols], total_ref[:, main + start : main + start + 128]
+        gelu, slope = gelu_parts(gate)
+        act_ref[:, cols] = (gelu * up).astype(BF16)
+        a_ref[:, cols] = (slope * up).astype(BF16)
+        b_ref[:, cols] = gelu.astype(BF16)
+    last = total_ref[:, 2 * main :]
+    up = pltpu.roll(last, 64, 1)
+    gelu, slope = gelu_parts(last)
+    act_ref[:, main:] = (gelu * up)[:, :64].astype(BF16)
+    a_ref[:, main:] = (slope * up)[:, :64].astype(BF16)
+    b_ref[:, main:] = gelu[:, :64].astype(BF16)
+
+def ffn(x, w, rows=512):
+    count, width = x.shape
+    hidden = w.shape[1] // 2
+    tile = pl.BlockSpec((rows, hidden), lambda i: (i, 0))
+    return pl.pallas_call(
+        ffn_kernel,
+        out_shape=(jax.ShapeDtypeStruct((count, hidden), BF16),) * 3,
+        grid=(count // rows,),
+        in_specs=[
+            pl.BlockSpec((rows, width), lambda i: (i, 0)),
+            pl.BlockSpec(w.shape, lambda i: (0, 0), pipeline_mode=pl.Buffered(1)),
+        ],
+        out_specs=(tile,) * 3,
+        scratch_shapes=[pltpu.VMEM((rows, 2 * hidden), F32)],
+        compiler_params=pltpu.CompilerParams(vmem_limit_bytes=56 * 2**20),
+        cost_estimate=pl.CostEstimate(flops=1000, bytes_accessed=1000, transcendentals=0),
+        name="ffn",
+    )(x, w)
+
+def ffn_back_kernel(c_ref, d_ref, a_ref, b_ref, w_ref, g_ref, out_ref):
+    hidden = a_ref.shape[1]
+    main = hidden // 128 * 128
+    act_grad = lax.dot_general(c_ref[...], d_ref[...], NT, preferred_element_type=F32)
+    g_ref[:, :main] = (act_grad[:, :main] * a_ref[:, :main].astype(F32)).astype(BF16)
+    g_ref[:, main : 2 * main] = (act_grad[:, :main] * b_ref[:, :main].astype(F32)).astype(BF16)
+    last = act_grad[:, main:]
+    g_ref[:, 2 * main :] = jnp.concatenate(
+        [last * a_ref[:, main:].astype(F32), last * b_ref[:, main:].astype(F32)], axis=1
+    ).astype(BF16)
+    out_ref[...] = lax.dot_general(
+        g_ref[...], w_ref[...], NT, preferred_element_type=F32
+    ).astype(BF16)
+
+def ffn_back(cot, down, a, b, w, rows=256):
+    count, width = cot.shape
+    hidden = a.shape[1]
+    by_rows = lambda cols: pl.BlockSpec((rows, cols), lambda i: (i, 0))
+    once = lambda v: pl.BlockSpec(v.shape, lambda i: (0, 0), pipeline_mode=pl.Buffered(1))
+    return pl.pallas_call(
+        ffn_back_kernel,
+        out_shape=(
+            jax.ShapeDtypeStruct((count, 2 * hidden), BF16),
+            jax.ShapeDtypeStruct((count, width), BF16),
+        ),
+        grid=(count // rows,),
+        in_specs=[by_rows(width), once(down), by_rows(hidden), by_rows(hidden), once(w)],
+        out_specs=(by_rows(2 * hidden), by_rows(width)),
+        compiler_params=pltpu.CompilerParams(vmem_limit_bytes=56 * 2**20),
+        cost_estimate=pl.CostEstimate(flops=1000, bytes_accessed=1000, transcendentals=0),
+        name="ffn_back",
+    )(cot, down, a, b, w)
 
 
 def local(
@@ -125,10 +542,11 @@
         far = [swap(piece) if at or other is None else other for at, piece in enumerate(near)]
         return jnp.concatenate(near + far, axis=0)
 
-    def plane_sum(partial):
+    def plane_sum(partial, gate=None):
         count = seqs * half
         cores = partial[:count].astype(F32) + swap(partial[count:].astype(BF16)).astype(F32)
-        return plane_scatter(cores[:half], [cores[j * half : (j + 1) * half] for j in range(1, seqs)])
+        others = [cores[j * half : (j + 1) * half] for j in range(1, seqs)]
+        return plane_scatter(cores[:half], others, gate)
 
     def order_cols(pieces):
         stacked = jnp.stack(pieces)
@@ -153,12 +571,12 @@
         part_of(proj_shard, seq_at, proj_cols, 1), "fsdp", axis=0, tiled=True
     )
     out_rows = head_cols // seqs
-    out_quarter = lax.all_gather(
-        part_of(w_out, seq_at, out_rows, 0), "fsdp", axis=1, tiled=True
-    )
     hidden = w_gate.shape[1] // seqs
+    kernels = hidden % 128 == 64
+    main = hidden // 128 * 128 if kernels else hidden
+    gate_mine, up_mine = (part_of(value, seq_at, hidden, 1) for value in (w_gate, w_up))
     pair_in = jnp.concatenate(
-        [part_of(w_gate, seq_at, hidden, 1), part_of(w_up, seq_at, hidden, 1)], axis=1
+        [gate_mine[:, :main], up_mine[:, :main], gate_mine[:, main:], up_mine[:, main:]], axis=1
     )
     in_weight = lax.all_gather(pair_in, "fsdp", axis=0, tiled=True)
     down_weight = lax.all_gather(
@@ -168,7 +586,15 @@
     source = inputs.astype(F32)
     inverse_one = inverse_rms(source)
     unit_one = (source * inverse_one * gains[0]).astype(BF16)
-    rows_one = plane_rows(my_half(unit_one), other_half(unit_one))
+    square = seqs == 4
+    unit_one_half = my_half(unit_one)
+    rows_one = (
+        gather_rows(unit_one_half, 1) if square
+        else plane_rows(unit_one_half, other_half(unit_one))
+    )
+    out_quarter = lax.all_gather(
+        part_of(after(w_out, rows_one), seq_at, out_rows, 0), "fsdp", axis=1, tiled=True
+    )
     proj = jnp.dot(rows_one, proj_weight, preferred_element_type=F32)
     rotate_first = proj_cols % (2 * rot_half) == 0
     if rotate_first:
@@ -193,13 +619,16 @@
         exchange(proj[:, at].reshape(rows, proj_cols), at) for at in range(1, seqs)
     ]
     proj_here = jnp.concatenate(order_cols(proj_parts), axis=1)
-    queries = proj_here[:, :head_cols].reshape(rows, heads_here, head_size)
+    queries = proj_here[:, :head_cols]
     pair_here = proj_here[:, head_cols:]
     if not rotate_first:
-        queries = (rotate(queries.astype(F32), cosine[:, None], sine[:, None]) * scale).astype(BF16)
+        queries = queries.reshape(rows, heads_here, head_size).astype(F32)
+        queries = (rotate(queries, cosine[:, None], sine[:, None]) * scale).astype(BF16)
+        queries = queries.reshape(rows, head_cols)
         pair_here = jnp.where(first, rotate(pair_here.astype(F32), cosine, sine), pair_here)
         pair_here = pair_here.astype(BF16)
 
+    pair_here, out_quarter = lax.optimization_barrier((pair_here, out_quarter))
     earlier = seq_shift(pair_here, 1)
     slots = [
         lax.ppermute(
@@ -213,96 +642,56 @@
     key_rows = jnp.where(first, window_here, window_other)
     value_rows = jnp.where(first, window_other, window_here)
 
-    query_at = jnp.arange(rows, dtype=jnp.int32)[:, None]
-    key_at = jnp.arange(key_span, dtype=jnp.int32)[None, :]
-    allowed = (
-        (key_at > query_at) & (key_at <= query_at + WINDOW) & (first_pos - WINDOW + key_at >= 0)
-    )
-
-    def score_all():
-        raw_scores = jnp.einsum("rhd,kd->hrk", queries, key_rows, preferred_element_type=F32)
-        return jnp.where(allowed[None], raw_scores, -1e30)
-
-    scores = score_all()
-    row_max = jnp.max(scores, axis=-1, keepdims=True)
-    expon = jnp.exp(scores - row_max)
-    denominator = jnp.sum(expon, axis=-1, keepdims=True)
-    probability = expon / denominator
-    log_total = row_max + jnp.log(denominator)
-    attended = jnp.einsum(
-        "hrk,kd->rhd", probability.astype(BF16), value_rows, preferred_element_type=F32
-    )
-    head_outputs = attended.reshape(rows, head_cols).astype(BF16)
-
     out_weight = jnp.zeros((head_cols, width), BF16)
     for at, piece in enumerate(plane_gather(out_quarter)):
         out_weight = lax.dynamic_update_slice_in_dim(
             out_weight, piece, (seq_at ^ at) * out_rows, 0
         )
+
+    head_outputs, log_total = attend(first_pos, queries, key_rows, value_rows)
+
     out_part = jnp.dot(head_outputs, out_weight, preferred_element_type=F32)
     hidden_in = my_half(source) + my_half(out_part) + swap(other_half(out_part))
     inverse_two = inverse_rms(hidden_in)
     unit_two = (hidden_in * inverse_two * gains[1]).astype(BF16)
-    rows_two = plane_rows(unit_two)
-    cot_later = after(cotangent, window_here)
+    rows_two = gather_rows(unit_two, 2) if square else plane_rows(unit_two)
+    cot_later = after(cotangent, out_weight)
     rows_cot = plane_rows(my_half(cot_later), other_half(cot_later))
 
-    in_proj = jnp.dot(rows_two, in_weight, preferred_element_type=F32)
-    gate_pre, up_proj = in_proj[:, :hidden], in_proj[:, hidden:]
-    activation = gated_unit(gate_pre, up_proj).astype(BF16)
-    grad_activation = times_transpose(rows_cot, down_weight)
-    grad_gate, grad_up = jax.vjp(gated_unit, gate_pre, up_proj)[1](grad_activation)
-    grad_in = jnp.concatenate([grad_gate.astype(BF16), grad_up.astype(BF16)], axis=1)
-    grad_unit_two = plane_sum(times_transpose(grad_in, in_weight))
+    if kernels:
+        activation, gate_factor, up_factor = ffn(rows_two, in_weight)
+        down_term = rows_product(rows_cot, activation).astype(BF16)
+        gate_factor = after(gate_factor, down_term)
+        grad_in, back_part = ffn_back(rows_cot, down_weight, gate_factor, up_factor, in_weight)
+    else:
+        in_proj = jnp.dot(rows_two, in_weight, preferred_element_type=F32)
+        gate_pre, up_proj = in_proj[:, :hidden], in_proj[:, hidden:]
+        activation = gated_unit(gate_pre, up_proj).astype(BF16)
+        down_term = rows_product(rows_cot, activation).astype(BF16)
+        grad_activation = times_transpose(rows_cot, down_weight)
+        grad_gate, grad_up = jax.vjp(gated_unit, gate_pre, up_proj)[1](grad_activation)
+        grad_in = jnp.concatenate([grad_gate.astype(BF16), grad_up.astype(BF16)], axis=1)
+        back_part = times_transpose(grad_in, in_weight)
+    in_term = rows_product(rows_two, grad_in).astype(BF16)
+    back_part = after(back_part, in_term)
+    grad_unit_two = scatter_rows(back_part, 3) if square else plane_sum(back_part)
     grad_hidden = my_half(cotangent).astype(F32) + norm_pull(
         hidden_in, inverse_two, grad_unit_two * gains[1]
     )
-    ffn_out = plane_sum(
-        jnp.dot(after(activation, grad_unit_two), down_weight, preferred_element_type=F32)
-    )
-    layer_out = whole_rows((hidden_in + ffn_out).astype(BF16))
-
-    in_term = rows_product(rows_two, grad_in).astype(BF16)
-    down_term = rows_product(activation, rows_cot).astype(BF16)
+    out_rows_part = jnp.dot(
+        after(activation, grad_unit_two), down_weight, preferred_element_type=F32
+    )
+    down_shard = lax.psum_scatter(down_term, "fsdp", scatter_dimension=0, tiled=True).T
     in_shard = lax.psum_scatter(in_term, "fsdp", scatter_dimension=0, tiled=True)
-    down_shard = lax.psum_scatter(down_term, "fsdp", scatter_dimension=1, tiled=True)
-    in_parts = order_cols(plane_gather(in_shard))
-    gate_grad = jnp.concatenate([piece[:, :hidden] for piece in in_parts], axis=1).astype(F32)
-    up_grad = jnp.concatenate([piece[:, hidden:] for piece in in_parts], axis=1).astype(F32)
-    down_grad = jnp.concatenate(order_cols(plane_gather(down_shard)), axis=0).astype(F32)
-    gain_two_half = jnp.sum(
-        gate_grad * w_gate.astype(F32) + up_grad * w_up.astype(F32), axis=1
-    ) / gain_two[:, 0]
-
-    grad_attn_out = after(whole_rows(grad_hidden.astype(BF16)), in_term, down_term)
-    grad_heads = (
-        times_transpose(grad_attn_out, out_weight)
-        .reshape(rows, heads_here, head_size)
-        .astype(BF16)
-    )
-    out_term = rows_product(head_outputs, grad_attn_out).astype(BF16)
-    out_sum = plane_scatter(
-        part_of(out_term, seq_at, out_rows, 0),
-        [part_of(out_term, seq_at ^ at, out_rows, 0) for at in range(1, seqs)],
-    ).astype(BF16)
-    out_shard = lax.psum_scatter(out_sum, "fsdp", scatter_dimension=1, tiled=True)
-    out_grad = jnp.concatenate(order_cols(plane_gather(out_shard)), axis=0).astype(F32)
-
-    probability_again = jnp.exp(score_all() - log_total)
-    grad_probability = jnp.einsum(
-        "rhd,kd->hrk", grad_heads, value_rows, preferred_element_type=F32
-    )
-    inner = jnp.sum(probability_again * grad_probability, axis=-1, keepdims=True)
-    grad_scores = (probability_again * (grad_probability - inner)).astype(BF16)
-    grad_queries = jnp.einsum("hrk,kd->rhd", grad_scores, key_rows, preferred_element_type=F32)
-    grad_query_proj = (
-        rotate(grad_queries * scale, cosine[:, None], -sine[:, None])
-        .astype(BF16)
-        .reshape(rows, head_cols)
-    )
-    grad_keys = jnp.einsum("hrk,rhd->kd", grad_scores, queries, preferred_element_type=F32)
-    grad_values = jnp.einsum(
-        "hrk,rhd->kd", probability_again.astype(BF16), grad_heads, preferred_element_type=F32
+
+    grad_attn_out = whole_rows(grad_hidden.astype(BF16))
+    grad_heads = times_transpose(grad_attn_out, out_weight).astype(BF16)
+    grad_heads, out_rows_part, down_shard = lax.optimization_barrier(
+        (grad_heads, out_rows_part, down_shard)
+    )
+    grad_query_proj, grad_keys, grad_values = attend_back(
+        first_pos, queries, grad_heads, key_rows, value_rows, log_total,
+        jnp.concatenate([cosine, cosine], axis=1), jnp.concatenate([sine, -sine], axis=1),
     )
     pair_grads = jnp.where(first, grad_keys, grad_values) + swap(
         jnp.where(first, grad_values, grad_keys)
@@ -321,6 +710,7 @@
         earlier_total = earlier_total + jnp.where(shard_at >= at, piece, 0.0)
     own_total = own_total + seq_shift(earlier_total.astype(BF16), -1).astype(F32)
     grad_pair = jnp.where(first, rotate(own_total, cosine, -sine), own_total).astype(BF16)
+    grad_pair, in_shard = lax.optimization_barrier((grad_pair, in_shard))
     grad_proj = jnp.concatenate([grad_query_proj, grad_pair], axis=1)
     grad_parts = [part_of(grad_proj, seq_at, proj_cols, 1)] + [
         exchange(part_of(grad_proj, seq_at ^ at, proj_cols, 1), at) for at in range(1, seqs)
@@ -328,8 +718,41 @@
     grad_rows = jnp.stack(grad_parts).reshape(seqs, 2, half, proj_cols).swapaxes(0, 1)
     grad_rows = jnp.where(first, grad_rows, grad_rows[::-1]).reshape(2 * seqs * half, proj_cols)
 
+    ffn_out = plane_sum(after(out_rows_part, pair_grads), grad_pair)
+    layer_out = whole_rows((hidden_in + ffn_out).astype(BF16))
+    down_parts = lax.optimization_barrier((*plane_gather(down_shard), pair_grads))[:-1]
+    down_grad = jnp.concatenate(order_cols(down_parts), axis=0).astype(F32)
+    in_parts = order_cols(plane_gather(in_shard))
+    rest = hidden - main
+    gate_grad, up_grad = (
+        jnp.concatenate(
+            [
+                piece[:, first_at : first_at + count]
+                for piece in in_parts
+                for first_at, count in spans
+                if count
+            ],
+            axis=1,
+        ).astype(F32)
+        for spans in (((0, main), (2 * main, rest)), ((main, main), (2 * main + rest, rest)))
+    )
+    gain_two_half = jnp.sum(
+        gate_grad * w_gate.astype(F32) + up_grad * w_up.astype(F32), axis=1
+    ) / gain_two[:, 0]
+    out_term = rows_product(after(head_outputs, grad_rows), grad_attn_out).astype(BF16)
+    out_sum = plane_scatter(
+        part_of(out_term, seq_at, out_rows, 0),
+        [part_of(out_term, seq_at ^ at, out_rows, 0) for at in range(1, seqs)],
+    ).astype(BF16)
+    out_shard = lax.psum_scatter(out_sum, "fsdp", scatter_dimension=1, tiled=True)
+    out_grad = jnp.concatenate(order_cols(plane_gather(out_shard)), axis=0).astype(F32)
+
     proj_term = rows_product(rows_one, grad_rows).astype(BF16)
-    grad_unit_one = plane_sum(times_transpose(grad_rows, proj_weight))
+    grad_unit_one = times_transpose(grad_rows, proj_weight)
+    if square:
+        grad_unit_one = scatter_rows(after(grad_unit_one.astype(BF16), proj_term), 4)
+    else:
+        grad_unit_one = plane_sum(grad_unit_one)
     grad_input = whole_rows(
         grad_hidden + norm_pull(my_half(source), my_half(inverse_one), grad_unit_one * gains[0])
     )

time: 1170 us -> 1100 us (0.940)
  Pallas kernels: 0 us -> 388 us
  waiting for transfers between devices: 401 us -> 194 us
  matrix products: 255 us -> 100 us
  other arithmetic: 189 us -> 128 us
  local copies, waits for them, and re-layouts: 186 us -> 163 us
  starting transfers between devices: 112 us -> 98.2 us
    pallas_call x0 -> x8, Pallas kernels: none -> 388 us  [the longest x2 168 us: scatter_rows(): pl.pallas_call(sum_kernel, out_shape=jax.ShapeDtypeStruct((half, width),...]
    ppermute x50 -> x36, waiting for transfers between devices: 290 us -> 97.6 us  [exchange(): return lax.ppermute(value, 'seq', [(at, at ^ step) for at in range(count)])]
    dot_general x7 -> x0, matrix products: 93.3 us -> none  [the longest x1 27.9 us: local(): in_proj = jnp.dot(rows_two, in_weight, preferred_element_type=F32)]
    dot_general x4 -> x2, matrix products: 74.2 us -> 12.4 us  [times_transpose(): lax.dot_general(left, right, (((1,), (1,)), ((), ())), preferred_element_...]
    ppermute x21 -> x12, starting transfers between devices: 49.2 us -> 17.2 us  [swap(): return lax.ppermute(value, 'tensor', [(0, 1), (1, 0)])]
    another operation x6 -> x3, other arithmetic: 45 us -> 16.5 us
    reduce_scatter x1, waiting for transfers between devices: 33.3 us -> 11.9 us  [local(): lax.psum_scatter(in_term, 'fsdp', scatter_dimension=0, tiled=True)]
    convert_element_type x3, other arithmetic: 35.3 us -> 14.3 us  [the longest x1 12.2 us: local(): down_grad = jnp.concatenate(order_cols(down_parts), axis=0).astype(F32)]
  transfers between devices with their start and end apart: 90 -> 67, of which waited for: 36 -> 22; matrix products, arithmetic and copies ran while one was open for 46% -> 34% of each run, Pallas kernels for 0% -> 36%
where the time goes in v2:
time: 1100 us; the launch traced here: 1090 us
  Pallas kernels  388 us (35%)
  waiting for transfers between devices  194 us (18%)
  local copies, waits for them, and re-layouts  163 us (15%)
  other arithmetic  128 us (12%)
  matrix products  100 us (9%)
  starting transfers between devices  98.2 us (9%)
  between operations  15.8 us (1%)
    pallas_call x2, Pallas kernels, scatter_rows(): pl.pallas_call(sum_kernel, out_shape=jax.ShapeDtypeStruct((half, width),...  168 us
    pallas_call x2, Pallas kernels, gather_rows(): pl.pallas_call(rows_kernel, out_shape=jax.ShapeDtypeStruct((8 * half, wid...  102 us
    ppermute x36, waiting for transfers between devices, exchange(): return lax.ppermute(value, 'seq', [(at, at ^ step) for at in range(count)])  97.6 us
    dot_general x4, matrix products, rows_product(): lax.dot_general(left, right, (((0,), (0,)), ((), ())), preferred_element_...  59.4 us
    ppermute x36, starting transfers between devices, exchange(): return lax.ppermute(value, 'seq', [(at, at ^ step) for at in range(count)])  59.3 us
    unnamed x129, local copies, waits for them, and re-layouts  57.2 us
    pallas_call x1, Pallas kernels, ffn_back(): pl.pallas_call(ffn_back_kernel, out_shape=(jax.ShapeDtypeStruct((count, 2...  42.3 us
    ppermute x3, waiting for transfers between devices, local(): lax.ppermute(jnp.where(shard_at >= at, earlier, pair_here), 'fsdp', [(sou...  40.9 us
  transfers between devices with their start and end apart: 67, of which 22 were waited for; matrix products, arithmetic and copies ran while one was open for 34% of the time, Pallas kernels for 36%

profile of v2, /device:TPU:9, one launch (start us, length us, event | category | flops | bytes accessed | tf_op | source)
XLA Modules:
  0.0 1088.1 jit_solution(11635714391618426518)
XLA Ops:
  26.6 51.8 %gather_rows.2 = bf16[2048,2560]{1,0:T(8,128)(2,1)} custom-call(bf16[256,2560]{1,0:T(8,128)(2,1)} %multiply_convert_fusion.1.own_ref), custom_call_target="tpu_custom_call" | custom-call | flops 1000 | bytes 1000 | tf_op jit(solution)/shard_map/gather_rows/pallas_call | solution.py:152
  136.5 15.3 %collective-permute-done.7 = bf16[512,256]{1,0:T(8,128)(2,1)} collective-permute-done((bf16[512,256]{1,0:T(8,128)(2,1)}, bf16[512,256]{1,0:T(8,128)(2,1)}, u32[]{:S(2)}, u32[]{:S(2)}) %collective-permute-start.7) | collective-permute-done | bytes 262176 | tf_op jit(solution)/shard_map/ppermute | solution.py:634
  153.5 9.2 collective-permute-done.8
  164.4 16.4 %collective-permute-done.9 = bf16[512,256]{1,0:T(8,128)(2,1)} collective-permute-done((bf16[512,256]{1,0:T(8,128)(2,1)}, bf16[512,256]{1,0:T(8,128)(2,1)}, u32[]{:S(2)}, u32[]{:S(2)}) %collective-permute-start.9) | collective-permute-done | bytes 262176 | tf_op jit(solution)/shard_map/ppermute | solution.py:634
  200.9 15.4 %attend.1 = (bf16[512,1280]{1,0:T(8,128)(2,1)S(1)}, f32[5,1,512]{2,1,0:T(1,128)S(1)}) custom-call(s32[1]{0:T(128)} %bitcast.pos_ref, bf16[512,1280]{1,0:T(8,128)(2,1)S(1)} %pad_maximum_fusion.7.q_ref, bf16[2560,256]{1,0:T(8,128)(2,1)S(1)} %get-tuple-element.111.k_ref, bf16[2560,256]{1,0:T(8,128)(2,1)S(1)} %get-tuple-element.110.v_ref), custom_call_target="tpu_custom_call" | custom-call | flops 1000 | bytes 1000 | tf_op jit(solution)/shard_map/attend/pallas_call | solution.py:317
  233.8 17.0 %collective-permute-done.17 = bf16[256,2560]{1,0:T(8,128)(2,1)} collective-permute-done((bf16[256,2560]{1,0:T(8,128)(2,1)}, bf16[256,2560]{1,0:T(8,128)(2,1)}, u32[]{:S(2)}, u32[]{:S(2)}) %collective-permute-start.17) | collective-permute-done | bytes 1310752 | tf_op jit(solution)/shard_map/ppermute | solution.py:16
  280.5 50.6 %gather_rows.3.x_ref = bf16[2048,2560]{1,0:T(8,128)(2,1)} custom-call(bf16[256,2560]{1,0:T(8,128)(2,1)} %multiply_convert_fusion.own_ref), custom_call_target="tpu_custom_call" | custom-call | flops 1000 | bytes 1000 | tf_op jit(solution)/shard_map/gather_rows/pallas_call | solution.py:152
  338.6 33.1 %ffn.1 = (bf16[2048,960]{1,0:T(8,128)(2,1)}, bf16[2048,960]{1,0:T(8,128)(2,1)}, bf16[2048,960]{1,0:T(8,128)(2,1)}) custom-call(bf16[2048,2560]{1,0:T(8,128)(2,1)} %gather_rows.3.x_ref, bf16[2560,1920]{1,0:T(8,128)(2,1)} %all-gather.11.cloned.1.call-done.w_ref), custom_call_target="tpu_custom_call" | custom-call | flops 1000 | bytes 1000 | tf_op jit(solution)/shard_map/ffn/pallas_call | solution.py:459
  371.7 15.8 %convolution_convert_fusion.3 = bf16[2560,960]{0,1:T(8,128)(2,1)} fusion(bf16[2048,2560]{1,0:T(8,128)(2,1)} %constant_dynamic-update-slice_fusion.5.c_ref, bf16[2048,960]{1,0:T(8,128)(2,1)} %get-tuple-element.55), kind=kOutput, calls=%fused_computation.7 | convolution fusion | flops 10068787200 | bytes 19333120 | tf_op jit(solution)/shard_map/dot_general | solution.py:54
  401.7 42.3 %ffn_back.1 = (bf16[2048,1920]{1,0:T(8,128)(2,1)}, bf16[2048,2560]{1,0:T(8,128)(2,1)}) custom-call(bf16[2048,2560]{1,0:T(8,128)(2,1)} %constant_dynamic-update-slice_fusion.5.c_ref, bf16[960,2560]{1,0:T(8,128)(2,1)} %all-gather.9.cloned.1.call-done.d_ref, bf16[2048,960]{1,0:T(8,128)(2,1)} %get-tuple-element.50.a_ref, ...), custom_call_target="tpu_custom_call" | custom-call | flops 1000 | bytes 1000 | tf_op jit(solution)/shard_map/ffn_back/pallas_call | solution.py:493
  444.0 28.1 %convolution_convert_fusion = bf16[2560,1920]{1,0:T(8,128)(2,1)} fusion(bf16[2048,2560]{1,0:T(8,128)(2,1)} %gather_rows.3.x_ref, bf16[2048,1920]{1,0:T(8,128)(2,1)} %get-tuple-element.53), kind=kOutput, calls=%fused_computation | convolution fusion | flops 20137574400 | bytes 28180480 | tf_op jit(solution)/shard_map/dot_general | solution.py:54
  477.4 50.4 %scatter_rows.2 = f32[256,2560]{1,0:T(8,128)S(1)} custom-call(bf16[2048,2560]{1,0:T(8,128)(2,1)S(1)} %copy-done.7), custom_call_target="tpu_custom_call" | custom-call | flops 1000 | bytes 1000 | tf_op jit(solution)/shard_map/scatter_rows/pallas_call | solution.py:241
  530.5 17.2 %fusion.38 = f32[2048,2560]{1,0:T(8,128)} fusion(bf16[2048,960]{1,0:T(8,128)(2,1)} %get-tuple-element.55, bf16[960,2560]{1,0:T(8,128)(2,1)S(1)} %bitcast.137), kind=kOutput, calls=%fused_computation.200 | convolution fusion | flops 10066329600 | bytes 29818880 | tf_op jit(solution)/shard_map/dot_general | solution.py:681
  560.6 26.7 %attend_back.1 = (bf16[512,1280]{1,0:T(8,128)(2,1)S(1)}, f32[2560,256]{1,0:T(8,128)}, f32[2560,256]{1,0:T(8,128)}) custom-call(s32[1]{0:T(128)} %bitcast.pos_ref, bf16[512,1280]{1,0:T(8,128)(2,1)S(1)} %copy-done.3, bf16[512,1280]{1,0:T(8,128)(2,1)S(1)} %copy-done.10, bf16[2560,256]{1,0:T(8,128)(2,1)S(1)} %copy-done.6, bf16[2560,256]{1,0:T(8,128)(2,1)} %copy-done.4, ...), custom_call_target="tpu_custom_call" | custom-call | flops 1000 | bytes 1000 | tf_op jit(solution)/shard_map/attend_back/pallas_call | solution.py:399
  616.9 13.3 %fusion.24 = (bf16[1024,2560]{1,0:T(8,128)(2,1)}, f32[1024,2560]{1,0:T(8,128)}) fusion(bf16[1024,2560]{1,0:T(8,128)(2,1)} %collective-permute-done.25, f32[2048,2560]{1,0:T(8,128)} %fusion.38), kind=kLoop, calls=%fused_computation.186 | loop fusion | flops 7864320 | bytes 31457280 | tf_op jit(solution)/shard_map/convert.5
  635.0 26.0 %collective-permute-done.30 = bf16[512,256]{1,0:T(8,128)(2,1)S(1)} collective-permute-done((bf16[512,256]{1,0:T(8,128)(2,1)}, bf16[512,256]{1,0:T(8,128)(2,1)S(1)}, u32[]{:S(2)}, u32[]{:S(2)}) %collective-permute-start.30) | collective-permute-done | bytes 262176 | tf_op jit(solution)/shard_map/ppermute | solution.py:700
  680.1 11.9 %reduce-scatter.9.cloned.1.call-done = bf16[640,1920]{1,0:T(8,128)(2,1)} async-done(((bf16[2560,1920]{1,0:T(8,128)(2,1)}), bf16[640,1920]{1,0:T(8,128)(2,1)}) %reduce-scatter.9.cloned.1.call-update) | async-done | bytes 2457616 | tf_op jit(solution)/shard_map/reduce_scatter | solution.py:685
  697.6 18.9 %collective-permute-start.36 = (bf16[512,384]{1,0:T(8,128)(2,1)}, bf16[512,384]{1,0:T(8,128)(2,1)}, u32[]{:S(2)}, u32[]{:S(2)}) collective-permute-start(bf16[512,384]{1,0:T(8,128)(2,1)} %get-tuple-element.137), channel_id=1, source_target_pairs={{0,24},{8,16},{16,8},{24,0},{1,25},{9,17},{17,9},{25,1},{2,26},{10... | collective-permute-start | bytes 1179656 | tf_op jit(solution)/shard_map/ppermute | solution.py:16
  721.1 31.3 %collective-permute-done.27 = bf16[256,2560]{1,0:T(8,128)(2,1)} collective-permute-done((bf16[256,2560]{1,0:T(8,128)(2,1)}, bf16[256,2560]{1,0:T(8,128)(2,1)}, u32[]{:S(2)}, u32[]{:S(2)}) %collective-permute-start.27) | collective-permute-done | bytes 1310752 | tf_op jit(solution)/shard_map/ppermute | solution.py:16
  777.5 9.8 convolution_convert_fusion.4
  809.0 117.3 %scatter_rows.3 = f32[256,2560]{1,0:T(8,128)S(1)} custom-call(bf16[2048,2560]{1,0:T(8,128)(2,1)S(1)} %convolution_convert_fusion.2.part_ref), custom_call_target="tpu_custom_call" | custom-call | flops 1000 | bytes 1000 | tf_op jit(solution)/shard_map/scatter_rows/pallas_call | solution.py:241
  941.8 12.2 %maximum_convert_fusion = f32[3840,640]{1,0:T(8,128)} fusion(bf16[960,640]{1,0:T(8,128)(2,1)S(1)} %get-tuple-element.101, bf16[960,640]{1,0:T(8,128)(2,1)S(1)} %get-tuple-element.102, bf16[960,640]{1,0:T(8,128)(2,1)S(1)} %get-tuple-element.103, bf16[960,640]{1,0:T(8,128)(2,1)S(1)} %get-tuple-element.100), kind=kLoop, calls=%fused_computation.11 | loop fusion | flops 19660800 | bytes 14745600 | tf_op jit(solution)/shard_map/convert_element_type | solution.py:724
  969.6 15.7 %collective-permute-done.44 = bf16[320,1920]{1,0:T(8,128)(2,1)S(1)} collective-permute-done((bf16[320,1920]{1,0:T(8,128)(2,1)}, bf16[320,1920]{1,0:T(8,128)(2,1)S(1)}, u32[]{:S(2)}, u32[]{:S(2)}) %collective-permute-start.44) | collective-permute-done | bytes 1228832 | tf_op jit(solution)/shard_map/ppermute | solution.py:16
  1032.6 17.6 %add_reduce_fusion = (f32[640]{0:T(1024)S(1)}, f32[640,3840]{1,0:T(8,128)}, f32[640,3840]{1,0:T(8,128)}) fusion(bf16[640,3840]{1,0:T(8,128)(2,1)} %param.20, bf16[640,3840]{1,0:T(8,128)(2,1)} %param.19, bf16[640,3840]{1,0:T(8,128)(2,1)} %concatenate.85, bf16[640,3840]{1,0:T(8,128)(2,1)} %concatenate.86), kind=kLoop, calls=%fused_computation.6 | loop fusion | flops 19660160 | bytes 39324160 | tf_op jit(solution)/shard_map/reduce_sum | solution.py:739
  (405 shorter events, 409.0 us)
Async XLA Ops:
  7.2 81.4 %all-gather.5.cloned.1.call-start = ((), (), s32[]{:S(2)}) async-start(), calls=%async_computation.4 | async-start | bytes 2457600 | tf_op jit(solution)/shard_map/all_gather | solution.py:570
  11.1 112.8 %all-gather.7.cloned.1.call-start = ((), (), s32[]{:S(2)}) async-start(), calls=%async_computation.5 | async-start | bytes 2048000 | tf_op jit(solution)/shard_map/all_gather | solution.py:595
  79.3 259.3 %all-gather.11.cloned.1.call-start = ((), (), s32[]{:S(2)}) async-start(), calls=%async_computation.7 | async-start | bytes 12288000 | tf_op jit(solution)/shard_map/all_gather | solution.py:581
  86.2 315.5 %all-gather.9.cloned.1.call-start = ((), (), s32[]{:S(2)}) async-start(), calls=%async_computation.6 | async-start | bytes 6144000 | tf_op jit(solution)/shard_map/all_gather | solution.py:582
  127.7 71.6 %collective-permute-start.11 = (bf16[320,2560]{1,0:T(8,128)(2,1)}, bf16[320,2560]{1,0:T(8,128)(2,1)S(1)}, u32[]{:S(2)}, u32[]{:S(2)}) collective-permute-start(bf16[320,2560]{1,0:T(8,128)(2,1)} %all-gather.7.cloned.1.call-done), channel_id=1, source_target_pairs={{0,8},{8,0},{16,24},{24,16},{1,9},{9,1},{17,25},{25,17},{2,10},{10... | collective-permute-start | bytes 4915208 | tf_op jit(solution)/shard_map/ppermute | solution.py:16
  233.7 320.5 %reduce-scatter.13.cloned.1.call-start = ((), (), s32[]{:S(2)}) async-start(), calls=%async_computation.10 | async-start | bytes 6553600
  255.0 76.1 %collective-permute-start.20 = (bf16[256,2560]{1,0:T(8,128)(2,1)}, bf16[256,2560]{1,0:T(8,128)(2,1)}, u32[]{:S(2)}, u32[]{:S(2)}) collective-permute-start(bf16[256,2560]{1,0:T(8,128)(2,1)} %collective-permute-done.16), channel_id=1, source_target_pairs={{0,1},{1,0},{2,3},{3,2},{4,5},{5,4},{6,7},{7,6},{8,9},{9,8},{10,11... | collective-permute-start | bytes 3932168 | tf_op jit(solution)/shard_map/ppermute | solution.py:20
  257.5 76.1 %collective-permute-start.21 = (bf16[256,2560]{1,0:T(8,128)(2,1)}, bf16[256,2560]{1,0:T(8,128)(2,1)}, u32[]{:S(2)}, u32[]{:S(2)}) collective-permute-start(bf16[256,2560]{1,0:T(8,128)(2,1)} %collective-permute-done.17), channel_id=1, source_target_pairs={{0,1},{1,0},{2,3},{3,2},{4,5},{5,4},{6,7},{7,6},{8,9},{9,8},{10,11... | collective-permute-start | bytes 3932168 | tf_op jit(solution)/shard_map/ppermute | solution.py:20
  269.8 66.3 %collective-permute-start.22 = (bf16[256,2560]{1,0:T(8,128)(2,1)}, bf16[256,2560]{1,0:T(8,128)(2,1)}, u32[]{:S(2)}, u32[]{:S(2)}) collective-permute-start(bf16[256,2560]{1,0:T(8,128)(2,1)} %pad_maximum_fusion.10), channel_id=1, source_target_pairs={{0,1},{1,0},{2,3},{3,2},{4,5},{5,4},{6,7},{7,6},{8,9},{9,8},{10,11... | collective-permute-start | bytes 3932168 | tf_op jit(solution)/shard_map/ppermute | solution.py:20
  395.5 296.5 %reduce-scatter.9.cloned.1.call-start = ((), (), s32[]{:S(2)}) async-start(), calls=%async_computation.8 | async-start | bytes 12288000 | tf_op jit(solution)/shard_map/reduce_scatter | solution.py:685
  472.1 535.9 %reduce-scatter.11.cloned.1.call-start = ((), (), s32[]{:S(2)}) async-start(), calls=%async_computation.9 | async-start | bytes 2457600 | tf_op jit(solution)/shard_map/reduce_scatter | solution.py:759
  605.4 66.7 %collective-permute-start.55 = (bf16[960,640]{1,0:T(8,128)(2,1)}, bf16[960,640]{1,0:T(8,128)(2,1)}, u32[]{:S(2)}, u32[]{:S(2)}) collective-permute-start(bf16[960,640]{1,0:T(8,128)(2,1)} %bitcast.133), channel_id=1, source_target_pairs={{0,8},{8,0},{16,24},{24,16},{1,9},{9,1},{17,25},{25,17},{2,10},{10... | collective-permute-start | bytes 3686408 | tf_op jit(solution)/shard_map/ppermute | solution.py:16
  634.4 63.3 %collective-permute-start.26 = (bf16[256,2560]{1,0:T(8,128)(2,1)}, bf16[256,2560]{1,0:T(8,128)(2,1)}, u32[]{:S(2)}, u32[]{:S(2)}) collective-permute-start(bf16[256,2560]{1,0:T(8,128)(2,1)} %get-tuple-element.99), channel_id=1, source_target_pairs={{0,8},{8,0},{16,24},{24,16},{1,9},{9,1},{17,25},{25,17},{2,10},{10... | collective-permute-start | bytes 3932168 | tf_op jit(solution)/shard_map/ppermute | solution.py:16
  674.7 77.7 %collective-permute-start.27 = (bf16[256,2560]{1,0:T(8,128)(2,1)}, bf16[256,2560]{1,0:T(8,128)(2,1)}, u32[]{:S(2)}, u32[]{:S(2)}) collective-permute-start(bf16[256,2560]{1,0:T(8,128)(2,1)} %get-tuple-element.98), channel_id=1, source_target_pairs={{0,16},{8,24},{16,0},{24,8},{1,17},{9,25},{17,1},{25,9},{2,18},{10... | collective-permute-start | bytes 3932168 | tf_op jit(solution)/shard_map/ppermute | solution.py:16
  675.5 77.8 %collective-permute-start.28 = (bf16[256,2560]{1,0:T(8,128)(2,1)}, bf16[256,2560]{1,0:T(8,128)(2,1)}, u32[]{:S(2)}, u32[]{:S(2)}) collective-permute-start(bf16[256,2560]{1,0:T(8,128)(2,1)} %get-tuple-element.97), channel_id=1, source_target_pairs={{0,24},{8,16},{16,8},{24,0},{1,25},{9,17},{17,9},{25,1},{2,26},{10... | collective-permute-start | bytes 3932168 | tf_op jit(solution)/shard_map/ppermute | solution.py:16
  696.4 64.4 %collective-permute-start.35 = (bf16[512,384]{1,0:T(8,128)(2,1)}, bf16[512,384]{1,0:T(8,128)(2,1)}, u32[]{:S(2)}, u32[]{:S(2)}) collective-permute-start(bf16[512,384]{1,0:T(8,128)(2,1)} %get-tuple-element.138), channel_id=1, source_target_pairs={{0,16},{8,24},{16,0},{24,8},{1,17},{9,25},{17,1},{25,9},{2,18},{10... | collective-permute-start | bytes 1179656 | tf_op jit(solution)/shard_map/ppermute | solution.py:16
  697.6 66.1 %collective-permute-start.36 = (bf16[512,384]{1,0:T(8,128)(2,1)}, bf16[512,384]{1,0:T(8,128)(2,1)}, u32[]{:S(2)}, u32[]{:S(2)}) collective-permute-start(bf16[512,384]{1,0:T(8,128)(2,1)} %get-tuple-element.137), channel_id=1, source_target_pairs={{0,24},{8,16},{16,8},{24,0},{1,25},{9,17},{17,9},{25,1},{2,26},{10... | collective-permute-start | bytes 1179656 | tf_op jit(solution)/shard_map/ppermute | solution.py:16
  752.4 183.4 %collective-permute-start.43 = (bf16[640,1920]{1,0:T(8,128)(2,1)}, bf16[640,1920]{1,0:T(8,128)(2,1)}, u32[]{:S(2)}, u32[]{:S(2)}) collective-permute-start(bf16[640,1920]{1,0:T(8,128)(2,1)} %reduce-scatter.9.cloned.1.call-done), channel_id=1, source_target_pairs={{0,16},{8,24},{16,0},{24,8},{1,17},{9,25},{17,1},{25,9},{2,18},{10... | collective-permute-start | bytes 7372808 | tf_op jit(solution)/shard_map/ppermute | solution.py:16
  753.3 203.1 %collective-permute-start.42 = (bf16[640,1920]{1,0:T(8,128)(2,1)}, bf16[640,1920]{1,0:T(8,128)(2,1)}, u32[]{:S(2)}, u32[]{:S(2)}) collective-permute-start(bf16[640,1920]{1,0:T(8,128)(2,1)} %reduce-scatter.9.cloned.1.call-done), channel_id=1, source_target_pairs={{0,8},{8,0},{16,24},{24,16},{1,9},{9,1},{17,25},{25,17},{2,10},{10... | collective-permute-start | bytes 7372808 | tf_op jit(solution)/shard_map/ppermute | solution.py:16
  797.3 165.5 %collective-permute-start.48 = (bf16[320,2560]{1,0:T(8,128)(2,1)}, bf16[320,2560]{1,0:T(8,128)(2,1)}, u32[]{:S(2)}, u32[]{:S(2)}) collective-permute-start(bf16[320,2560]{1,0:T(8,128)(2,1)} %get-tuple-element.94), channel_id=1, source_target_pairs={{0,8},{8,0},{16,24},{24,16},{1,9},{9,1},{17,25},{25,17},{2,10},{10... | collective-permute-start | bytes 4915208 | tf_op jit(solution)/shard_map/ppermute | solution.py:16
  799.9 163.5 %collective-permute-start.49 = (bf16[320,2560]{1,0:T(8,128)(2,1)}, bf16[320,2560]{1,0:T(8,128)(2,1)}, u32[]{:S(2)}, u32[]{:S(2)}) collective-permute-start(bf16[320,2560]{1,0:T(8,128)(2,1)} %get-tuple-element.96), channel_id=1, source_target_pairs={{0,16},{8,24},{16,0},{24,8},{1,17},{9,25},{17,1},{25,9},{2,18},{10... | collective-permute-start | bytes 4915208 | tf_op jit(solution)/shard_map/ppermute | solution.py:16
  799.9 163.5 %collective-permute-start.50 = (bf16[320,2560]{1,0:T(8,128)(2,1)}, bf16[320,2560]{1,0:T(8,128)(2,1)}, u32[]{:S(2)}, u32[]{:S(2)}) collective-permute-start(bf16[320,2560]{1,0:T(8,128)(2,1)} %get-tuple-element.95), channel_id=1, source_target_pairs={{0,24},{8,16},{16,8},{24,0},{1,25},{9,17},{17,9},{25,1},{2,26},{10... | collective-permute-start | bytes 4915208 | tf_op jit(solution)/shard_map/ppermute | solution.py:16
  801.1 258.3 %reduce-scatter.15.cloned.1.call-start = ((), (), s32[]{:S(2)}) async-start(), calls=%async_computation.11 | async-start | bytes 2457600
  962.7 98.9 %collective-permute-start.37 = (f32[256,2560]{1,0:T(8,128)}, f32[256,2560]{1,0:T(8,128)}, u32[]{:S(2)}, u32[]{:S(2)}) collective-permute-start(f32[256,2560]{1,0:T(8,128)} %get-tuple-element.108), channel_id=1, source_target_pairs={{0,1},{1,0},{2,3},{3,2},{4,5},{5,4},{6,7},{7,6},{8,9},{9,8},{10,11... | collective-permute-start | bytes 7864328 | tf_op jit(solution)/shard_map/ppermute | solution.py:20
  (99 other events, 1918.0 us)
Sparse Core Ops, SparseCore 0:
  11.3 43.0 all-gather.4
  79.4 34.9 all-gather.6
  116.6 191.4 all-gather.10
  309.5 92.1 all-gather.8
  403.9 94.8 reduce-scatter.12
  501.6 190.3 reduce-scatter.8
  801.3 45.8 reduce-scatter.10
  969.7 40.6 reduce-scatter.14

commit v3 on v2

--- a/solution.py
+++ b/solution.py
@@ -1,3 +1,5 @@
+import functools
+
 import jax
 import jax.numpy as jnp
 from jax import lax
@@ -26,24 +28,46 @@
     return lax.ppermute(value, "seq", [(at, at + steps) for at in range(leading, last)])
 
 
+def gather_near(value):
+    count = lax.axis_size("seq")
+    steps = (1, 2) if count == 4 else range(1, count)
+    return [exchange(value, step) for step in steps]
+
+
+def gather_far(value, near):
+    if lax.axis_size("seq") != 4:
+        return [value, *near]
+    half = value.shape[0] // 2
+    far = jnp.concatenate([exchange(near[1][:half], 1), exchange(near[0][half:], 2)], axis=0)
+    return [value, *near, far]
+
+
 def plane_gather(value):
-    count = lax.axis_size("seq")
-    if count != 4:
-        return [value] + [exchange(value, step) for step in range(1, count)]
-    half = value.shape[0] // 2
-    near_one, near_two = exchange(value, 1), exchange(value, 2)
-    far = jnp.concatenate([exchange(near_two[:half], 1), exchange(near_one[half:], 2)], axis=0)
-    return [value, near_one, near_two, far]
-
-
-def plane_scatter(own, others, gate=None):
-    total = own.astype(F32)
-    parts = [exchange(part.astype(BF16), step) for step, part in enumerate(others, 1)]
-    if gate is not None:
-        parts = lax.optimization_barrier((*parts, gate))[:-1]
-    for part in parts:
-        total = total + part.astype(F32)
-    return total
+    return gather_far(value, gather_near(value))
+
+
+def scatter_near(parts):
+    if len(parts) != 4:
+        return [exchange(part.astype(BF16), step) for step, part in enumerate(parts[1:], 1)]
+    cut = parts[0].shape[0] // 2
+    by_one = jnp.concatenate([parts[1][:cut], parts[3][:cut]]).astype(BF16)
+    by_two = jnp.concatenate([parts[2][cut:], parts[3][cut:]]).astype(BF16)
+    return [exchange(by_one, 1), exchange(by_two, 2)]
+
+
+def scatter_far(parts, near):
+    if len(parts) != 4:
+        return sum((part.astype(F32) for part in near), parts[0].astype(F32)), []
+    cut = parts[0].shape[0] // 2
+    by_one, by_two = near
+    last_top = (parts[2][:cut].astype(F32) + by_one[cut:].astype(F32)).astype(BF16)
+    last_low = (parts[1][cut:].astype(F32) + by_two[cut:].astype(F32)).astype(BF16)
+    total = parts[0].astype(F32) + jnp.concatenate([by_one[:cut], by_two[:cut]]).astype(F32)
+    return total, [exchange(last_top, 2), exchange(last_low, 1)]
+
+
+def scatter_end(total, far):
+    return total + jnp.concatenate(far).astype(F32) if far else total
 
 
 def times_transpose(left, right):
@@ -159,6 +183,73 @@
         cost_estimate=pl.CostEstimate(flops=1000, bytes_accessed=1000, transcendentals=0),
         name="gather_rows",
     )(own)
+
+
+def unit_kernel(seq_ref, grad_ref, *refs):
+    weights, out_ref = refs[:-1], refs[-1]
+    cols = weights[0].shape[1]
+    for at, weight_ref in enumerate(weights):
+        part = pl.ds(pl.multiple_of((seq_ref[0] ^ at) * cols, 128), cols)
+        term = lax.dot_general(
+            grad_ref[:, part], weight_ref[...], NT, preferred_element_type=F32
+        )
+        if at:
+            out_ref[...] += term
+        else:
+            out_ref[...] = term
+
+
+def unit_grads(seq_at, grads, weights):
+    vmem = pl.BlockSpec(memory_space=pltpu.VMEM)
+    return pl.pallas_call(
+        unit_kernel,
+        out_shape=jax.ShapeDtypeStruct((grads.shape[0], weights[0].shape[0]), F32),
+        in_specs=[pl.BlockSpec(memory_space=pltpu.SMEM), vmem] + [vmem] * len(weights),
+        out_specs=vmem,
+        compiler_params=pltpu.CompilerParams(vmem_limit_bytes=40 * 2**20),
+        cost_estimate=pl.CostEstimate(flops=1000, bytes_accessed=1000, transcendentals=0),
+        name="unit_grads",
+    )(seq_at.reshape(1), grads, *weights)
+
+
+def trade_kernel(to_rows, value_ref, out_ref, sems, local_sems):
+    seq_at, core = lax.axis_index("seq"), lax.axis_index("tensor")
+    plane_ref, chip_ref = (out_ref, value_ref) if to_rows else (value_ref, out_ref)
+    cols, half = plane_ref.shape[1], plane_ref.shape[0] // 8
+    greet([{"seq": seq_at ^ step} for step in range(1, 4)])
+    copies = []
+    for step in (3, 1, 2, 0):
+        for at in range(2):
+            plane = plane_ref.at[pl.ds((at * 4 + step) * half, half), :]
+            rows = pl.ds(pl.multiple_of((core if at == 0 else 1 - core) * half, half), half)
+            owner = seq_at ^ step if to_rows else seq_at
+            chip = chip_ref.at[rows, pl.ds(pl.multiple_of(owner * cols, 128), cols)]
+            source, target = (chip, plane) if to_rows else (plane, chip)
+            if step:
+                sem_at = 2 * (step - 1) + at
+                copies.append(send(source, target, sems, sem_at, {"seq": seq_at ^ step}))
+            else:
+                here = pltpu.make_async_copy(source, target, local_sems.at[at])
+                here.start()
+                copies.append(here)
+    for copy in copies:
+        copy.wait()
+
+
+def trade(value, to_rows, collective_id):
+    rows, cols = value.shape
+    return pl.pallas_call(
+        functools.partial(trade_kernel, to_rows),
+        out_shape=jax.ShapeDtypeStruct(
+            (rows * 4, cols // 4) if to_rows else (rows // 4, cols * 4), value.dtype
+        ),
+        in_specs=[pl.BlockSpec(memory_space=pl.ANY)],
+        out_specs=pl.BlockSpec(memory_space=pl.ANY),
+        scratch_shapes=[pltpu.SemaphoreType.DMA((2, 6)), pltpu.SemaphoreType.DMA((2,))],
+        compiler_params=pltpu.CompilerParams(collective_id=collective_id, has_side_effects=True),
+        cost_estimate=pl.CostEstimate(flops=1000, bytes_accessed=1000, transcendentals=0),
+        name="trade",
+    )(value)
 
 
 def sum_kernel(
@@ -342,7 +433,7 @@
 
 def attend_back_kernel(
     pos_ref, q_ref, g_ref, k_ref, v_ref, log_ref, cos_ref, sin_ref,
-    q_grad_ref, k_grad_ref, v_grad_ref, turned_ref, p_ref, gp_ref,
+    q_grad_ref, keep_ref, sent_ref, turned_ref, p_ref, gp_ref, k_grad_ref, v_grad_ref,
 ):
     tiles = WINDOW // TILE + 1
     size = k_ref.shape[1]
@@ -389,7 +480,17 @@
         q_grad_ref[block, :turn] = rotated.astype(BF16)
         q_grad_ref[block, turn:] = query_grad[:, turn:].astype(BF16)
 
-def attend_back(first_pos, queries, grads, key_rows, value_rows, log_total, cosine, sine):
+    @pl.when(pl.program_id(0) == pl.num_programs(0) - 1)
+    def _():
+        first = pos_ref[1] == 0
+        for start in range(0, k_ref.shape[0], TILE):
+            block = slice(start, start + TILE)
+            k_grad, v_grad = k_grad_ref[block, :], v_grad_ref[block, :]
+            keep_ref[block, :] = jnp.where(first, k_grad, v_grad)
+            sent_ref[block, :] = jnp.where(first, v_grad, k_grad).astype(BF16)
+
+
+def attend_back(first_pos, core, queries, grads, key_rows, value_rows, log_total, cosine, sine):
     rows, cols = queries.shape
     span, size = key_rows.shape
     heads = cols // size
@@ -401,7 +502,7 @@
         out_shape=(
             jax.ShapeDtypeStruct((rows, cols), BF16),
             jax.ShapeDtypeStruct((span, size), F32),
-            jax.ShapeDtypeStruct((span, size), F32),
+            jax.ShapeDtypeStruct((span, size), BF16),
         ),
         grid=(heads,),
         in_specs=[
@@ -415,11 +516,13 @@
             pltpu.VMEM((size, span), BF16),
             pltpu.VMEM(tile_shape, F32),
             pltpu.VMEM(tile_shape, F32),
+            pltpu.VMEM((span, size), F32),
+            pltpu.VMEM((span, size), F32),
         ],
         compiler_params=pltpu.CompilerParams(vmem_limit_bytes=48 * 2**20),
         cost_estimate=pl.CostEstimate(flops=1000, bytes_accessed=1000, transcendentals=0),
         name="attend_back",
-    )(first_pos.reshape(1), queries, grads, key_rows, value_rows, log_total, cosine, sine)
+    )(jnp.stack([first_pos, core]), queries, grads, key_rows, value_rows, log_total, cosine, sine)
 
 def gelu_parts(gate):
     root = 0.7978845608028654
@@ -505,6 +608,51 @@
     )(cot, down, a, b, w)
 
 
+def join_kernel(seq_ref, *refs):
+    pieces, (gate_w_ref, up_w_ref, gate_ref, up_ref, gain_ref) = refs[:4], refs[4:]
+    hidden = pieces[0].shape[1] // 2
+    main, rest = hidden // 128 * 128, hidden % 128
+    for seq_at in range(4):
+
+        @pl.when(seq_ref[0] == seq_at)
+        def _():
+            gain = jnp.zeros((gate_ref.shape[0], 1), F32)
+            for out_ref, w_ref, spans in (
+                (gate_ref, gate_w_ref, ((0, main), (2 * main, rest))),
+                (up_ref, up_w_ref, ((main, main), (2 * main + rest, rest))),
+            ):
+                grad = jnp.concatenate(
+                    [
+                        pieces[at ^ seq_at][:, start : start + count].astype(F32)
+                        for at in range(4)
+                        for start, count in spans
+                    ],
+                    axis=1,
+                )
+                out_ref[...] = grad
+                gain += jnp.sum(grad * w_ref[...].astype(F32), axis=1, keepdims=True)
+            gain_ref[...] = gain
+
+
+def join_columns(seq_at, pieces, w_gate, w_up):
+    rows, cols = w_gate.shape
+    tile = 64
+    by_rows = lambda width: pl.BlockSpec((tile, width), lambda i: (i, 0))
+    whole = jax.ShapeDtypeStruct((rows, cols), F32)
+    gate, up, gain = pl.pallas_call(
+        join_kernel,
+        out_shape=(whole, whole, jax.ShapeDtypeStruct((rows, 1), F32)),
+        grid=(rows // tile,),
+        in_specs=[pl.BlockSpec(memory_space=pltpu.SMEM)]
+        + [by_rows(pieces[0].shape[1])] * 4 + [by_rows(cols)] * 2,
+        out_specs=(by_rows(cols), by_rows(cols), by_rows(1)),
+        compiler_params=pltpu.CompilerParams(vmem_limit_bytes=40 * 2**20),
+        cost_estimate=pl.CostEstimate(flops=1000, bytes_accessed=1000, transcendentals=0),
+        name="join_columns",
+    )(seq_at.reshape(1), *pieces, w_gate, w_up)
+    return gate, up, gain[:, 0]
+
+
 def local(
     inputs, cotangent, gain_attn, gain_ffn, w_query, w_key, w_value, w_out, w_gate, w_up, w_down
 ):
@@ -542,11 +690,14 @@
         far = [swap(piece) if at or other is None else other for at, piece in enumerate(near)]
         return jnp.concatenate(near + far, axis=0)
 
-    def plane_sum(partial, gate=None):
+    def core_sum(partial):
         count = seqs * half
         cores = partial[:count].astype(F32) + swap(partial[count:].astype(BF16)).astype(F32)
-        others = [cores[j * half : (j + 1) * half] for j in range(1, seqs)]
-        return plane_scatter(cores[:half], others, gate)
+        return [cores[j * half : (j + 1) * half] for j in range(seqs)]
+
+    def plane_sum(partial):
+        parts = core_sum(partial)
+        return scatter_end(*scatter_far(parts, scatter_near(parts)))
 
     def order_cols(pieces):
         stacked = jnp.stack(pieces)
@@ -567,10 +718,10 @@
     pair_shard = jnp.where(first, w_key, w_value)
     proj_shard = jnp.concatenate([w_query, pair_shard], axis=1)
     proj_cols = proj_shard.shape[1] // seqs
+    out_rows = head_cols // seqs
     proj_weight = lax.all_gather(
         part_of(proj_shard, seq_at, proj_cols, 1), "fsdp", axis=0, tiled=True
     )
-    out_rows = head_cols // seqs
     hidden = w_gate.shape[1] // seqs
     kernels = hidden % 128 == 64
     main = hidden // 128 * 128 if kernels else hidden
@@ -583,18 +734,14 @@
         part_of(w_down, seq_at, hidden, 0), "fsdp", axis=1, tiled=True
     )
 
-    source = inputs.astype(F32)
+    source = my_half(inputs).astype(F32)
     inverse_one = inverse_rms(source)
     unit_one = (source * inverse_one * gains[0]).astype(BF16)
     square = seqs == 4
-    unit_one_half = my_half(unit_one)
-    rows_one = (
-        gather_rows(unit_one_half, 1) if square
-        else plane_rows(unit_one_half, other_half(unit_one))
-    )
     out_quarter = lax.all_gather(
-        part_of(after(w_out, rows_one), seq_at, out_rows, 0), "fsdp", axis=1, tiled=True
-    )
+        part_of(w_out, seq_at, out_rows, 0), "fsdp", axis=1, tiled=True
+    )
+    rows_one = gather_rows(unit_one, 1) if square else plane_rows(unit_one)
     proj = jnp.dot(rows_one, proj_weight, preferred_element_type=F32)
     rotate_first = proj_cols % (2 * rot_half) == 0
     if rotate_first:
@@ -613,12 +760,16 @@
         row_cos = jnp.where(turned, jnp.cos(row_angles)[:, None], 1.0) * unit_scale
         row_sin = jnp.where(turned, jnp.sin(row_angles)[:, None], 0.0) * unit_scale
         proj = rotate(proj.reshape(-1, units, 2 * rot_half), row_cos, row_sin)
-    proj = proj.astype(BF16).reshape(2, seqs, half, proj_cols)
-    proj = jnp.where(first, proj, proj[::-1])
-    proj_parts = [proj[:, 0].reshape(rows, proj_cols)] + [
-        exchange(proj[:, at].reshape(rows, proj_cols), at) for at in range(1, seqs)
-    ]
-    proj_here = jnp.concatenate(order_cols(proj_parts), axis=1)
+    proj = proj.astype(BF16).reshape(2 * seqs * half, proj_cols)
+    if square and rotate_first:
+        proj_here = trade(proj, False, 5)
+    else:
+        proj = proj.reshape(2, seqs, half, proj_cols)
+        proj = jnp.where(first, proj, proj[::-1])
+        proj_parts = [proj[:, 0].reshape(rows, proj_cols)] + [
+            exchange(proj[:, at].reshape(rows, proj_cols), at) for at in range(1, seqs)
+        ]
+        proj_here = jnp.concatenate(order_cols(proj_parts), axis=1)
     queries = proj_here[:, :head_cols]
     pair_here = proj_here[:, head_cols:]
     if not rotate_first:
@@ -628,7 +779,6 @@
         pair_here = jnp.where(first, rotate(pair_here.astype(F32), cosine, sine), pair_here)
         pair_here = pair_here.astype(BF16)
 
-    pair_here, out_quarter = lax.optimization_barrier((pair_here, out_quarter))
     earlier = seq_shift(pair_here, 1)
     slots = [
         lax.ppermute(
@@ -638,12 +788,13 @@
         for at in range(1, shards)
     ]
     window_here = jnp.concatenate([earlier] + slots + [pair_here], axis=0)
+    window_here, *out_pieces = lax.optimization_barrier((window_here, *plane_gather(out_quarter)))
     window_other = swap(window_here)
     key_rows = jnp.where(first, window_here, window_other)
     value_rows = jnp.where(first, window_other, window_here)
 
     out_weight = jnp.zeros((head_cols, width), BF16)
-    for at, piece in enumerate(plane_gather(out_quarter)):
+    for at, piece in enumerate(out_pieces):
         out_weight = lax.dynamic_update_slice_in_dim(
             out_weight, piece, (seq_at ^ at) * out_rows, 0
         )
@@ -651,7 +802,7 @@
     head_outputs, log_total = attend(first_pos, queries, key_rows, value_rows)
 
     out_part = jnp.dot(head_outputs, out_weight, preferred_element_type=F32)
-    hidden_in = my_half(source) + my_half(out_part) + swap(other_half(out_part))
+    hidden_in = source + my_half(out_part) + swap(other_half(out_part))
     inverse_two = inverse_rms(hidden_in)
     unit_two = (hidden_in * inverse_two * gains[1]).astype(BF16)
     rows_two = gather_rows(unit_two, 2) if square else plane_rows(unit_two)
@@ -661,7 +812,9 @@
     if kernels:
         activation, gate_factor, up_factor = ffn(rows_two, in_weight)
         down_term = rows_product(rows_cot, activation).astype(BF16)
-        gate_factor = after(gate_factor, down_term)
+        gate_factor, proj_later, _ = lax.optimization_barrier(
+            (gate_factor, proj_weight, down_term)
+        )
         grad_in, back_part = ffn_back(rows_cot, down_weight, gate_factor, up_factor, in_weight)
     else:
         in_proj = jnp.dot(rows_two, in_weight, preferred_element_type=F32)
@@ -672,91 +825,117 @@
         grad_gate, grad_up = jax.vjp(gated_unit, gate_pre, up_proj)[1](grad_activation)
         grad_in = jnp.concatenate([grad_gate.astype(BF16), grad_up.astype(BF16)], axis=1)
         back_part = times_transpose(grad_in, in_weight)
+        proj_later = after(proj_weight, down_term)
+    grad_in, proj_near = lax.optimization_barrier((grad_in, gather_near(proj_later)))
+    proj_pieces = gather_far(proj_later, proj_near)
     in_term = rows_product(rows_two, grad_in).astype(BF16)
-    back_part = after(back_part, in_term)
+    back_part, proj_pieces, in_term = lax.optimization_barrier((back_part, proj_pieces, in_term))
     grad_unit_two = scatter_rows(back_part, 3) if square else plane_sum(back_part)
     grad_hidden = my_half(cotangent).astype(F32) + norm_pull(
         hidden_in, inverse_two, grad_unit_two * gains[1]
     )
-    out_rows_part = jnp.dot(
-        after(activation, grad_unit_two), down_weight, preferred_element_type=F32
-    )
     down_shard = lax.psum_scatter(down_term, "fsdp", scatter_dimension=0, tiled=True).T
     in_shard = lax.psum_scatter(in_term, "fsdp", scatter_dimension=0, tiled=True)
 
     grad_attn_out = whole_rows(grad_hidden.astype(BF16))
     grad_heads = times_transpose(grad_attn_out, out_weight).astype(BF16)
-    grad_heads, out_rows_part, down_shard = lax.optimization_barrier(
-        (grad_heads, out_rows_part, down_shard)
-    )
-    grad_query_proj, grad_keys, grad_values = attend_back(
-        first_pos, queries, grad_heads, key_rows, value_rows, log_total,
+    ffn_part = jnp.dot(
+        after(activation, grad_unit_two), down_weight, preferred_element_type=F32
+    ).astype(BF16)
+    out_term = rows_product(head_outputs, grad_attn_out).astype(BF16)
+    down_near = gather_near(down_shard)
+    grad_heads, down_near, ffn_part, out_term = lax.optimization_barrier(
+        (grad_heads, down_near, ffn_part, out_term)
+    )
+    out_parts = [part_of(out_term, seq_at ^ at, out_rows, 0) for at in range(seqs)]
+    out_near = scatter_near(out_parts)
+    grad_query_proj, pair_keep, pair_sent = attend_back(
+        first_pos, core, queries, grad_heads, key_rows, value_rows, log_total,
         jnp.concatenate([cosine, cosine], axis=1), jnp.concatenate([sine, -sine], axis=1),
     )
-    pair_grads = jnp.where(first, grad_keys, grad_values) + swap(
-        jnp.where(first, grad_values, grad_keys)
-    )
+    pair_grads = pair_keep + swap(pair_sent).astype(F32)
+    pair_grads, down_near = lax.optimization_barrier((pair_grads, down_near))
     returned = [
         lax.ppermute(
             pair_grads[at * rows : (at + 1) * rows].astype(BF16),
             "fsdp", [((source_at - at) % shards, source_at) for source_at in range(shards)],
-        ).astype(F32)
+        )
         for at in range(1, shards)
     ]
+    ffn_cores = core_sum(ffn_part)
+    returned, out_near, ffn_cores = lax.optimization_barrier((returned, out_near, ffn_cores))
+    out_sum, out_far = scatter_far(out_parts, out_near)
     own_total = pair_grads[shards * rows :]
     earlier_total = pair_grads[:rows]
     for at, piece in enumerate(returned, 1):
-        own_total = own_total + jnp.where(shard_at >= at, 0.0, piece)
-        earlier_total = earlier_total + jnp.where(shard_at >= at, piece, 0.0)
+        own_total = own_total + jnp.where(shard_at >= at, 0.0, piece.astype(F32))
+        earlier_total = earlier_total + jnp.where(shard_at >= at, piece.astype(F32), 0.0)
     own_total = own_total + seq_shift(earlier_total.astype(BF16), -1).astype(F32)
     grad_pair = jnp.where(first, rotate(own_total, cosine, -sine), own_total).astype(BF16)
-    grad_pair, in_shard = lax.optimization_barrier((grad_pair, in_shard))
+    ffn_near = scatter_near(ffn_cores)
+    grad_pair, in_shard, out_far, ffn_near, down_parts = lax.optimization_barrier(
+        (grad_pair, in_shard, out_far, ffn_near, gather_far(down_shard, down_near))
+    )
+    out_sum = scatter_end(out_sum, out_far)
     grad_proj = jnp.concatenate([grad_query_proj, grad_pair], axis=1)
-    grad_parts = [part_of(grad_proj, seq_at, proj_cols, 1)] + [
-        exchange(part_of(grad_proj, seq_at ^ at, proj_cols, 1), at) for at in range(1, seqs)
-    ]
-    grad_rows = jnp.stack(grad_parts).reshape(seqs, 2, half, proj_cols).swapaxes(0, 1)
-    grad_rows = jnp.where(first, grad_rows, grad_rows[::-1]).reshape(2 * seqs * half, proj_cols)
-
-    ffn_out = plane_sum(after(out_rows_part, pair_grads), grad_pair)
+    if square:
+        grad_rows = trade(grad_proj, True, 6)
+    else:
+        grad_parts = [part_of(grad_proj, seq_at, proj_cols, 1)] + [
+            exchange(part_of(grad_proj, seq_at ^ at, proj_cols, 1), at) for at in range(1, seqs)
+        ]
+        grad_rows = jnp.stack(grad_parts).reshape(seqs, 2, half, proj_cols).swapaxes(0, 1)
+        grad_rows = jnp.where(first, grad_rows, grad_rows[::-1])
+        grad_rows = grad_rows.reshape(2 * seqs * half, proj_cols)
+    proj_term = rows_product(rows_one, grad_rows).astype(BF16)
+
+    out_shard = lax.psum_scatter(out_sum.astype(BF16), "fsdp", scatter_dimension=1, tiled=True)
+    proj_sum = lax.psum_scatter(proj_term, "fsdp", scatter_dimension=0, tiled=True)
+    in_parts = plane_gather(after(in_shard, grad_rows))
+    grad_proj = after(grad_proj, proj_term)
+    if square:
+        unit_part = unit_grads(seq_at, grad_proj, proj_pieces)
+    else:
+        unit_part = sum(
+            times_transpose(part_of(grad_proj, seq_at ^ at, proj_cols, 1), proj_pieces[at])
+            for at in range(seqs)
+        )
+    grad_unit_one = my_half(unit_part) + swap(other_half(unit_part))
+    grad_unit_one, proj_sum = lax.optimization_barrier((grad_unit_one, proj_sum))
+    ffn_sum, ffn_far = scatter_far(ffn_cores, after(ffn_near, proj_term))
+    ffn_out = scatter_end(ffn_sum, after(ffn_far, grad_unit_one))
     layer_out = whole_rows((hidden_in + ffn_out).astype(BF16))
-    down_parts = lax.optimization_barrier((*plane_gather(down_shard), pair_grads))[:-1]
+    down_parts = lax.optimization_barrier((*down_parts, grad_unit_one))[:-1]
     down_grad = jnp.concatenate(order_cols(down_parts), axis=0).astype(F32)
-    in_parts = order_cols(plane_gather(in_shard))
-    rest = hidden - main
-    gate_grad, up_grad = (
-        jnp.concatenate(
-            [
-                piece[:, first_at : first_at + count]
-                for piece in in_parts
-                for first_at, count in spans
-                if count
-            ],
-            axis=1,
-        ).astype(F32)
-        for spans in (((0, main), (2 * main, rest)), ((main, main), (2 * main + rest, rest)))
-    )
-    gain_two_half = jnp.sum(
-        gate_grad * w_gate.astype(F32) + up_grad * w_up.astype(F32), axis=1
-    ) / gain_two[:, 0]
-    out_term = rows_product(after(head_outputs, grad_rows), grad_attn_out).astype(BF16)
-    out_sum = plane_scatter(
-        part_of(out_term, seq_at, out_rows, 0),
-        [part_of(out_term, seq_at ^ at, out_rows, 0) for at in range(1, seqs)],
-    ).astype(BF16)
-    out_shard = lax.psum_scatter(out_sum, "fsdp", scatter_dimension=1, tiled=True)
+    grad_input = whole_rows(
+        grad_hidden + norm_pull(source, inverse_one, grad_unit_one * gains[0])
+    )
+    if kernels and square:
+        in_parts, down_grad, grad_input, layer_out = lax.optimization_barrier(
+            (in_parts, down_grad, grad_input, layer_out)
+        )
+        gate_grad, up_grad, gain_two_half = join_columns(seq_at, in_parts, w_gate, w_up)
+    else:
+        in_parts = order_cols(in_parts)
+        rest = hidden - main
+        gate_grad, up_grad = (
+            jnp.concatenate(
+                [
+                    piece[:, first_at : first_at + count]
+                    for piece in in_parts
+                    for first_at, count in spans
+                    if count
+                ],
+                axis=1,
+            ).astype(F32)
+            for spans in (((0, main), (2 * main, rest)), ((main, main), (2 * main + rest, rest)))
+        )
+        gain_two_half = jnp.sum(
+            gate_grad * w_gate.astype(F32) + up_grad * w_up.astype(F32), axis=1
+        )
+    gain_two_half = gain_two_half / gain_two[:, 0]
     out_grad = jnp.concatenate(order_cols(plane_gather(out_shard)), axis=0).astype(F32)
 
-    proj_term = rows_product(rows_one, grad_rows).astype(BF16)
-    grad_unit_one = times_transpose(grad_rows, proj_weight)
-    if square:
-        grad_unit_one = scatter_rows(after(grad_unit_one.astype(BF16), proj_term), 4)
-    else:
-        grad_unit_one = plane_sum(grad_unit_one)
-    grad_input = whole_rows(
-        grad_hidden + norm_pull(my_half(source), my_half(inverse_one), grad_unit_one * gains[0])
-    )
-    proj_sum = lax.psum_scatter(proj_term, "fsdp", scatter_dimension=0, tiled=True)
     proj_grad = jnp.concatenate(order_cols(plane_gather(proj_sum)), axis=1).astype(F32)
     gain_one_half = jnp.sum(proj_grad * proj_shard.astype(F32), axis=1) / gain_one[:, 0]
     query_grad = proj_grad[:, :head_cols]

time: 1100 us -> 972 us (0.88)
  local copies, waits for them, and re-layouts: 163 us -> 120 us
  other arithmetic: 128 us -> 94.4 us
  Pallas kernels: 388 us -> 359 us
  starting transfers between devices: 98.2 us -> 71.9 us
  waiting for transfers between devices: 194 us -> 208 us
    pallas_call x2 -> x1, Pallas kernels: 168 us -> 50.3 us  [scatter_rows(): pl.pallas_call(sum_kernel, out_shape=jax.ShapeDtypeStruct((half, width),...]
    pallas_call x0 -> x4, Pallas kernels: none -> 87.8 us  [the longest x2 61.4 us: trade(): pl.pallas_call(functools.partial(trade_kernel, to_rows), out_shape=jax.Sh...]
    ppermute x36, starting transfers between devices: 59.3 us -> 31.4 us  [exchange(): return lax.ppermute(value, 'seq', [(at, at ^ step) for at in range(count)])]
    reduce_sum x1 -> x0, other arithmetic: 17.6 us -> none  [local(): jnp.sum(gate_grad * w_gate.astype(F32) + up_grad * w_up.astype(F32), axis=1)]
    concatenate x2 -> x0, local copies, waits for them, and re-layouts: 17.2 us -> none  [local(): jnp.concatenate([piece[:, first_at:first_at + count] for piece in in_part...]
    ppermute x2, waiting for transfers between devices: 3.65 us -> 19.9 us  [seq_shift(): lax.ppermute(value, 'seq', [(at, at + steps) for at in range(leading, las...]
    another operation x3, other arithmetic: 16.5 us -> 0.87 us
    reduce_scatter x1, waiting for transfers between devices: 11.9 us -> 0.01 us  [local(): lax.psum_scatter(in_term, 'fsdp', scatter_dimension=0, tiled=True)]
  transfers between devices with their start and end apart: 67 -> 68, of which waited for: 22 -> 20; matrix products, arithmetic and copies ran while one was open for 34% -> 29% of each run, Pallas kernels for 36% -> 37%
where the time goes in v3:
time: 972 us; the launch traced here: 962 us
  Pallas kernels  359 us (37%)
  waiting for transfers between devices  208 us (21%)
  local copies, waits for them, and re-layouts  120 us (12%)
  other arithmetic  94.4 us (10%)
  matrix products  93.6 us (10%)
  starting transfers between devices  71.9 us (7%)
  between operations  15.6 us (2%)
    ppermute x36, waiting for transfers between devices, exchange(): return lax.ppermute(value, 'seq', [(at, at ^ step) for at in range(count)])  109 us
    pallas_call x2, Pallas kernels, gather_rows(): pl.pallas_call(rows_kernel, out_shape=jax.ShapeDtypeStruct((8 * half, wid...  102 us
    dot_general x4, matrix products, rows_product(): lax.dot_general(left, right, (((0,), (0,)), ((), ())), preferred_element_...  62.5 us
    pallas_call x2, Pallas kernels, trade(): pl.pallas_call(functools.partial(trade_kernel, to_rows), out_shape=jax.Sh...  61.4 us
    unnamed x145, local copies, waits for them, and re-layouts  53.5 us
    pallas_call x1, Pallas kernels, scatter_rows(): pl.pallas_call(sum_kernel, out_shape=jax.ShapeDtypeStruct((half, width),...  50.3 us
    pallas_call x1, Pallas kernels, ffn_back(): pl.pallas_call(ffn_back_kernel, out_shape=(jax.ShapeDtypeStruct((count, 2...  43.2 us
    ppermute x3, waiting for transfers between devices, local(): lax.ppermute(pair_grads[at * rows:(at + 1) * rows].astype(BF16), 'fsdp',...  36.1 us
  transfers between devices with their start and end apart: 68, of which 20 were waited for; matrix products, arithmetic and copies ran while one was open for 29% of the time, Pallas kernels for 37%

profile of v3, /device:TPU:9, one launch (start us, length us, event | category | flops | bytes accessed | tf_op | source)
XLA Modules:
  0.0 962.3 jit_solution(15140577018219619731)
XLA Ops:
  32.7 51.9 %gather_rows.2 = bf16[2048,2560]{1,0:T(8,128)(2,1)} custom-call(bf16[256,2560]{1,0:T(8,128)(2,1)} %fusion.3.own_ref), custom_call_target="tpu_custom_call" | custom-call | flops 1000 | bytes 1000 | tf_op jit(solution)/shard_map/gather_rows/pallas_call | solution.py:176
  105.2 34.2 %trade.2 = bf16[512,1536]{1,0:T(8,128)(2,1)} custom-call(bf16[2048,384]{1,0:T(8,128)(2,1)} %copy.25.value_ref), custom_call_target="tpu_custom_call" | custom-call | flops 1000 | bytes 1000 | tf_op jit(solution)/shard_map/trade/pallas_call | solution.py:241
  169.3 15.3 %collective-permute-done.5 = bf16[512,256]{1,0:T(8,128)(2,1)} collective-permute-done((bf16[512,256]{1,0:T(8,128)(2,1)}, bf16[512,256]{1,0:T(8,128)(2,1)}, u32[]{:S(2)}, u32[]{:S(2)}) %collective-permute-start.5) | collective-permute-done | bytes 262176 | tf_op jit(solution)/shard_map/ppermute | solution.py:784
  185.5 16.8 %collective-permute-done.6 = bf16[512,256]{1,0:T(8,128)(2,1)} collective-permute-done((bf16[512,256]{1,0:T(8,128)(2,1)}, bf16[512,256]{1,0:T(8,128)(2,1)}, u32[]{:S(2)}, u32[]{:S(2)}) %collective-permute-start.6) | collective-permute-done | bytes 262176 | tf_op jit(solution)/shard_map/ppermute | solution.py:784
  222.9 15.4 %attend.1 = (bf16[512,1280]{1,0:T(8,128)(2,1)S(1)}, f32[5,1,512]{2,1,0:T(1,128)S(1)}) custom-call(s32[1]{0:T(128)} %bitcast.pos_ref, bf16[512,1280]{1,0:T(8,128)(2,1)S(1)} %slice.198.q_ref, bf16[2560,256]{1,0:T(8,128)(2,1)S(1)} %get-tuple-element.193.k_ref, bf16[2560,256]{1,0:T(8,128)(2,1)S(1)} %get-tuple-element.192.v_ref), custom_call_target="tpu_custom_call" | custom-call | flops 1000 | bytes 1000 | tf_op jit(solution)/shard_map/attend/pallas_call | solution.py:408
  280.8 50.1 %gather_rows.3.x_ref = bf16[2048,2560]{1,0:T(8,128)(2,1)} custom-call(bf16[256,2560]{1,0:T(8,128)(2,1)} %multiply_convert_fusion.own_ref), custom_call_target="tpu_custom_call" | custom-call | flops 1000 | bytes 1000 | tf_op jit(solution)/shard_map/gather_rows/pallas_call | solution.py:176
  330.9 32.8 %ffn.1 = (bf16[2048,960]{1,0:T(8,128)(2,1)}, bf16[2048,960]{1,0:T(8,128)(2,1)}, bf16[2048,960]{1,0:T(8,128)(2,1)}) custom-call(bf16[2048,2560]{1,0:T(8,128)(2,1)} %gather_rows.3.x_ref, bf16[2560,1920]{1,0:T(8,128)(2,1)} %all-gather.11.cloned.1.call-done.w_ref), custom_call_target="tpu_custom_call" | custom-call | flops 1000 | bytes 1000 | tf_op jit(solution)/shard_map/ffn/pallas_call | solution.py:562
  363.8 15.9 %convolution_convert_fusion.3 = bf16[2560,960]{0,1:T(8,128)(2,1)} fusion(bf16[2048,2560]{1,0:T(8,128)(2,1)} %constant_dynamic-update-slice_fusion.5.c_ref, bf16[2048,960]{1,0:T(8,128)(2,1)} %get-tuple-element.106), kind=kOutput, calls=%fused_computation.4 | convolution fusion | flops 10068787200 | bytes 19333120 | tf_op jit(solution)/shard_map/dot_general | solution.py:78
  389.1 43.2 %ffn_back.1 = (bf16[2048,1920]{1,0:T(8,128)(2,1)}, bf16[2048,2560]{1,0:T(8,128)(2,1)}) custom-call(bf16[2048,2560]{1,0:T(8,128)(2,1)} %constant_dynamic-update-slice_fusion.5.c_ref, bf16[960,2560]{1,0:T(8,128)(2,1)} %all-gather.9.cloned.1.call-done.d_ref, bf16[2048,960]{1,0:T(8,128)(2,1)} %get-tuple-element.97.a_ref, ...), custom_call_target="tpu_custom_call" | custom-call | flops 1000 | bytes 1000 | tf_op jit(solution)/shard_map/ffn_back/pallas_call | solution.py:596
  437.8 28.0 %convolution_convert_fusion = bf16[2560,1920]{1,0:T(8,128)(2,1)} fusion(bf16[2048,2560]{1,0:T(8,128)(2,1)} %gather_rows.3.x_ref, bf16[2048,1920]{1,0:T(8,128)(2,1)} %get-tuple-element.104), kind=kOutput, calls=%fused_computation | convolution fusion | flops 20137574400 | bytes 28180480 | tf_op jit(solution)/shard_map/dot_general | solution.py:78
  472.9 50.3 %scatter_rows.1 = f32[256,2560]{1,0:T(8,128)S(1)} custom-call(bf16[2048,2560]{1,0:T(8,128)(2,1)S(1)} %copy-done.6), custom_call_target="tpu_custom_call" | custom-call | flops 1000 | bytes 1000 | tf_op jit(solution)/shard_map/scatter_rows/pallas_call | solution.py:332
  528.0 13.3 %convolution_convert_fusion.2 = bf16[2048,2560]{1,0:T(8,128)(2,1)} fusion(bf16[2048,960]{1,0:T(8,128)(2,1)S(1)} %copy-done.58, bf16[960,2560]{1,0:T(8,128)(2,1)S(1)} %bitcast.101), kind=kOutput, calls=%fused_computation.2 | convolution fusion | flops 10071572480 | bytes 19333120 | tf_op jit(solution)/shard_map/dot_general | solution.py:842
  562.1 12.3 %collective-permute-done.25 = bf16[960,640]{1,0:T(8,128)(2,1)} collective-permute-done((bf16[960,640]{1,0:T(8,128)(2,1)}, bf16[960,640]{1,0:T(8,128)(2,1)}, u32[]{:S(2)}, u32[]{:S(2)}) %collective-permute-start.25) | collective-permute-done | bytes 1228832 | tf_op jit(solution)/shard_map/ppermute | solution.py:18
  580.0 26.9 %attend_back.1 = (bf16[512,1280]{1,0:T(8,128)(2,1)S(1)}, f32[2560,256]{1,0:T(8,128)}, bf16[2560,256]{1,0:T(8,128)(2,1)}) custom-call(s32[2]{0:T(128)S(1)} %pad_add_fusion.pos_ref, bf16[512,1280]{1,0:T(8,128)(2,1)S(1)} %copy-done.3, bf16[512,1280]{1,0:T(8,128)(2,1)S(1)} %convolution_convert_fusion.5.g_ref, bf16[2560,256]{1,0:T(8,128)(2,1)} %copy-done.5, ...), custom_call_target="tpu_custom_call" | custom-call | flops 1000 | bytes 1000 | tf_op jit(solution)/shard_map/attend_back/pallas_call | solution.py:500
  642.7 27.4 %collective-permute-done.29 = bf16[512,256]{1,0:T(8,128)(2,1)S(1)} collective-permute-done((bf16[512,256]{1,0:T(8,128)(2,1)}, bf16[512,256]{1,0:T(8,128)(2,1)S(1)}, u32[]{:S(2)}, u32[]{:S(2)}) %collective-permute-start.29) | collective-permute-done | bytes 262176 | tf_op jit(solution)/shard_map/ppermute | solution.py:859
  690.5 15.6 %collective-permute-done.34 = bf16[512,256]{1,0:T(8,128)(2,1)S(1)} collective-permute-done((bf16[512,256]{1,0:T(8,128)(2,1)S(1)}, bf16[512,256]{1,0:T(8,128)(2,1)S(1)}, u32[]{:S(2)}, u32[]{:S(2)}) %collective-permute-start.34) | collective-permute-done | bytes 262176 | tf_op jit(solution)/shard_map/ppermute | solution.py:28
  709.5 20.1 %collective-permute-done.35 = bf16[160,2560]{1,0:T(8,128)(2,1)S(1)} collective-permute-done((bf16[160,2560]{1,0:T(8,128)(2,1)S(1)}, bf16[160,2560]{1,0:T(8,128)(2,1)S(1)}, u32[]{:S(2)}, u32[]{:S(2)}) %collective-permute-start.35) | collective-permute-done | bytes 819232 | tf_op jit(solution)/shard_map/ppermute | solution.py:18
  741.8 27.2 %trade.3 = bf16[2048,384]{1,0:T(8,128)(2,1)} custom-call(bf16[512,1536]{1,0:T(8,128)(2,1)} %constant_dynamic-update-slice_fusion.13.value_ref.grad_ref), custom_call_target="tpu_custom_call" | custom-call | flops 1000 | bytes 1000 | tf_op jit(solution)/shard_map/trade/pallas_call | solution.py:241
  769.2 10.0 %convolution_convert_fusion.4 = bf16[2560,384]{1,0:T(8,128)(2,1)} fusion(bf16[2048,2560]{1,0:T(8,128)(2,1)} %gather_rows.2, bf16[2048,384]{1,0:T(8,128)(2,1)} %trade.3), kind=kOutput, calls=%fused_computation.8 | convolution fusion | flops 4027514880 | bytes 14024704 | tf_op jit(solution)/shard_map/dot_general | solution.py:78
  783.8 10.2 %unit_grads.1 = f32[512,2560]{1,0:T(8,128)} custom-call(s32[1]{0:T(128)} %bitcast.16.seq_ref, bf16[512,1536]{1,0:T(8,128)(2,1)} %constant_dynamic-update-slice_fusion.13.value_ref.grad_ref, bf16[2560,384]{1,0:T(8,128)(2,1)S(1)} %copy-done.12, bf16[2560,384]{1,0:T(8,128)(2,1)S(1)} %copy-done.10, bf16[2560,384]{1,0:T(8,128)(2,1)} %collective-permute-done.21.refs_2_, ...), custom_call_target="tpu_custom_call" | custom-call | flops 1000 | bytes 1000 | tf_op jit(solution)/shard_map/unit_grads/pallas_call | solution.py:204
  805.7 18.1 %collective-permute-done.42.refs_2_ = bf16[640,1920]{1,0:T(8,128)(2,1)} collective-permute-done((bf16[640,1920]{1,0:T(8,128)(2,1)}, bf16[640,1920]{1,0:T(8,128)(2,1)}, u32[]{:S(2)}, u32[]{:S(2)}) %collective-permute-start.42) | collective-permute-done | bytes 2457632 | tf_op jit(solution)/shard_map/ppermute | solution.py:18
  840.0 24.9 %collective-permute-done.57 = bf16[320,640]{1,0:T(8,128)(2,1)S(1)} collective-permute-done((bf16[320,640]{1,0:T(8,128)(2,1)}, bf16[320,640]{1,0:T(8,128)(2,1)S(1)}, u32[]{:S(2)}, u32[]{:S(2)}) %collective-permute-start.57) | collective-permute-done | bytes 409632 | tf_op jit(solution)/shard_map/ppermute | solution.py:18
  906.8 12.2 %maximum_convert_fusion = f32[3840,640]{1,0:T(8,128)} fusion(bf16[960,640]{1,0:T(8,128)(2,1)S(1)} %get-tuple-element.183, bf16[960,640]{1,0:T(8,128)(2,1)S(1)} %get-tuple-element.184, bf16[960,640]{1,0:T(8,128)(2,1)S(1)} %get-tuple-element.185, bf16[960,640]{1,0:T(8,128)(2,1)S(1)} %get-tuple-element.182), kind=kLoop, calls=%fused_computation.7 | loop fusion | flops 19660800 | bytes 14745600 | tf_op jit(solution)/shard_map/convert_element_type | solution.py:909
  935.1 16.3 %join_columns.1 = (f32[640,3840]{1,0:T(8,128)}, f32[640,3840]{1,0:T(8,128)}, f32[640,1]{1,0:T(8,128)S(1)}) custom-call(s32[1]{0:T(128)} %bitcast.16.seq_ref, bf16[640,1920]{1,0:T(8,128)(2,1)S(1)} %copy-done.11, bf16[640,1920]{1,0:T(8,128)(2,1)} %collective-permute-done.41.refs_1_, bf16[640,1920]{1,0:T(8,128)(2,1)} %collective-permute-done.42.refs_2_, ...), custom_call_target="tpu_custom_call" | custom-call | flops 1000 | bytes 1000 | tf_op jit(solution)/shard_map/join_columns/pallas_call | solution.py:642
  (416 shorter events, 358.4 us)
Async XLA Ops:
  7.2 77.5 %all-gather.7.cloned.1.call-start = ((), (), s32[]{:S(2)}) async-start(), calls=%async_computation.5 | async-start | bytes 2048000 | tf_op jit(solution)/shard_map/all_gather | solution.py:741
  9.4 83.4 %all-gather.5.cloned.1.call-start = ((), (), s32[]{:S(2)}) async-start(), calls=%async_computation.4 | async-start | bytes 2457600 | tf_op jit(solution)/shard_map/all_gather | solution.py:722
  12.2 318.7 %all-gather.11.cloned.1.call-start = ((), (), s32[]{:S(2)}) async-start(), calls=%async_computation.7 | async-start | bytes 12288000 | tf_op jit(solution)/shard_map/all_gather | solution.py:732
  22.9 366.2 %all-gather.9.cloned.1.call-start = ((), (), s32[]{:S(2)}) async-start(), calls=%async_computation.6 | async-start | bytes 6144000 | tf_op jit(solution)/shard_map/all_gather | solution.py:733
  84.7 65.4 %collective-permute-start.7 = (bf16[320,2560]{1,0:T(8,128)(2,1)}, bf16[320,2560]{1,0:T(8,128)(2,1)}, u32[]{:S(2)}, u32[]{:S(2)}) collective-permute-start(bf16[320,2560]{1,0:T(8,128)(2,1)} %all-gather.7.cloned.1.call-done), channel_id=1, source_target_pairs={{0,8},{8,0},{16,24},{24,16},{1,9},{9,1},{17,25},{25,17},{2,10},{10... | collective-permute-start | bytes 4915208 | tf_op jit(solution)/shard_map/ppermute | solution.py:18
  84.8 70.5 %collective-permute-start.8 = (bf16[320,2560]{1,0:T(8,128)(2,1)}, bf16[320,2560]{1,0:T(8,128)(2,1)}, u32[]{:S(2)}, u32[]{:S(2)}) collective-permute-start(bf16[320,2560]{1,0:T(8,128)(2,1)} %all-gather.7.cloned.1.call-done), channel_id=1, source_target_pairs={{0,16},{8,24},{16,0},{24,8},{1,17},{9,25},{17,1},{25,9},{2,18},{10... | collective-permute-start | bytes 4915208 | tf_op jit(solution)/shard_map/ppermute | solution.py:18
  152.2 52.1 %collective-permute-start.10 = (bf16[160,2560]{1,0:T(8,128)(2,1)}, bf16[160,2560]{1,0:T(8,128)(2,1)S(1)}, u32[]{:S(2)}, u32[]{:S(2)}) collective-permute-start(bf16[160,2560]{1,0:T(8,128)(2,1)} %slice.261), channel_id=1, source_target_pairs={{0,16},{8,24},{16,0},{24,8},{1,17},{9,25},{17,1},{25,9},{2,18},{10... | collective-permute-start | bytes 2457608 | tf_op jit(solution)/shard_map/ppermute | solution.py:18
  157.4 46.8 %collective-permute-start.9 = (bf16[160,2560]{1,0:T(8,128)(2,1)}, bf16[160,2560]{1,0:T(8,128)(2,1)}, u32[]{:S(2)}, u32[]{:S(2)}) collective-permute-start(bf16[160,2560]{1,0:T(8,128)(2,1)} %slice.260), channel_id=1, source_target_pairs={{0,8},{8,0},{16,24},{24,16},{1,9},{9,1},{17,25},{25,17},{2,10},{10... | collective-permute-start | bytes 2457608 | tf_op jit(solution)/shard_map/ppermute | solution.py:18
  162.5 380.4 %reduce-scatter.13.cloned.1.call-start = ((), (), s32[]{:S(2)}) async-start(), calls=%async_computation.10 | async-start | bytes 6553600
  387.5 343.2 %reduce-scatter.9.cloned.1.call-start = ((), (), s32[]{:S(2)}) async-start(), calls=%async_computation.8 | async-start | bytes 12288000 | tf_op jit(solution)/shard_map/reduce_scatter | solution.py:838
  468.9 361.8 %reduce-scatter.15.cloned.1.call-start = ((), (), s32[]{:S(2)}) async-start(), calls=%async_computation.11 | async-start | bytes 2457600
  611.5 60.1 %collective-permute-start.32 = (bf16[320,2560]{1,0:T(8,128)(2,1)}, bf16[320,2560]{1,0:T(8,128)(2,1)}, u32[]{:S(2)}, u32[]{:S(2)}) collective-permute-start(bf16[320,2560]{1,0:T(8,128)(2,1)} %pad_maximum_fusion.7), channel_id=1, source_target_pairs={{0,16},{8,24},{16,0},{24,8},{1,17},{9,25},{17,1},{25,9},{2,18},{10... | collective-permute-start | bytes 4915208 | tf_op jit(solution)/shard_map/ppermute | solution.py:18
  613.4 58.2 %collective-permute-start.31 = (bf16[320,2560]{1,0:T(8,128)(2,1)}, bf16[320,2560]{1,0:T(8,128)(2,1)}, u32[]{:S(2)}, u32[]{:S(2)}) collective-permute-start(bf16[320,2560]{1,0:T(8,128)(2,1)} %pad_maximum_fusion.6), channel_id=1, source_target_pairs={{0,8},{8,0},{16,24},{24,16},{1,9},{9,1},{17,25},{25,17},{2,10},{10... | collective-permute-start | bytes 4915208 | tf_op jit(solution)/shard_map/ppermute | solution.py:18
  622.7 47.4 %collective-permute-start.29 = (bf16[512,256]{1,0:T(8,128)(2,1)}, bf16[512,256]{1,0:T(8,128)(2,1)S(1)}, u32[]{:S(2)}, u32[]{:S(2)}) collective-permute-start(bf16[512,256]{1,0:T(8,128)(2,1)} %get-tuple-element.208), channel_id=1, source_target_pairs={{4,0},{6,2},{0,4},{2,6},{5,1},{7,3},{1,5},{3,7},{12,8},{14,10},{8,... | collective-permute-start | bytes 786440 | tf_op jit(solution)/shard_map/ppermute | solution.py:859
  622.8 48.8 %collective-permute-start.30 = (bf16[512,256]{1,0:T(8,128)(2,1)}, bf16[512,256]{1,0:T(8,128)(2,1)S(1)}, u32[]{:S(2)}, u32[]{:S(2)}) collective-permute-start(bf16[512,256]{1,0:T(8,128)(2,1)} %get-tuple-element.207), channel_id=1, source_target_pairs={{2,0},{4,2},{6,4},{0,6},{3,1},{5,3},{7,5},{1,7},{10,8},{12,10},{14... | collective-permute-start | bytes 786440 | tf_op jit(solution)/shard_map/ppermute | solution.py:859
  671.8 57.7 %collective-permute-start.38 = (bf16[256,2560]{1,0:T(8,128)(2,1)S(1)}, bf16[256,2560]{1,0:T(8,128)(2,1)}, u32[]{:S(2)}, u32[]{:S(2)}) collective-permute-start(bf16[256,2560]{1,0:T(8,128)(2,1)S(1)} %pad_maximum_fusion.12), channel_id=1, source_target_pairs={{0,16},{8,24},{16,0},{24,8},{1,17},{9,25},{17,1},{25,9},{2,18},{10... | collective-permute-start | bytes 3932168 | tf_op jit(solution)/shard_map/ppermute | solution.py:18
  672.1 58.6 %collective-permute-start.37 = (bf16[256,2560]{1,0:T(8,128)(2,1)S(1)}, bf16[256,2560]{1,0:T(8,128)(2,1)}, u32[]{:S(2)}, u32[]{:S(2)}) collective-permute-start(bf16[256,2560]{1,0:T(8,128)(2,1)S(1)} %pad_maximum_fusion.11), channel_id=1, source_target_pairs={{0,8},{8,0},{16,24},{24,16},{1,9},{9,1},{17,25},{25,17},{2,10},{10... | collective-permute-start | bytes 3932168 | tf_op jit(solution)/shard_map/ppermute | solution.py:18
  678.5 51.1 %collective-permute-start.35 = (bf16[160,2560]{1,0:T(8,128)(2,1)S(1)}, bf16[160,2560]{1,0:T(8,128)(2,1)S(1)}, u32[]{:S(2)}, u32[]{:S(2)}) collective-permute-start(bf16[160,2560]{1,0:T(8,128)(2,1)S(1)} %get-tuple-element.177), channel_id=1, source_target_pairs={{0,16},{8,24},{16,0},{24,8},{1,17},{9,25},{17,1},{25,9},{2,18},{10... | collective-permute-start | bytes 2457608 | tf_op jit(solution)/shard_map/ppermute | solution.py:18
  738.5 147.6 %reduce-scatter.11.cloned.1.call-start = ((), (), s32[]{:S(2)}) async-start(), calls=%async_computation.9 | async-start | bytes 2457600 | tf_op jit(solution)/shard_map/reduce_scatter | solution.py:893
  769.0 54.8 %collective-permute-start.42 = (bf16[640,1920]{1,0:T(8,128)(2,1)}, bf16[640,1920]{1,0:T(8,128)(2,1)}, u32[]{:S(2)}, u32[]{:S(2)}) collective-permute-start(bf16[640,1920]{1,0:T(8,128)(2,1)} %reduce-scatter.9.cloned.1.call-done.refs_0_), channel_id=1, source_target_pairs={{0,16},{8,24},{16,0},{24,8},{1,17},{9,25},{17,1},{25,9},{2,18},{10... | collective-permute-start | bytes 7372808 | tf_op jit(solution)/shard_map/ppermute | solution.py:18
  769.1 57.1 %collective-permute-start.41 = (bf16[640,1920]{1,0:T(8,128)(2,1)}, bf16[640,1920]{1,0:T(8,128)(2,1)}, u32[]{:S(2)}, u32[]{:S(2)}) collective-permute-start(bf16[640,1920]{1,0:T(8,128)(2,1)} %reduce-scatter.9.cloned.1.call-done.refs_0_), channel_id=1, source_target_pairs={{0,8},{8,0},{16,24},{24,16},{1,9},{9,1},{17,25},{25,17},{2,10},{10... | collective-permute-start | bytes 7372808 | tf_op jit(solution)/shard_map/ppermute | solution.py:18
  803.5 86.3 %collective-permute-start.48 = (bf16[128,2560]{1,0:T(8,128)(2,1)}, bf16[128,2560]{1,0:T(8,128)(2,1)}, u32[]{:S(2)}, u32[]{:S(2)}) collective-permute-start(bf16[128,2560]{1,0:T(8,128)(2,1)} %add_convert_fusion.5), channel_id=1, source_target_pairs={{0,8},{8,0},{16,24},{24,16},{1,9},{9,1},{17,25},{25,17},{2,10},{10... | collective-permute-start | bytes 1966088 | tf_op jit(solution)/shard_map/ppermute | solution.py:18
  826.2 46.3 %collective-permute-start.43 = (bf16[320,1920]{1,0:T(8,128)(2,1)}, bf16[320,1920]{1,0:T(8,128)(2,1)}, u32[]{:S(2)}, u32[]{:S(2)}) collective-permute-start(bf16[320,1920]{1,0:T(8,128)(2,1)} %slice.279), channel_id=1, source_target_pairs={{0,8},{8,0},{16,24},{24,16},{1,9},{9,1},{17,25},{25,17},{2,10},{10... | collective-permute-start | bytes 3686408 | tf_op jit(solution)/shard_map/ppermute | solution.py:18
  828.6 45.6 %collective-permute-start.44 = (bf16[320,1920]{1,0:T(8,128)(2,1)}, bf16[320,1920]{1,0:T(8,128)(2,1)}, u32[]{:S(2)}, u32[]{:S(2)}) collective-permute-start(bf16[320,1920]{1,0:T(8,128)(2,1)} %slice.280), channel_id=1, source_target_pairs={{0,16},{8,24},{16,0},{24,8},{1,17},{9,25},{17,1},{25,9},{2,18},{10... | collective-permute-start | bytes 3686408 | tf_op jit(solution)/shard_map/ppermute | solution.py:18
  (108 other events, 1781.7 us)
Sparse Core Ops, SparseCore 0:
  10.2 38.4 all-gather.6
  50.8 41.9 all-gather.4
  95.0 191.8 all-gather.10
  288.8 92.2 all-gather.8
  387.6 93.3 reduce-scatter.12
  483.9 190.3 reduce-scatter.8
  738.6 49.1 reduce-scatter.14
  800.0 40.9 reduce-scatter.10

commit v4 on v3

--- a/solution.py
+++ b/solution.py
@@ -210,6 +210,70 @@
         cost_estimate=pl.CostEstimate(flops=1000, bytes_accessed=1000, transcendentals=0),
         name="unit_grads",
     )(seq_at.reshape(1), grads, *weights)
+
+
+def return_kernel(
+    keep_ref, sent_ref, out_ref, land_ref, pass_ref, ring_ref, early_ref, back_ref, sems
+):
+    seqs, shards = lax.axis_size("seq"), lax.axis_size("fsdp")
+    seq_at, shard_at = lax.axis_index("seq"), lax.axis_index("fsdp")
+    rows = out_ref.shape[0]
+    core = {"tensor": 1 - lax.axis_index("tensor")}
+    behind, ahead = ({"seq": lax.rem(seq_at + by, seqs)} for by in (seqs - 1, 1))
+    ring = [{"fsdp": lax.rem(shard_at + at, shards)} for at in range(1, shards)]
+    greet([core, behind, ahead, *ring])
+    slots = [pl.ds(at * rows, rows) for at in range(shards + 1)]
+    lands = {
+        at: send(sent_ref.at[slots[at], :], land_ref.at[slots[at], :], sems, at, core)
+        for at in (*range(1, shards), 0, shards)
+    }
+
+    def chip_sum(at):
+        lands[at].wait_recv()
+        return keep_ref[slots[at], :] + land_ref[slots[at], :].astype(F32)
+
+    rings = []
+    for at in range(1, shards):
+        pass_ref[at - 1] = chip_sum(at).astype(BF16)
+        rings.append(send(pass_ref.at[at - 1], ring_ref.at[at - 1], sems, shards + at, ring[at - 1]))
+    early, own = chip_sum(0), chip_sum(shards)
+    for at, copy in enumerate(rings, 1):
+        copy.wait_recv()
+        piece = ring_ref[at - 1].astype(F32)
+        share = jnp.where(shard_at >= at, 1.0, 0.0).astype(F32)
+        early = early + piece * share
+        own = own + piece * (1.0 - share)
+    early_ref[...] = early.astype(BF16)
+    shift = send(early_ref, back_ref, sems, 2 * shards, behind)
+    shift.wait_recv()
+    share = jnp.where(seq_at < seqs - 1, 1.0, 0.0).astype(F32)
+    out_ref[...] = own + back_ref[...].astype(F32) * share
+    for copy in (*lands.values(), *rings, shift):
+        copy.wait_send()
+
+
+def return_pairs(keep, sent, rows, shards, collective_id):
+    size = keep.shape[1]
+    vmem = pl.BlockSpec(memory_space=pltpu.VMEM)
+    return pl.pallas_call(
+        return_kernel,
+        out_shape=jax.ShapeDtypeStruct((rows, size), F32),
+        in_specs=[vmem, vmem],
+        out_specs=vmem,
+        scratch_shapes=[
+            pltpu.VMEM(sent.shape, BF16),
+            pltpu.VMEM((shards - 1, rows, size), BF16),
+            pltpu.VMEM((shards - 1, rows, size), BF16),
+            pltpu.VMEM((rows, size), BF16),
+            pltpu.VMEM((rows, size), BF16),
+            pltpu.SemaphoreType.DMA((2, 2 * shards + 1)),
+        ],
+        compiler_params=pltpu.CompilerParams(
+            collective_id=collective_id, has_side_effects=True, vmem_limit_bytes=24 * 2**20
+        ),
+        cost_estimate=pl.CostEstimate(flops=1000, bytes_accessed=1000, transcendentals=0),
+        name="return_pairs",
+    )(keep, sent)
 
 
 def trade_kernel(to_rows, value_ref, out_ref, sems, local_sems):
@@ -702,6 +766,15 @@
     def order_cols(pieces):
         stacked = jnp.stack(pieces)
         return [pick(stacked, seq_at ^ at) for at in range(seqs)]
+
+    def order_rows(pieces):
+        count, width = pieces[0].shape
+        rows_all = jnp.zeros((seqs * count, width), F32)
+        for at, piece in enumerate(pieces):
+            rows_all = lax.dynamic_update_slice_in_dim(
+                rows_all, piece.astype(F32), (seq_at ^ at) * count, 0
+            )
+        return rows_all
 
     gain_one, gain_two = gain_attn.astype(F32)[:, None], gain_ffn.astype(F32)[:, None]
     gains = jnp.stack([gain_attn, gain_ffn])
@@ -839,44 +912,48 @@
 
     grad_attn_out = whole_rows(grad_hidden.astype(BF16))
     grad_heads = times_transpose(grad_attn_out, out_weight).astype(BF16)
-    ffn_part = jnp.dot(
-        after(activation, grad_unit_two), down_weight, preferred_element_type=F32
-    ).astype(BF16)
-    out_term = rows_product(head_outputs, grad_attn_out).astype(BF16)
-    down_near = gather_near(down_shard)
-    grad_heads, down_near, ffn_part, out_term = lax.optimization_barrier(
-        (grad_heads, down_near, ffn_part, out_term)
-    )
-    out_parts = [part_of(out_term, seq_at ^ at, out_rows, 0) for at in range(seqs)]
-    out_near = scatter_near(out_parts)
+    grad_heads, down_shard = lax.optimization_barrier((grad_heads, down_shard))
     grad_query_proj, pair_keep, pair_sent = attend_back(
         first_pos, core, queries, grad_heads, key_rows, value_rows, log_total,
         jnp.concatenate([cosine, cosine], axis=1), jnp.concatenate([sine, -sine], axis=1),
     )
-    pair_grads = pair_keep + swap(pair_sent).astype(F32)
-    pair_grads, down_near = lax.optimization_barrier((pair_grads, down_near))
-    returned = [
-        lax.ppermute(
-            pair_grads[at * rows : (at + 1) * rows].astype(BF16),
-            "fsdp", [((source_at - at) % shards, source_at) for source_at in range(shards)],
-        )
-        for at in range(1, shards)
-    ]
-    ffn_cores = core_sum(ffn_part)
-    returned, out_near, ffn_cores = lax.optimization_barrier((returned, out_near, ffn_cores))
+    pair_sent, down_near = lax.optimization_barrier((pair_sent, gather_near(down_shard)))
+    out_term = rows_product(after(head_outputs, pair_sent), grad_attn_out).astype(BF16)
+    out_parts = [part_of(out_term, seq_at ^ at, out_rows, 0) for at in range(seqs)]
+    out_near = scatter_near(out_parts)
+    count = seqs * half
+    activation = after(activation, out_term)
+    ffn_other = jnp.dot(activation[count:], down_weight, preferred_element_type=F32)
+    ffn_part = jnp.dot(
+        after(activation[:count], ffn_other), down_weight, preferred_element_type=F32
+    )
+    ffn_part = (ffn_part + swap(ffn_other.astype(BF16)).astype(F32)).astype(BF16)
+    ffn_cores = [ffn_part[j * half : (j + 1) * half] for j in range(seqs)]
+    ffn_near = scatter_near(ffn_cores)
+    pair_keep, pair_sent, _ = lax.optimization_barrier((pair_keep, pair_sent, ffn_part))
+    if square:
+        own_total = return_pairs(pair_keep, pair_sent, rows, shards, 1 + 6)
+    else:
+        pair_grads = pair_keep + swap(pair_sent).astype(F32)
+        own_total = pair_grads[shards * rows :]
+        earlier_total = pair_grads[:rows]
+        for at in range(1, shards):
+            piece = lax.ppermute(
+                pair_grads[at * rows : (at + 1) * rows].astype(BF16),
+                "fsdp",
+                [((source_at - at) % shards, source_at) for source_at in range(shards)],
+            ).astype(F32)
+            own_total = own_total + jnp.where(shard_at >= at, 0.0, piece)
+            earlier_total = earlier_total + jnp.where(shard_at >= at, piece, 0.0)
+        own_total = own_total + seq_shift(earlier_total.astype(BF16), -1).astype(F32)
+    own_total, out_near, ffn_near, down_near = lax.optimization_barrier(
+        (own_total, out_near, ffn_near, down_near)
+    )
     out_sum, out_far = scatter_far(out_parts, out_near)
-    own_total = pair_grads[shards * rows :]
-    earlier_total = pair_grads[:rows]
-    for at, piece in enumerate(returned, 1):
-        own_total = own_total + jnp.where(shard_at >= at, 0.0, piece.astype(F32))
-        earlier_total = earlier_total + jnp.where(shard_at >= at, piece.astype(F32), 0.0)
-    own_total = own_total + seq_shift(earlier_total.astype(BF16), -1).astype(F32)
     grad_pair = jnp.where(first, rotate(own_total, cosine, -sine), own_total).astype(BF16)
-    ffn_near = scatter_near(ffn_cores)
-    grad_pair, in_shard, out_far, ffn_near, down_parts = lax.optimization_barrier(
-        (grad_pair, in_shard, out_far, ffn_near, gather_far(down_shard, down_near))
-    )
-    out_sum = scatter_end(out_sum, out_far)
+    grad_pair, in_shard, out_far, down_parts = lax.optimization_barrier(
+        (grad_pair, in_shard, out_far, gather_far(down_shard, down_near))
+    )
     grad_proj = jnp.concatenate([grad_query_proj, grad_pair], axis=1)
     if square:
         grad_rows = trade(grad_proj, True, 6)
@@ -889,9 +966,10 @@
         grad_rows = grad_rows.reshape(2 * seqs * half, proj_cols)
     proj_term = rows_product(rows_one, grad_rows).astype(BF16)
 
-    out_shard = lax.psum_scatter(out_sum.astype(BF16), "fsdp", scatter_dimension=1, tiled=True)
-    proj_sum = lax.psum_scatter(proj_term, "fsdp", scatter_dimension=0, tiled=True)
-    in_parts = plane_gather(after(in_shard, grad_rows))
+    out_sum = scatter_end(out_sum, after(out_far, proj_term))
+    last_term = jnp.concatenate([proj_term, out_sum.astype(BF16).T], axis=1)
+    last_sum = lax.psum_scatter(last_term, "fsdp", scatter_dimension=0, tiled=True)
+    in_near = gather_near(after(in_shard, grad_rows))
     grad_proj = after(grad_proj, proj_term)
     if square:
         unit_part = unit_grads(seq_at, grad_proj, proj_pieces)
@@ -900,20 +978,16 @@
             times_transpose(part_of(grad_proj, seq_at ^ at, proj_cols, 1), proj_pieces[at])
             for at in range(seqs)
         )
+    down_grad = order_rows(after(down_parts, grad_rows))
+    ffn_sum, ffn_far = scatter_far(ffn_cores, after(ffn_near, proj_term))
+    in_near, unit_part, down_grad = lax.optimization_barrier((in_near, unit_part, down_grad))
+    in_parts = gather_far(in_shard, in_near)
     grad_unit_one = my_half(unit_part) + swap(other_half(unit_part))
-    grad_unit_one, proj_sum = lax.optimization_barrier((grad_unit_one, proj_sum))
-    ffn_sum, ffn_far = scatter_far(ffn_cores, after(ffn_near, proj_term))
-    ffn_out = scatter_end(ffn_sum, after(ffn_far, grad_unit_one))
-    layer_out = whole_rows((hidden_in + ffn_out).astype(BF16))
-    down_parts = lax.optimization_barrier((*down_parts, grad_unit_one))[:-1]
-    down_grad = jnp.concatenate(order_cols(down_parts), axis=0).astype(F32)
-    grad_input = whole_rows(
-        grad_hidden + norm_pull(source, inverse_one, grad_unit_one * gains[0])
-    )
+    layer_half = (hidden_in + scatter_end(ffn_sum, ffn_far)).astype(BF16)
+    grad_half = grad_hidden + norm_pull(source, inverse_one, grad_unit_one * gains[0])
+    in_parts, grad_half = lax.optimization_barrier((in_parts, grad_half))
+    layer_out, grad_input = whole_rows(layer_half), whole_rows(grad_half)
     if kernels and square:
-        in_parts, down_grad, grad_input, layer_out = lax.optimization_barrier(
-            (in_parts, down_grad, grad_input, layer_out)
-        )
         gate_grad, up_grad, gain_two_half = join_columns(seq_at, in_parts, w_gate, w_up)
     else:
         in_parts = order_cols(in_parts)
@@ -934,9 +1008,11 @@
             gate_grad * w_gate.astype(F32) + up_grad * w_up.astype(F32), axis=1
         )
     gain_two_half = gain_two_half / gain_two[:, 0]
-    out_grad = jnp.concatenate(order_cols(plane_gather(out_shard)), axis=0).astype(F32)
-
-    proj_grad = jnp.concatenate(order_cols(plane_gather(proj_sum)), axis=1).astype(F32)
+    last_parts = gather_far(last_sum, after(gather_near(last_sum), gate_grad))
+    out_grad = order_rows([piece[:, proj_cols:].T for piece in last_parts])
+    proj_grad = jnp.concatenate(
+        order_cols([piece[:, :proj_cols] for piece in last_parts]), axis=1
+    ).astype(F32)
     gain_one_half = jnp.sum(proj_grad * proj_shard.astype(F32), axis=1) / gain_one[:, 0]
     query_grad = proj_grad[:, :head_cols]
     pair_grad = proj_grad[:, head_cols:]

time: 972 us -> 940 us (0.967)
  Pallas kernels: 359 us -> 415 us
  waiting for transfers between devices: 208 us -> 158 us
  other arithmetic: 94.4 us -> 68.8 us
  starting transfers between devices: 71.9 us -> 60.8 us
    pallas_call x0 -> x1, Pallas kernels: none -> 65.2 us  [return_pairs(): pl.pallas_call(return_kernel, out_shape=jax.ShapeDtypeStruct((rows, size)...]
    ppermute x3 -> x0, waiting for transfers between devices: 36.1 us -> none  [local(): lax.ppermute(pair_grads[at * rows:(at + 1) * rows].astype(BF16), 'fsdp',...]
    convert_element_type x6 -> x1, other arithmetic: 25.3 us -> 0.51 us  [local(): proj_grad = jnp.concatenate(order_cols([piece[:, :proj_cols] for piece in...]
    ppermute x2 -> x1, waiting for transfers between devices: 19.9 us -> 4.29 us  [seq_shift(): lax.ppermute(value, 'seq', [(at, at + steps) for at in range(leading, las...]
    ppermute x36 -> x32, starting transfers between devices: 31.4 us -> 27.6 us  [exchange(): return lax.ppermute(value, 'seq', [(at, at ^ step) for at in range(count)])]
    ppermute x13 -> x12, starting transfers between devices: 24.5 us -> 21.9 us  [swap(): return lax.ppermute(value, 'tensor', [(0, 1), (1, 0)])]
    ppermute x36 -> x32, waiting for transfers between devices: 109 us -> 107 us  [exchange(): return lax.ppermute(value, 'seq', [(at, at ^ step) for at in range(count)])]
  transfers between devices with their start and end apart: 68 -> 58, of which waited for: 20 -> 23; matrix products, arithmetic and copies ran while one was open for 29% -> 26% of each run, Pallas kernels for 37% -> 43%
where the time goes in v4:
time: 940 us; the launch traced here: 931 us
  Pallas kernels  415 us (44%)
  waiting for transfers between devices  158 us (17%)
  local copies, waits for them, and re-layouts  121 us (13%)
  matrix products  92 us (10%)
  other arithmetic  68.8 us (7%)
  starting transfers between devices  60.8 us (6%)
  between operations  15.7 us (2%)
    ppermute x32, waiting for transfers between devices, exchange(): return lax.ppermute(value, 'seq', [(at, at ^ step) for at in range(count)])  107 us
    pallas_call x2, Pallas kernels, gather_rows(): pl.pallas_call(rows_kernel, out_shape=jax.ShapeDtypeStruct((8 * half, wid...  102 us
    pallas_call x1, Pallas kernels, return_pairs(): pl.pallas_call(return_kernel, out_shape=jax.ShapeDtypeStruct((rows, size)...  65.2 us
    dot_general x4, matrix products, rows_product(): lax.dot_general(left, right, (((0,), (0,)), ((), ())), preferred_element_...  61.3 us
    unnamed x145, local copies, waits for them, and re-layouts  57.5 us
    pallas_call x2, Pallas kernels, trade(): pl.pallas_call(functools.partial(trade_kernel, to_rows), out_shape=jax.Sh...  53.3 us
    pallas_call x1, Pallas kernels, scatter_rows(): pl.pallas_call(sum_kernel, out_shape=jax.ShapeDtypeStruct((half, width),...  50.3 us
    pallas_call x1, Pallas kernels, ffn_back(): pl.pallas_call(ffn_back_kernel, out_shape=(jax.ShapeDtypeStruct((count, 2...  43.2 us
  transfers between devices with their start and end apart: 58, of which 23 were waited for; matrix products, arithmetic and copies ran while one was open for 26% of the time, Pallas kernels for 43%

profile of v4, /device:TPU:9, one launch (start us, length us, event | category | flops | bytes accessed | tf_op | source)
XLA Modules:
  0.0 930.8 jit_solution(2416350135399814330)
XLA Ops:
  32.7 51.9 %gather_rows.2 = bf16[2048,2560]{1,0:T(8,128)(2,1)} custom-call(bf16[256,2560]{1,0:T(8,128)(2,1)} %fusion.3.own_ref), custom_call_target="tpu_custom_call" | custom-call | flops 1000 | bytes 1000 | tf_op jit(solution)/shard_map/gather_rows/pallas_call | solution.py:176
  105.3 34.1 %trade.2 = bf16[512,1536]{1,0:T(8,128)(2,1)} custom-call(bf16[2048,384]{1,0:T(8,128)(2,1)} %copy.33.value_ref), custom_call_target="tpu_custom_call" | custom-call | flops 1000 | bytes 1000 | tf_op jit(solution)/shard_map/trade/pallas_call | solution.py:305
  169.3 15.2 %collective-permute-done.5 = bf16[512,256]{1,0:T(8,128)(2,1)} collective-permute-done((bf16[512,256]{1,0:T(8,128)(2,1)}, bf16[512,256]{1,0:T(8,128)(2,1)}, u32[]{:S(2)}, u32[]{:S(2)}) %collective-permute-start.5) | collective-permute-done | bytes 262176 | tf_op jit(solution)/shard_map/ppermute | solution.py:857
  185.5 16.8 %collective-permute-done.6 = bf16[512,256]{1,0:T(8,128)(2,1)} collective-permute-done((bf16[512,256]{1,0:T(8,128)(2,1)}, bf16[512,256]{1,0:T(8,128)(2,1)}, u32[]{:S(2)}, u32[]{:S(2)}) %collective-permute-start.6) | collective-permute-done | bytes 262176 | tf_op jit(solution)/shard_map/ppermute | solution.py:857
  205.6 8.6 collective-permute-start.11
  222.9 15.4 %attend.1 = (bf16[512,1280]{1,0:T(8,128)(2,1)S(1)}, f32[5,1,512]{2,1,0:T(1,128)S(1)}) custom-call(s32[1]{0:T(128)} %bitcast.pos_ref, bf16[512,1280]{1,0:T(8,128)(2,1)S(1)} %slice.194.q_ref, bf16[2560,256]{1,0:T(8,128)(2,1)S(1)} %get-tuple-element.190.k_ref, bf16[2560,256]{1,0:T(8,128)(2,1)S(1)} %get-tuple-element.189.v_ref), custom_call_target="tpu_custom_call" | custom-call | flops 1000 | bytes 1000 | tf_op jit(solution)/shard_map/attend/pallas_call | solution.py:472
  280.8 50.1 %gather_rows.3.x_ref = bf16[2048,2560]{1,0:T(8,128)(2,1)} custom-call(bf16[256,2560]{1,0:T(8,128)(2,1)} %multiply_convert_fusion.own_ref), custom_call_target="tpu_custom_call" | custom-call | flops 1000 | bytes 1000 | tf_op jit(solution)/shard_map/gather_rows/pallas_call | solution.py:176
  330.9 32.8 %ffn.1 = (bf16[2048,960]{1,0:T(8,128)(2,1)}, bf16[2048,960]{1,0:T(8,128)(2,1)}, bf16[2048,960]{1,0:T(8,128)(2,1)}) custom-call(bf16[2048,2560]{1,0:T(8,128)(2,1)} %gather_rows.3.x_ref, bf16[2560,1920]{1,0:T(8,128)(2,1)} %all-gather.9.cloned.1.call-done.w_ref), custom_call_target="tpu_custom_call" | custom-call | flops 1000 | bytes 1000 | tf_op jit(solution)/shard_map/ffn/pallas_call | solution.py:626
  363.8 15.9 %convolution_convert_fusion.2 = bf16[2560,960]{0,1:T(8,128)(2,1)} fusion(bf16[2048,2560]{1,0:T(8,128)(2,1)} %constant_dynamic-update-slice_fusion.5.c_ref, bf16[2048,960]{1,0:T(8,128)(2,1)} %get-tuple-element.111), kind=kOutput, calls=%fused_computation.3 | convolution fusion | flops 10068787200 | bytes 19333120 | tf_op jit(solution)/shard_map/dot_general | solution.py:78
  389.1 43.2 %ffn_back.1 = (bf16[2048,1920]{1,0:T(8,128)(2,1)}, bf16[2048,2560]{1,0:T(8,128)(2,1)}) custom-call(bf16[2048,2560]{1,0:T(8,128)(2,1)} %constant_dynamic-update-slice_fusion.5.c_ref, bf16[960,2560]{1,0:T(8,128)(2,1)} %all-gather.11.cloned.1.call-done.d_ref, bf16[2048,960]{1,0:T(8,128)(2,1)} %get-tuple-element.96.a_ref, ...), custom_call_target="tpu_custom_call" | custom-call | flops 1000 | bytes 1000 | tf_op jit(solution)/shard_map/ffn_back/pallas_call | solution.py:660
  437.8 28.0 %convolution_convert_fusion = bf16[2560,1920]{1,0:T(8,128)(2,1)} fusion(bf16[2048,2560]{1,0:T(8,128)(2,1)} %gather_rows.3.x_ref, bf16[2048,1920]{1,0:T(8,128)(2,1)} %get-tuple-element.103), kind=kOutput, calls=%fused_computation | convolution fusion | flops 20137574400 | bytes 28180480 | tf_op jit(solution)/shard_map/dot_general | solution.py:78
  472.9 50.3 %scatter_rows.1 = f32[256,2560]{1,0:T(8,128)S(1)} custom-call(bf16[2048,2560]{1,0:T(8,128)(2,1)S(1)} %copy-done.7), custom_call_target="tpu_custom_call" | custom-call | flops 1000 | bytes 1000 | tf_op jit(solution)/shard_map/scatter_rows/pallas_call | solution.py:396
  542.0 26.2 %attend_back.1 = (bf16[512,1280]{1,0:T(8,128)(2,1)S(1)}, f32[2560,256]{1,0:T(8,128)}, bf16[2560,256]{1,0:T(8,128)(2,1)S(1)}) custom-call(s32[2]{0:T(128)S(1)} %pad_add_fusion.pos_ref, bf16[512,1280]{1,0:T(8,128)(2,1)S(1)} %copy-done.4, bf16[512,1280]{1,0:T(8,128)(2,1)S(1)} %copy-done.19, bf16[2560,256]{1,0:T(8,128)(2,1)} %copy-done.6, ...), custom_call_target="tpu_custom_call" | custom-call | flops 1000 | bytes 1000 | tf_op jit(solution)/shard_map/attend_back/pallas_call | solution.py:564
  568.3 8.8 convolution_convert_fusion.1
  610.7 65.2 %return_pairs.1 = f32[512,256]{1,0:T(8,128)S(1)} custom-call(f32[2560,256]{1,0:T(8,128)S(1)} %copy-done.12, bf16[2560,256]{1,0:T(8,128)(2,1)S(1)} %copy-done.18), custom_call_target="tpu_custom_call" | custom-call | flops 1000 | bytes 1000 | tf_op jit(solution)/shard_map/return_pairs/pallas_call | solution.py:258
  694.9 16.5 %collective-permute-done.32 = bf16[160,2560]{1,0:T(8,128)(2,1)} collective-permute-done((bf16[160,2560]{1,0:T(8,128)(2,1)S(1)}, bf16[160,2560]{1,0:T(8,128)(2,1)}, u32[]{:S(2)}, u32[]{:S(2)}) %collective-permute-start.32) | collective-permute-done | bytes 819232 | tf_op jit(solution)/shard_map/ppermute | solution.py:18
  715.2 19.2 %trade.3 = bf16[2048,384]{1,0:T(8,128)(2,1)} custom-call(bf16[512,1536]{1,0:T(8,128)(2,1)} %constant_dynamic-update-slice_fusion.13.value_ref.grad_ref), custom_call_target="tpu_custom_call" | custom-call | flops 1000 | bytes 1000 | tf_op jit(solution)/shard_map/trade/pallas_call | solution.py:305
  736.9 8.7 convolution_convert_fusion.3
  762.1 10.1 %unit_grads.1 = f32[512,2560]{1,0:T(8,128)} custom-call(s32[1]{0:T(128)} %bitcast.19.seq_ref, bf16[512,1536]{1,0:T(8,128)(2,1)S(1)} %copy-done.2, bf16[2560,384]{1,0:T(8,128)(2,1)S(1)} %copy-done.14, bf16[2560,384]{1,0:T(8,128)(2,1)S(1)} %copy-done.11, bf16[2560,384]{1,0:T(8,128)(2,1)} %collective-permute-done.21.refs_2_, bf16[2560,384]{1,0:T(8,128)(2,1)S(1)} %copy-done.9), custom_call_target="tpu_custom_call" | custom-call | flops 1000 | bytes 1000 | tf_op jit(solution)/shard_map/unit_grads/pallas_call | solution.py:204
  772.5 16.4 %collective-permute-done.39.refs_1_ = bf16[640,1920]{1,0:T(8,128)(2,1)} collective-permute-done((bf16[640,1920]{1,0:T(8,128)(2,1)}, bf16[640,1920]{1,0:T(8,128)(2,1)}, u32[]{:S(2)}, u32[]{:S(2)}) %collective-permute-start.39) | collective-permute-done | bytes 2457632 | tf_op jit(solution)/shard_map/ppermute | solution.py:18
  804.9 19.6 %collective-permute-done.41 = bf16[320,1920]{1,0:T(8,128)(2,1)S(1)} collective-permute-done((bf16[320,1920]{1,0:T(8,128)(2,1)S(1)}, bf16[320,1920]{1,0:T(8,128)(2,1)S(1)}, u32[]{:S(2)}, u32[]{:S(2)}) %collective-permute-start.41) | collective-permute-done | bytes 1228832 | tf_op jit(solution)/shard_map/ppermute | solution.py:18
  828.1 11.6 %collective-permute-done.36 = bf16[128,2560]{1,0:T(8,128)(2,1)S(1)} collective-permute-done((bf16[128,2560]{1,0:T(8,128)(2,1)S(1)}, bf16[128,2560]{1,0:T(8,128)(2,1)S(1)}, u32[]{:S(2)}, u32[]{:S(2)}) %collective-permute-start.36) | collective-permute-done | bytes 655392 | tf_op jit(solution)/shard_map/ppermute | solution.py:18
  850.1 16.2 %join_columns.1 = (f32[640,3840]{1,0:T(8,128)}, f32[640,3840]{1,0:T(8,128)}, f32[640,1]{1,0:T(8,128)S(1)}) custom-call(s32[1]{0:T(128)} %bitcast.19.seq_ref, bf16[640,1920]{1,0:T(8,128)(2,1)S(1)} %copy-done.13, bf16[640,1920]{1,0:T(8,128)(2,1)} %collective-permute-done.39.refs_1_, bf16[640,1920]{1,0:T(8,128)(2,1)} %collective-permute-done.40.refs_2_, ...), custom_call_target="tpu_custom_call" | custom-call | flops 1000 | bytes 1000 | tf_op jit(solution)/shard_map/join_columns/pallas_call | solution.py:706
  884.1 9.8 %collective-permute-done.45 = bf16[640,704]{0,1:T(8,128)(2,1)S(1)} collective-permute-done((bf16[640,704]{0,1:T(8,128)(2,1)S(1)}, bf16[640,704]{0,1:T(8,128)(2,1)S(1)}, u32[]{:S(2)}, u32[]{:S(2)}) %collective-permute-start.45) | collective-permute-done | bytes 901152 | tf_op jit(solution)/shard_map/ppermute | solution.py:18
  (400 shorter events, 324.5 us)
Async XLA Ops:
  7.2 77.5 %all-gather.7.cloned.1.call-start = ((), (), s32[]{:S(2)}) async-start(), calls=%async_computation.4 | async-start | bytes 2048000 | tf_op jit(solution)/shard_map/all_gather | solution.py:814
  9.4 83.4 %all-gather.5.cloned.1.call-start = ((), (), s32[]{:S(2)}) async-start(), calls=%async_computation.3 | async-start | bytes 2457600 | tf_op jit(solution)/shard_map/all_gather | solution.py:795
  12.2 318.7 %all-gather.9.cloned.1.call-start = ((), (), s32[]{:S(2)}) async-start(), calls=%async_computation.5 | async-start | bytes 12288000 | tf_op jit(solution)/shard_map/all_gather | solution.py:805
  22.9 366.2 %all-gather.11.cloned.1.call-start = ((), (), s32[]{:S(2)}) async-start(), calls=%async_computation.6 | async-start | bytes 6144000 | tf_op jit(solution)/shard_map/all_gather | solution.py:806
  84.7 65.4 %collective-permute-start.7 = (bf16[320,2560]{1,0:T(8,128)(2,1)}, bf16[320,2560]{1,0:T(8,128)(2,1)}, u32[]{:S(2)}, u32[]{:S(2)}) collective-permute-start(bf16[320,2560]{1,0:T(8,128)(2,1)} %all-gather.7.cloned.1.call-done), channel_id=1, source_target_pairs={{0,8},{8,0},{16,24},{24,16},{1,9},{9,1},{17,25},{25,17},{2,10},{10... | collective-permute-start | bytes 4915208 | tf_op jit(solution)/shard_map/ppermute | solution.py:18
  84.8 70.6 %collective-permute-start.8 = (bf16[320,2560]{1,0:T(8,128)(2,1)}, bf16[320,2560]{1,0:T(8,128)(2,1)}, u32[]{:S(2)}, u32[]{:S(2)}) collective-permute-start(bf16[320,2560]{1,0:T(8,128)(2,1)} %all-gather.7.cloned.1.call-done), channel_id=1, source_target_pairs={{0,16},{8,24},{16,0},{24,8},{1,17},{9,25},{17,1},{25,9},{2,18},{10... | collective-permute-start | bytes 4915208 | tf_op jit(solution)/shard_map/ppermute | solution.py:18
  152.2 52.1 %collective-permute-start.10 = (bf16[160,2560]{1,0:T(8,128)(2,1)}, bf16[160,2560]{1,0:T(8,128)(2,1)S(1)}, u32[]{:S(2)}, u32[]{:S(2)}) collective-permute-start(bf16[160,2560]{1,0:T(8,128)(2,1)} %slice.255), channel_id=1, source_target_pairs={{0,16},{8,24},{16,0},{24,8},{1,17},{9,25},{17,1},{25,9},{2,18},{10... | collective-permute-start | bytes 2457608 | tf_op jit(solution)/shard_map/ppermute | solution.py:18
  157.4 46.9 %collective-permute-start.9 = (bf16[160,2560]{1,0:T(8,128)(2,1)}, bf16[160,2560]{1,0:T(8,128)(2,1)}, u32[]{:S(2)}, u32[]{:S(2)}) collective-permute-start(bf16[160,2560]{1,0:T(8,128)(2,1)} %slice.254), channel_id=1, source_target_pairs={{0,8},{8,0},{16,24},{24,16},{1,9},{9,1},{17,25},{25,17},{2,10},{10... | collective-permute-start | bytes 2457608 | tf_op jit(solution)/shard_map/ppermute | solution.py:18
  158.3 44.0 %collective-permute-start.6 = (bf16[512,256]{1,0:T(8,128)(2,1)}, bf16[512,256]{1,0:T(8,128)(2,1)}, u32[]{:S(2)}, u32[]{:S(2)}) collective-permute-start(bf16[512,256]{1,0:T(8,128)(2,1)} %get-tuple-element.195), channel_id=1, source_target_pairs={{0,2},{2,4},{4,6},{6,0},{1,3},{3,5},{5,7},{7,1},{8,10},{10,12},{12... | collective-permute-start | bytes 786440 | tf_op jit(solution)/shard_map/ppermute | solution.py:857
  162.5 373.1 %reduce-scatter.10.cloned.1.call-start = ((), (), s32[]{:S(2)}) async-start(), calls=%async_computation.8 | async-start | bytes 6553600
  242.1 34.0 %collective-permute-start.12 = (f32[256,2560]{1,0:T(8,128)S(1)}, f32[256,2560]{1,0:T(8,128)S(1)}, u32[]{:S(2)}, u32[]{:S(2)}) collective-permute-start(f32[256,2560]{1,0:T(8,128)S(1)} %constant_dynamic-slice_fusion.15), channel_id=1, source_target_pairs={{0,1},{1,0},{2,3},{3,2},{4,5},{5,4},{6,7},{7,6},{8,9},{9,8},{10,11... | collective-permute-start | bytes 7864328 | tf_op jit(solution)/shard_map/ppermute | solution.py:22
  387.5 324.0 %reduce-scatter.8.cloned.1.call-start = ((), (), s32[]{:S(2)}) async-start(), calls=%async_computation.7 | async-start | bytes 12288000 | tf_op jit(solution)/shard_map/reduce_scatter | solution.py:911
  387.5 44.8 %collective-permute-start.20 = (bf16[2560,384]{1,0:T(8,128)(2,1)}, bf16[2560,384]{1,0:T(8,128)(2,1)S(1)}, u32[]{:S(2)}, u32[]{:S(2)}) collective-permute-start(bf16[2560,384]{1,0:T(8,128)(2,1)} %all-gather.5.cloned.1.call-done.refs_0_), channel_id=1, source_target_pairs={{0,8},{8,0},{16,24},{24,16},{1,9},{9,1},{17,25},{25,17},{2,10},{10... | collective-permute-start | bytes 5898248 | tf_op jit(solution)/shard_map/ppermute | solution.py:18
  388.8 44.3 %collective-permute-start.21 = (bf16[2560,384]{1,0:T(8,128)(2,1)}, bf16[2560,384]{1,0:T(8,128)(2,1)}, u32[]{:S(2)}, u32[]{:S(2)}) collective-permute-start(bf16[2560,384]{1,0:T(8,128)(2,1)} %all-gather.5.cloned.1.call-done.refs_0_), channel_id=1, source_target_pairs={{0,16},{8,24},{16,0},{24,8},{1,17},{9,25},{17,1},{25,9},{2,18},{10... | collective-permute-start | bytes 5898248 | tf_op jit(solution)/shard_map/ppermute | solution.py:18
  468.9 401.8 %reduce-scatter.12.cloned.1.call-start = ((), (), s32[]{:S(2)}) async-start(), calls=%async_computation.9 | async-start | bytes 4915200
  590.6 85.2 %collective-permute-start.29 = (bf16[320,2560]{1,0:T(8,128)(2,1)}, bf16[320,2560]{1,0:T(8,128)(2,1)}, u32[]{:S(2)}, u32[]{:S(2)}) collective-permute-start(bf16[320,2560]{1,0:T(8,128)(2,1)} %pad_maximum_fusion.7), channel_id=1, source_target_pairs={{0,16},{8,24},{16,0},{24,8},{1,17},{9,25},{17,1},{25,9},{2,18},{10... | collective-permute-start | bytes 4915208 | tf_op jit(solution)/shard_map/ppermute | solution.py:18
  592.8 83.0 %collective-permute-start.28 = (bf16[320,2560]{1,0:T(8,128)(2,1)}, bf16[320,2560]{1,0:T(8,128)(2,1)}, u32[]{:S(2)}, u32[]{:S(2)}) collective-permute-start(bf16[320,2560]{1,0:T(8,128)(2,1)} %pad_maximum_fusion.6), channel_id=1, source_target_pairs={{0,8},{8,0},{16,24},{24,16},{1,9},{9,1},{17,25},{25,17},{2,10},{10... | collective-permute-start | bytes 4915208 | tf_op jit(solution)/shard_map/ppermute | solution.py:18
  604.9 71.0 %collective-permute-start.31 = (bf16[256,2560]{1,0:T(8,128)(2,1)}, bf16[256,2560]{1,0:T(8,128)(2,1)}, u32[]{:S(2)}, u32[]{:S(2)}) collective-permute-start(bf16[256,2560]{1,0:T(8,128)(2,1)} %pad_maximum_fusion.11), channel_id=1, source_target_pairs={{0,16},{8,24},{16,0},{24,8},{1,17},{9,25},{17,1},{25,9},{2,18},{10... | collective-permute-start | bytes 3932168 | tf_op jit(solution)/shard_map/ppermute | solution.py:18
  607.0 68.9 %collective-permute-start.30 = (bf16[256,2560]{1,0:T(8,128)(2,1)}, bf16[256,2560]{1,0:T(8,128)(2,1)}, u32[]{:S(2)}, u32[]{:S(2)}) collective-permute-start(bf16[256,2560]{1,0:T(8,128)(2,1)} %pad_maximum_fusion.10), channel_id=1, source_target_pairs={{0,8},{8,0},{16,24},{24,16},{1,9},{9,1},{17,25},{25,17},{2,10},{10... | collective-permute-start | bytes 3932168 | tf_op jit(solution)/shard_map/ppermute | solution.py:18
  734.4 54.4 %collective-permute-start.39 = (bf16[640,1920]{1,0:T(8,128)(2,1)}, bf16[640,1920]{1,0:T(8,128)(2,1)}, u32[]{:S(2)}, u32[]{:S(2)}) collective-permute-start(bf16[640,1920]{1,0:T(8,128)(2,1)} %reduce-scatter.8.cloned.1.call-done.refs_0_), channel_id=1, source_target_pairs={{0,8},{8,0},{16,24},{24,16},{1,9},{9,1},{17,25},{25,17},{2,10},{10... | collective-permute-start | bytes 7372808 | tf_op jit(solution)/shard_map/ppermute | solution.py:18
  736.3 54.3 %collective-permute-start.40 = (bf16[640,1920]{1,0:T(8,128)(2,1)}, bf16[640,1920]{1,0:T(8,128)(2,1)}, u32[]{:S(2)}, u32[]{:S(2)}) collective-permute-start(bf16[640,1920]{1,0:T(8,128)(2,1)} %reduce-scatter.8.cloned.1.call-done.refs_0_), channel_id=1, source_target_pairs={{0,16},{8,24},{16,0},{24,8},{1,17},{9,25},{17,1},{25,9},{2,18},{10... | collective-permute-start | bytes 7372808 | tf_op jit(solution)/shard_map/ppermute | solution.py:18
  792.5 34.9 %collective-permute-start.43 = (f32[256,2560]{1,0:T(8,128)S(1)}, f32[256,2560]{1,0:T(8,128)S(1)}, u32[]{:S(2)}, u32[]{:S(2)}) collective-permute-start(f32[256,2560]{1,0:T(8,128)S(1)} %constant_dynamic-slice_fusion.9), channel_id=1, source_target_pairs={{0,1},{1,0},{2,3},{3,2},{4,5},{5,4},{6,7},{7,6},{8,9},{9,8},{10,11... | collective-permute-start | bytes 7864328 | tf_op jit(solution)/shard_map/ppermute | solution.py:22
  802.6 37.1 %collective-permute-start.36 = (bf16[128,2560]{1,0:T(8,128)(2,1)S(1)}, bf16[128,2560]{1,0:T(8,128)(2,1)S(1)}, u32[]{:S(2)}, u32[]{:S(2)}) collective-permute-start(bf16[128,2560]{1,0:T(8,128)(2,1)S(1)} %get-tuple-element.177), channel_id=1, source_target_pairs={{0,16},{8,24},{16,0},{24,8},{1,17},{9,25},{17,1},{25,9},{2,18},{10... | collective-permute-start | bytes 1966088 | tf_op jit(solution)/shard_map/ppermute | solution.py:18
  803.5 36.2 %collective-permute-start.37 = (bf16[128,2560]{1,0:T(8,128)(2,1)S(1)}, bf16[128,2560]{1,0:T(8,128)(2,1)S(1)}, u32[]{:S(2)}, u32[]{:S(2)}) collective-permute-start(bf16[128,2560]{1,0:T(8,128)(2,1)S(1)} %get-tuple-element.178), channel_id=1, source_target_pairs={{0,8},{8,0},{16,24},{24,16},{1,9},{9,1},{17,25},{25,17},{2,10},{10... | collective-permute-start | bytes 1966088 | tf_op jit(solution)/shard_map/ppermute | solution.py:18
  (98 other events, 1410.0 us)
Sparse Core Ops, SparseCore 0:
  10.2 38.4 all-gather.6
  50.8 41.9 all-gather.4
  95.0 191.8 all-gather.8
  288.8 92.2 all-gather.10
  387.6 93.3 reduce-scatter.9
  483.8 190.3 reduce-scatter.7
  756.6 72.7 reduce-scatter.11

commit v5 on v4

--- a/solution.py
+++ b/solution.py
@@ -55,7 +55,7 @@
     return [exchange(by_one, 1), exchange(by_two, 2)]
 
 
-def scatter_far(parts, near):
+def scatter_far(parts, near, send_on=True):
     if len(parts) != 4:
         return sum((part.astype(F32) for part in near), parts[0].astype(F32)), []
     cut = parts[0].shape[0] // 2
@@ -63,6 +63,8 @@
     last_top = (parts[2][:cut].astype(F32) + by_one[cut:].astype(F32)).astype(BF16)
     last_low = (parts[1][cut:].astype(F32) + by_two[cut:].astype(F32)).astype(BF16)
     total = parts[0].astype(F32) + jnp.concatenate([by_one[:cut], by_two[:cut]]).astype(F32)
+    if not send_on:
+        return total, [last_top, last_low]
     return total, [exchange(last_top, 2), exchange(last_low, 1)]
 
 
@@ -212,21 +214,27 @@
     )(seq_at.reshape(1), grads, *weights)
 
 
-def return_kernel(
-    keep_ref, sent_ref, out_ref, land_ref, pass_ref, ring_ref, early_ref, back_ref, sems
-):
+def return_kernel(steps, keep_ref, sent_ref, *refs):
+    extras, (out_ref, *refs) = refs[: len(steps)], refs[len(steps) :]
+    extra_outs, refs = refs[: len(steps)], refs[len(steps) :]
+    land_ref, pass_ref, ring_ref, early_ref, back_ref, sems, extra_sems = refs
     seqs, shards = lax.axis_size("seq"), lax.axis_size("fsdp")
     seq_at, shard_at = lax.axis_index("seq"), lax.axis_index("fsdp")
     rows = out_ref.shape[0]
     core = {"tensor": 1 - lax.axis_index("tensor")}
-    behind, ahead = ({"seq": lax.rem(seq_at + by, seqs)} for by in (seqs - 1, 1))
+    behind = {"seq": lax.rem(seq_at + seqs - 1, seqs)}
     ring = [{"fsdp": lax.rem(shard_at + at, shards)} for at in range(1, shards)]
-    greet([core, behind, ahead, *ring])
+    greet([core, *({"seq": seq_at ^ step} for step in range(1, 4)), *ring])
     slots = [pl.ds(at * rows, rows) for at in range(shards + 1)]
     lands = {
         at: send(sent_ref.at[slots[at], :], land_ref.at[slots[at], :], sems, at, core)
         for at in (*range(1, shards), 0, shards)
     }
+
+    traded = [
+        send(source, target, extra_sems, at, {"seq": seq_at ^ step})
+        for at, (source, target, step) in enumerate(zip(extras, extra_outs, steps))
+    ]
 
     def chip_sum(at):
         lands[at].wait_recv()
@@ -250,16 +258,20 @@
     out_ref[...] = own + back_ref[...].astype(F32) * share
     for copy in (*lands.values(), *rings, shift):
         copy.wait_send()
-
-
-def return_pairs(keep, sent, rows, shards, collective_id):
+    for copy in traded:
+        copy.wait()
+
+
+def return_pairs(keep, sent, extras, steps, rows, shards, collective_id):
     size = keep.shape[1]
+    any_place = [pl.BlockSpec(memory_space=pl.ANY)] * len(steps)
     vmem = pl.BlockSpec(memory_space=pltpu.VMEM)
     return pl.pallas_call(
-        return_kernel,
-        out_shape=jax.ShapeDtypeStruct((rows, size), F32),
-        in_specs=[vmem, vmem],
-        out_specs=vmem,
+        functools.partial(return_kernel, steps),
+        out_shape=[jax.ShapeDtypeStruct((rows, size), F32)]
+        + [jax.ShapeDtypeStruct(value.shape, value.dtype) for value in extras],
+        in_specs=[vmem, vmem] + any_place,
+        out_specs=[vmem] + any_place,
         scratch_shapes=[
             pltpu.VMEM(sent.shape, BF16),
             pltpu.VMEM((shards - 1, rows, size), BF16),
@@ -267,13 +279,14 @@
             pltpu.VMEM((rows, size), BF16),
             pltpu.VMEM((rows, size), BF16),
             pltpu.SemaphoreType.DMA((2, 2 * shards + 1)),
+            pltpu.SemaphoreType.DMA((2, len(steps))),
         ],
         compiler_params=pltpu.CompilerParams(
             collective_id=collective_id, has_side_effects=True, vmem_limit_bytes=24 * 2**20
         ),
         cost_estimate=pl.CostEstimate(flops=1000, bytes_accessed=1000, transcendentals=0),
         name="return_pairs",
-    )(keep, sent)
+    )(keep, sent, *extras)
 
 
 def trade_kernel(to_rows, value_ref, out_ref, sems, local_sems):
@@ -911,19 +924,22 @@
     in_shard = lax.psum_scatter(in_term, "fsdp", scatter_dimension=0, tiled=True)
 
     grad_attn_out = whole_rows(grad_hidden.astype(BF16))
+    out_term = rows_product(head_outputs, grad_attn_out).astype(BF16)
+    grad_attn_out, down_shard, out_term = lax.optimization_barrier(
+        (grad_attn_out, down_shard, out_term)
+    )
     grad_heads = times_transpose(grad_attn_out, out_weight).astype(BF16)
-    grad_heads, down_shard = lax.optimization_barrier((grad_heads, down_shard))
+    out_parts = [part_of(out_term, seq_at ^ at, out_rows, 0) for at in range(seqs)]
+    out_near = scatter_near(out_parts)
     grad_query_proj, pair_keep, pair_sent = attend_back(
         first_pos, core, queries, grad_heads, key_rows, value_rows, log_total,
         jnp.concatenate([cosine, cosine], axis=1), jnp.concatenate([sine, -sine], axis=1),
     )
     pair_sent, down_near = lax.optimization_barrier((pair_sent, gather_near(down_shard)))
-    out_term = rows_product(after(head_outputs, pair_sent), grad_attn_out).astype(BF16)
-    out_parts = [part_of(out_term, seq_at ^ at, out_rows, 0) for at in range(seqs)]
-    out_near = scatter_near(out_parts)
     count = seqs * half
-    activation = after(activation, out_term)
+    activation = after(activation, pair_sent)
     ffn_other = jnp.dot(activation[count:], down_weight, preferred_element_type=F32)
+    ffn_other, out_near = lax.optimization_barrier((ffn_other, out_near))
     ffn_part = jnp.dot(
         after(activation[:count], ffn_other), down_weight, preferred_element_type=F32
     )
@@ -931,8 +947,15 @@
     ffn_cores = [ffn_part[j * half : (j + 1) * half] for j in range(seqs)]
     ffn_near = scatter_near(ffn_cores)
     pair_keep, pair_sent, _ = lax.optimization_barrier((pair_keep, pair_sent, ffn_part))
+    out_sum, out_far = scatter_far(out_parts, out_near, not square)
     if square:
-        own_total = return_pairs(pair_keep, pair_sent, rows, shards, 1 + 6)
+        down_cut = down_shard.shape[0] // 2
+        extras = [*out_far, down_near[1][:down_cut], down_near[0][down_cut:]]
+        own_total, out_top, out_low, down_top, down_low = return_pairs(
+            pair_keep, pair_sent, extras, (2, 1, 1, 2), rows, shards, 7
+        )
+        out_far = [out_top, out_low]
+        down_parts = [down_shard, *down_near, jnp.concatenate([down_top, down_low], axis=0)]
     else:
         pair_grads = pair_keep + swap(pair_sent).astype(F32)
         own_total = pair_grads[shards * rows :]
@@ -946,14 +969,10 @@
             own_total = own_total + jnp.where(shard_at >= at, 0.0, piece)
             earlier_total = earlier_total + jnp.where(shard_at >= at, piece, 0.0)
         own_total = own_total + seq_shift(earlier_total.astype(BF16), -1).astype(F32)
-    own_total, out_near, ffn_near, down_near = lax.optimization_barrier(
-        (own_total, out_near, ffn_near, down_near)
-    )
-    out_sum, out_far = scatter_far(out_parts, out_near)
+        down_parts = gather_far(down_shard, down_near)
+    own_total, ffn_near = lax.optimization_barrier((own_total, ffn_near))
     grad_pair = jnp.where(first, rotate(own_total, cosine, -sine), own_total).astype(BF16)
-    grad_pair, in_shard, out_far, down_parts = lax.optimization_barrier(
-        (grad_pair, in_shard, out_far, gather_far(down_shard, down_near))
-    )
+    grad_pair, in_shard = lax.optimization_barrier((grad_pair, in_shard))
     grad_proj = jnp.concatenate([grad_query_proj, grad_pair], axis=1)
     if square:
         grad_rows = trade(grad_proj, True, 6)
@@ -985,7 +1004,10 @@
     grad_unit_one = my_half(unit_part) + swap(other_half(unit_part))
     layer_half = (hidden_in + scatter_end(ffn_sum, ffn_far)).astype(BF16)
     grad_half = grad_hidden + norm_pull(source, inverse_one, grad_unit_one * gains[0])
-    in_parts, grad_half = lax.optimization_barrier((in_parts, grad_half))
+    in_parts, grad_half, last_near = lax.optimization_barrier(
+        (in_parts, grad_half, gather_near(last_sum))
+    )
+    last_parts = gather_far(last_sum, last_near)
     layer_out, grad_input = whole_rows(layer_half), whole_rows(grad_half)
     if kernels and square:
         gate_grad, up_grad, gain_two_half = join_columns(seq_at, in_parts, w_gate, w_up)
@@ -1008,7 +1030,7 @@
             gate_grad * w_gate.astype(F32) + up_grad * w_up.astype(F32), axis=1
         )
     gain_two_half = gain_two_half / gain_two[:, 0]
-    last_parts = gather_far(last_sum, after(gather_near(last_sum), gate_grad))
+    last_parts = after(last_parts, gate_grad)
     out_grad = order_rows([piece[:, proj_cols:].T for piece in last_parts])
     proj_grad = jnp.concatenate(
         order_cols([piece[:, :proj_cols] for piece in last_parts]), axis=1

time: 940 us -> 930 us (0.989)
  waiting for transfers between devices: 158 us -> 141 us
  other arithmetic: 68.8 us -> 79.1 us
    ppermute x32 -> x28, waiting for transfers between devices: 107 us -> 88.2 us  [exchange(): return lax.ppermute(value, 'seq', [(at, at ^ step) for at in range(count)])]
    convert_element_type x0 -> x1, other arithmetic: none -> 9.62 us  [local(): (ffn_part + swap(ffn_other.astype(BF16)).astype(F32)).astype(BF16)]
    ppermute x32 -> x28, starting transfers between devices: 27.6 us -> 24.2 us  [exchange(): return lax.ppermute(value, 'seq', [(at, at ^ step) for at in range(count)])]
    unnamed x145 -> x148, local copies, waits for them, and re-layouts: 57.5 us -> 54.4 us
  transfers between devices with their start and end apart: 58 -> 54, of which waited for: 23 -> 17; matrix products, arithmetic and copies ran while one was open for 26% -> 28% of each run, Pallas kernels for 43% -> 42%
where the time goes in v5:
time: 930 us; the launch traced here: 919 us
  Pallas kernels  411 us (44%)
  waiting for transfers between devices  141 us (15%)
  local copies, waits for them, and re-layouts  123 us (13%)
  matrix products  93.1 us (10%)
  other arithmetic  79.1 us (9%)
  starting transfers between devices  57.3 us (6%)
  between operations  15.7 us (2%)
    pallas_call x2, Pallas kernels, gather_rows(): pl.pallas_call(rows_kernel, out_shape=jax.ShapeDtypeStruct((8 * half, wid...  102 us
    ppermute x28, waiting for transfers between devices, exchange(): return lax.ppermute(value, 'seq', [(at, at ^ step) for at in range(count)])  88.2 us
    dot_general x4, matrix products, rows_product(): lax.dot_general(left, right, (((0,), (0,)), ((), ())), preferred_element_...  58.2 us
    pallas_call x1, Pallas kernels, return_pairs(): pl.pallas_call(functools.partial(return_kernel, steps), out_shape=[jax.Sh...  58.1 us
    pallas_call x2, Pallas kernels, trade(): pl.pallas_call(functools.partial(trade_kernel, to_rows), out_shape=jax.Sh...  55 us
    unnamed x148, local copies, waits for them, and re-layouts  54.4 us
    pallas_call x1, Pallas kernels, scatter_rows(): pl.pallas_call(sum_kernel, out_shape=jax.ShapeDtypeStruct((half, width),...  50.3 us
    pallas_call x1, Pallas kernels, ffn_back(): pl.pallas_call(ffn_back_kernel, out_shape=(jax.ShapeDtypeStruct((count, 2...  43.3 us
  transfers between devices with their start and end apart: 54, of which 17 were waited for; matrix products, arithmetic and copies ran while one was open for 28% of the time, Pallas kernels for 42%

profile of v5, /device:TPU:9, one launch (start us, length us, event | category | flops | bytes accessed | tf_op | source)
XLA Modules:
  0.0 919.4 jit_solution(15022268433455398501)
XLA Ops:
  32.7 51.9 %gather_rows.2 = bf16[2048,2560]{1,0:T(8,128)(2,1)} custom-call(bf16[256,2560]{1,0:T(8,128)(2,1)} %fusion.3.own_ref), custom_call_target="tpu_custom_call" | custom-call | flops 1000 | bytes 1000 | tf_op jit(solution)/shard_map/gather_rows/pallas_call | solution.py:178
  105.3 34.1 %trade.2 = bf16[512,1536]{1,0:T(8,128)(2,1)} custom-call(bf16[2048,384]{1,0:T(8,128)(2,1)} %copy.33.value_ref), custom_call_target="tpu_custom_call" | custom-call | flops 1000 | bytes 1000 | tf_op jit(solution)/shard_map/trade/pallas_call | solution.py:318
  169.3 15.2 %collective-permute-done.5 = bf16[512,256]{1,0:T(8,128)(2,1)} collective-permute-done((bf16[512,256]{1,0:T(8,128)(2,1)}, bf16[512,256]{1,0:T(8,128)(2,1)}, u32[]{:S(2)}, u32[]{:S(2)}) %collective-permute-start.5) | collective-permute-done | bytes 262176 | tf_op jit(solution)/shard_map/ppermute | solution.py:870
  185.5 16.8 %collective-permute-done.6 = bf16[512,256]{1,0:T(8,128)(2,1)} collective-permute-done((bf16[512,256]{1,0:T(8,128)(2,1)}, bf16[512,256]{1,0:T(8,128)(2,1)}, u32[]{:S(2)}, u32[]{:S(2)}) %collective-permute-start.6) | collective-permute-done | bytes 262176 | tf_op jit(solution)/shard_map/ppermute | solution.py:870
  205.6 8.6 collective-permute-start.11
  222.9 15.4 %attend.1 = (bf16[512,1280]{1,0:T(8,128)(2,1)S(1)}, f32[5,1,512]{2,1,0:T(1,128)S(1)}) custom-call(s32[1]{0:T(128)} %bitcast.pos_ref, bf16[512,1280]{1,0:T(8,128)(2,1)S(1)} %slice.194.q_ref, bf16[2560,256]{1,0:T(8,128)(2,1)S(1)} %get-tuple-element.194.k_ref, bf16[2560,256]{1,0:T(8,128)(2,1)S(1)} %get-tuple-element.193.v_ref), custom_call_target="tpu_custom_call" | custom-call | flops 1000 | bytes 1000 | tf_op jit(solution)/shard_map/attend/pallas_call | solution.py:485
  280.8 50.1 %gather_rows.3.x_ref = bf16[2048,2560]{1,0:T(8,128)(2,1)} custom-call(bf16[256,2560]{1,0:T(8,128)(2,1)} %multiply_convert_fusion.own_ref), custom_call_target="tpu_custom_call" | custom-call | flops 1000 | bytes 1000 | tf_op jit(solution)/shard_map/gather_rows/pallas_call | solution.py:178
  330.9 32.8 %ffn.1 = (bf16[2048,960]{1,0:T(8,128)(2,1)}, bf16[2048,960]{1,0:T(8,128)(2,1)}, bf16[2048,960]{1,0:T(8,128)(2,1)}) custom-call(bf16[2048,2560]{1,0:T(8,128)(2,1)} %gather_rows.3.x_ref, bf16[2560,1920]{1,0:T(8,128)(2,1)} %all-gather.9.cloned.1.call-done.w_ref), custom_call_target="tpu_custom_call" | custom-call | flops 1000 | bytes 1000 | tf_op jit(solution)/shard_map/ffn/pallas_call | solution.py:639
  363.8 15.9 %convolution_convert_fusion.2 = bf16[2560,960]{0,1:T(8,128)(2,1)} fusion(bf16[2048,2560]{1,0:T(8,128)(2,1)} %constant_dynamic-update-slice_fusion.5.c_ref, bf16[2048,960]{1,0:T(8,128)(2,1)} %get-tuple-element.112), kind=kOutput, calls=%fused_computation.3 | convolution fusion | flops 10068787200 | bytes 19333120 | tf_op jit(solution)/shard_map/dot_general | solution.py:80
  389.1 43.3 %ffn_back.1 = (bf16[2048,1920]{1,0:T(8,128)(2,1)}, bf16[2048,2560]{1,0:T(8,128)(2,1)}) custom-call(bf16[2048,2560]{1,0:T(8,128)(2,1)} %constant_dynamic-update-slice_fusion.5.c_ref, bf16[960,2560]{1,0:T(8,128)(2,1)} %all-gather.11.cloned.1.call-done.d_ref, bf16[2048,960]{1,0:T(8,128)(2,1)} %get-tuple-element.98.a_ref, ...), custom_call_target="tpu_custom_call" | custom-call | flops 1000 | bytes 1000 | tf_op jit(solution)/shard_map/ffn_back/pallas_call | solution.py:673
  436.9 28.0 %convolution_convert_fusion = bf16[2560,1920]{1,0:T(8,128)(2,1)} fusion(bf16[2048,2560]{1,0:T(8,128)(2,1)} %gather_rows.3.x_ref, bf16[2048,1920]{1,0:T(8,128)(2,1)} %get-tuple-element.105), kind=kOutput, calls=%fused_computation | convolution fusion | flops 20137574400 | bytes 28180480 | tf_op jit(solution)/shard_map/dot_general | solution.py:80
  472.0 50.3 %scatter_rows.1 = f32[256,2560]{1,0:T(8,128)S(1)} custom-call(bf16[2048,2560]{1,0:T(8,128)(2,1)S(1)} %copy-done.7), custom_call_target="tpu_custom_call" | custom-call | flops 1000 | bytes 1000 | tf_op jit(solution)/shard_map/scatter_rows/pallas_call | solution.py:409
  556.2 26.3 %attend_back.1 = (bf16[512,1280]{1,0:T(8,128)(2,1)S(1)}, f32[2560,256]{1,0:T(8,128)}, bf16[2560,256]{1,0:T(8,128)(2,1)S(1)}) custom-call(s32[2]{0:T(128)S(1)} %pad_add_fusion.pos_ref, bf16[512,1280]{1,0:T(8,128)(2,1)S(1)} %copy-done.4, bf16[512,1280]{1,0:T(8,128)(2,1)S(1)} %convolution_convert_fusion.4.g_ref, bf16[2560,256]{1,0:T(8,128)(2,1)} %copy-done.6, ...), custom_call_target="tpu_custom_call" | custom-call | flops 1000 | bytes 1000 | tf_op jit(solution)/shard_map/attend_back/pallas_call | solution.py:577
  590.9 15.3 %collective-permute-done.28 = bf16[320,2560]{1,0:T(8,128)(2,1)} collective-permute-done((bf16[320,2560]{1,0:T(8,128)(2,1)}, bf16[320,2560]{1,0:T(8,128)(2,1)}, u32[]{:S(2)}, u32[]{:S(2)}) %collective-permute-start.28) | collective-permute-done | bytes 1638432 | tf_op jit(solution)/shard_map/ppermute | solution.py:18
  607.6 8.5 fusion.28
  616.2 9.6 %add_convert_fusion = bf16[1024,2560]{1,0:T(8,128)(2,1)} fusion(f32[1024,2560]{1,0:T(8,128)} %fusion.28, bf16[1024,2560]{1,0:T(8,128)(2,1)} %collective-permute-done.29), kind=kLoop, calls=%fused_computation.2 | loop fusion | flops 7864320 | bytes 20971520 | tf_op jit(solution)/shard_map/convert_element_type | solution.py:946
  639.5 58.1 %return_pairs.1 = (f32[512,256]{1,0:T(8,128)S(1)}, bf16[160,2560]{1,0:T(8,128)(2,1)S(1)}, bf16[160,2560]{1,0:T(8,128)(2,1)S(1)}, bf16[480,640]{1,0:T(8,128)(2,1)S(1)}, bf16[480,640]{1,0:T(8,128)(2,1)S(1)}) custom-call(f32[2560,256]{1,0:T(8,128)S(1)} %copy-done.11, bf16[2560,256]{1,0:T(8,128)(2,1)S(1)} %copy-done.14, ...), custom_call_target="tpu_custom_call" | custom-call | flops 1000 | bytes 1000 | tf_op jit(solution)/shard_map/return_pairs/pallas_call | solution.py:269
  706.0 20.8 %trade.3 = bf16[2048,384]{1,0:T(8,128)(2,1)} custom-call(bf16[512,1536]{1,0:T(8,128)(2,1)} %constant_dynamic-update-slice_fusion.13.value_ref.grad_ref), custom_call_target="tpu_custom_call" | custom-call | flops 1000 | bytes 1000 | tf_op jit(solution)/shard_map/trade/pallas_call | solution.py:318
  726.9 8.8 convolution_convert_fusion.3
  754.1 10.2 %unit_grads.1 = f32[512,2560]{1,0:T(8,128)} custom-call(s32[1]{0:T(128)} %bitcast.19.seq_ref, bf16[512,1536]{1,0:T(8,128)(2,1)S(1)} %copy-done.2, bf16[2560,384]{1,0:T(8,128)(2,1)S(1)} %copy-done.12, bf16[2560,384]{1,0:T(8,128)(2,1)S(1)} %copy-done.10, bf16[2560,384]{1,0:T(8,128)(2,1)} %collective-permute-done.21.refs_2_, bf16[2560,384]{1,0:T(8,128)(2,1)S(1)} %copy-done.8), custom_call_target="tpu_custom_call" | custom-call | flops 1000 | bytes 1000 | tf_op jit(solution)/shard_map/unit_grads/pallas_call | solution.py:206
  769.6 20.9 %collective-permute-done.35.refs_1_ = bf16[640,1920]{1,0:T(8,128)(2,1)} collective-permute-done((bf16[640,1920]{1,0:T(8,128)(2,1)}, bf16[640,1920]{1,0:T(8,128)(2,1)}, u32[]{:S(2)}, u32[]{:S(2)}) %collective-permute-start.35) | collective-permute-done | bytes 2457632 | tf_op jit(solution)/shard_map/ppermute | solution.py:18
  825.2 12.1 %collective-permute-done.37 = bf16[320,1920]{1,0:T(8,128)(2,1)} collective-permute-done((bf16[320,1920]{1,0:T(8,128)(2,1)}, bf16[320,1920]{1,0:T(8,128)(2,1)}, u32[]{:S(2)}, u32[]{:S(2)}) %collective-permute-start.37) | collective-permute-done | bytes 1228832 | tf_op jit(solution)/shard_map/ppermute | solution.py:18
  839.2 17.5 %collective-permute-done.40 = bf16[640,704]{0,1:T(8,128)(2,1)} collective-permute-done((bf16[640,704]{0,1:T(8,128)(2,1)S(1)}, bf16[640,704]{0,1:T(8,128)(2,1)}, u32[]{:S(2)}, u32[]{:S(2)}) %collective-permute-start.40) | collective-permute-done | bytes 901152 | tf_op jit(solution)/shard_map/ppermute | solution.py:18
  869.2 17.4 %join_columns.1 = (f32[640,3840]{1,0:T(8,128)}, f32[640,3840]{1,0:T(8,128)}, f32[640,1]{1,0:T(8,128)S(1)}) custom-call(s32[1]{0:T(128)} %bitcast.19.seq_ref, bf16[640,1920]{1,0:T(8,128)(2,1)} %reduce-scatter.8.cloned.1.call-done.refs_0_, bf16[640,1920]{1,0:T(8,128)(2,1)} %collective-permute-done.35.refs_1_, ...), custom_call_target="tpu_custom_call" | custom-call | flops 1000 | bytes 1000 | tf_op jit(solution)/shard_map/join_columns/pallas_call | solution.py:719
  (398 shorter events, 315.7 us)
Async XLA Ops:
  7.2 77.5 %all-gather.7.cloned.1.call-start = ((), (), s32[]{:S(2)}) async-start(), calls=%async_computation.4 | async-start | bytes 2048000 | tf_op jit(solution)/shard_map/all_gather | solution.py:827
  9.4 83.4 %all-gather.5.cloned.1.call-start = ((), (), s32[]{:S(2)}) async-start(), calls=%async_computation.3 | async-start | bytes 2457600 | tf_op jit(solution)/shard_map/all_gather | solution.py:808
  12.2 318.7 %all-gather.9.cloned.1.call-start = ((), (), s32[]{:S(2)}) async-start(), calls=%async_computation.5 | async-start | bytes 12288000 | tf_op jit(solution)/shard_map/all_gather | solution.py:818
  22.9 366.2 %all-gather.11.cloned.1.call-start = ((), (), s32[]{:S(2)}) async-start(), calls=%async_computation.6 | async-start | bytes 6144000 | tf_op jit(solution)/shard_map/all_gather | solution.py:819
  84.7 65.4 %collective-permute-start.7 = (bf16[320,2560]{1,0:T(8,128)(2,1)}, bf16[320,2560]{1,0:T(8,128)(2,1)}, u32[]{:S(2)}, u32[]{:S(2)}) collective-permute-start(bf16[320,2560]{1,0:T(8,128)(2,1)} %all-gather.7.cloned.1.call-done), channel_id=1, source_target_pairs={{0,8},{8,0},{16,24},{24,16},{1,9},{9,1},{17,25},{25,17},{2,10},{10... | collective-permute-start | bytes 4915208 | tf_op jit(solution)/shard_map/ppermute | solution.py:18
  84.8 70.6 %collective-permute-start.8 = (bf16[320,2560]{1,0:T(8,128)(2,1)}, bf16[320,2560]{1,0:T(8,128)(2,1)}, u32[]{:S(2)}, u32[]{:S(2)}) collective-permute-start(bf16[320,2560]{1,0:T(8,128)(2,1)} %all-gather.7.cloned.1.call-done), channel_id=1, source_target_pairs={{0,16},{8,24},{16,0},{24,8},{1,17},{9,25},{17,1},{25,9},{2,18},{10... | collective-permute-start | bytes 4915208 | tf_op jit(solution)/shard_map/ppermute | solution.py:18
  152.2 52.1 %collective-permute-start.10 = (bf16[160,2560]{1,0:T(8,128)(2,1)}, bf16[160,2560]{1,0:T(8,128)(2,1)S(1)}, u32[]{:S(2)}, u32[]{:S(2)}) collective-permute-start(bf16[160,2560]{1,0:T(8,128)(2,1)} %slice.255), channel_id=1, source_target_pairs={{0,16},{8,24},{16,0},{24,8},{1,17},{9,25},{17,1},{25,9},{2,18},{10... | collective-permute-start | bytes 2457608 | tf_op jit(solution)/shard_map/ppermute | solution.py:18
  157.4 46.9 %collective-permute-start.9 = (bf16[160,2560]{1,0:T(8,128)(2,1)}, bf16[160,2560]{1,0:T(8,128)(2,1)}, u32[]{:S(2)}, u32[]{:S(2)}) collective-permute-start(bf16[160,2560]{1,0:T(8,128)(2,1)} %slice.254), channel_id=1, source_target_pairs={{0,8},{8,0},{16,24},{24,16},{1,9},{9,1},{17,25},{25,17},{2,10},{10... | collective-permute-start | bytes 2457608 | tf_op jit(solution)/shard_map/ppermute | solution.py:18
  158.3 44.0 %collective-permute-start.6 = (bf16[512,256]{1,0:T(8,128)(2,1)}, bf16[512,256]{1,0:T(8,128)(2,1)}, u32[]{:S(2)}, u32[]{:S(2)}) collective-permute-start(bf16[512,256]{1,0:T(8,128)(2,1)} %get-tuple-element.199), channel_id=1, source_target_pairs={{0,2},{2,4},{4,6},{6,0},{1,3},{3,5},{5,7},{7,1},{8,10},{10,12},{12... | collective-permute-start | bytes 786440 | tf_op jit(solution)/shard_map/ppermute | solution.py:870
  162.5 376.7 %reduce-scatter.10.cloned.1.call-start = ((), (), s32[]{:S(2)}) async-start(), calls=%async_computation.8 | async-start | bytes 6553600
  387.5 314.8 %reduce-scatter.8.cloned.1.call-start = ((), (), s32[]{:S(2)}) async-start(), calls=%async_computation.7 | async-start | bytes 12288000 | tf_op jit(solution)/shard_map/reduce_scatter | solution.py:924
  387.5 44.8 %collective-permute-start.20 = (bf16[2560,384]{1,0:T(8,128)(2,1)}, bf16[2560,384]{1,0:T(8,128)(2,1)S(1)}, u32[]{:S(2)}, u32[]{:S(2)}) collective-permute-start(bf16[2560,384]{1,0:T(8,128)(2,1)} %all-gather.5.cloned.1.call-done.refs_0_), channel_id=1, source_target_pairs={{0,8},{8,0},{16,24},{24,16},{1,9},{9,1},{17,25},{25,17},{2,10},{10... | collective-permute-start | bytes 5898248 | tf_op jit(solution)/shard_map/ppermute | solution.py:18
  388.7 44.3 %collective-permute-start.21 = (bf16[2560,384]{1,0:T(8,128)(2,1)}, bf16[2560,384]{1,0:T(8,128)(2,1)}, u32[]{:S(2)}, u32[]{:S(2)}) collective-permute-start(bf16[2560,384]{1,0:T(8,128)(2,1)} %all-gather.5.cloned.1.call-done.refs_0_), channel_id=1, source_target_pairs={{0,16},{8,24},{16,0},{24,8},{1,17},{9,25},{17,1},{25,9},{2,18},{10... | collective-permute-start | bytes 5898248 | tf_op jit(solution)/shard_map/ppermute | solution.py:18
  467.9 352.9 %reduce-scatter.12.cloned.1.call-start = ((), (), s32[]{:S(2)}) async-start(), calls=%async_computation.9 | async-start | bytes 4915200
  541.7 40.8 %collective-permute-start.25 = (bf16[960,640]{1,0:T(8,128)(2,1)}, bf16[960,640]{1,0:T(8,128)(2,1)}, u32[]{:S(2)}, u32[]{:S(2)}) collective-permute-start(bf16[960,640]{1,0:T(8,128)(2,1)} %bitcast.79), channel_id=1, source_target_pairs={{0,8},{8,0},{16,24},{24,16},{1,9},{9,1},{17,25},{25,17},{2,10},{10... | collective-permute-start | bytes 3686408 | tf_op jit(solution)/shard_map/ppermute | solution.py:18
  542.6 39.9 %collective-permute-start.26 = (bf16[960,640]{1,0:T(8,128)(2,1)}, bf16[960,640]{1,0:T(8,128)(2,1)}, u32[]{:S(2)}, u32[]{:S(2)}) collective-permute-start(bf16[960,640]{1,0:T(8,128)(2,1)} %bitcast.80), channel_id=1, source_target_pairs={{0,16},{8,24},{16,0},{24,8},{1,17},{9,25},{17,1},{25,9},{2,18},{10... | collective-permute-start | bytes 3686408 | tf_op jit(solution)/shard_map/ppermute | solution.py:18
  546.6 59.5 %collective-permute-start.28 = (bf16[320,2560]{1,0:T(8,128)(2,1)}, bf16[320,2560]{1,0:T(8,128)(2,1)}, u32[]{:S(2)}, u32[]{:S(2)}) collective-permute-start(bf16[320,2560]{1,0:T(8,128)(2,1)} %pad_maximum_fusion.7), channel_id=1, source_target_pairs={{0,16},{8,24},{16,0},{24,8},{1,17},{9,25},{17,1},{25,9},{2,18},{10... | collective-permute-start | bytes 4915208 | tf_op jit(solution)/shard_map/ppermute | solution.py:18
  548.8 57.3 %collective-permute-start.27 = (bf16[320,2560]{1,0:T(8,128)(2,1)}, bf16[320,2560]{1,0:T(8,128)(2,1)S(1)}, u32[]{:S(2)}, u32[]{:S(2)}) collective-permute-start(bf16[320,2560]{1,0:T(8,128)(2,1)} %pad_maximum_fusion.6), channel_id=1, source_target_pairs={{0,8},{8,0},{16,24},{24,16},{1,9},{9,1},{17,25},{25,17},{2,10},{10... | collective-permute-start | bytes 4915208 | tf_op jit(solution)/shard_map/ppermute | solution.py:18
  628.8 71.3 %collective-permute-start.31 = (bf16[256,2560]{1,0:T(8,128)(2,1)}, bf16[256,2560]{1,0:T(8,128)(2,1)}, u32[]{:S(2)}, u32[]{:S(2)}) collective-permute-start(bf16[256,2560]{1,0:T(8,128)(2,1)} %pad_maximum_fusion.11), channel_id=1, source_target_pairs={{0,16},{8,24},{16,0},{24,8},{1,17},{9,25},{17,1},{25,9},{2,18},{10... | collective-permute-start | bytes 3932168 | tf_op jit(solution)/shard_map/ppermute | solution.py:18
  630.6 69.5 %collective-permute-start.30 = (bf16[256,2560]{1,0:T(8,128)(2,1)}, bf16[256,2560]{1,0:T(8,128)(2,1)}, u32[]{:S(2)}, u32[]{:S(2)}) collective-permute-start(bf16[256,2560]{1,0:T(8,128)(2,1)} %pad_maximum_fusion.10), channel_id=1, source_target_pairs={{0,8},{8,0},{16,24},{24,16},{1,9},{9,1},{17,25},{25,17},{2,10},{10... | collective-permute-start | bytes 3932168 | tf_op jit(solution)/shard_map/ppermute | solution.py:18
  735.7 54.8 %collective-permute-start.35 = (bf16[640,1920]{1,0:T(8,128)(2,1)}, bf16[640,1920]{1,0:T(8,128)(2,1)}, u32[]{:S(2)}, u32[]{:S(2)}) collective-permute-start(bf16[640,1920]{1,0:T(8,128)(2,1)} %reduce-scatter.8.cloned.1.call-done.refs_0_), channel_id=1, source_target_pairs={{0,8},{8,0},{16,24},{24,16},{1,9},{9,1},{17,25},{25,17},{2,10},{10... | collective-permute-start | bytes 7372808 | tf_op jit(solution)/shard_map/ppermute | solution.py:18
  735.8 54.7 %collective-permute-start.36 = (bf16[640,1920]{1,0:T(8,128)(2,1)}, bf16[640,1920]{1,0:T(8,128)(2,1)}, u32[]{:S(2)}, u32[]{:S(2)}) collective-permute-start(bf16[640,1920]{1,0:T(8,128)(2,1)} %reduce-scatter.8.cloned.1.call-done.refs_0_), channel_id=1, source_target_pairs={{0,16},{8,24},{16,0},{24,8},{1,17},{9,25},{17,1},{25,9},{2,18},{10... | collective-permute-start | bytes 7372808 | tf_op jit(solution)/shard_map/ppermute | solution.py:18
  801.2 36.2 %collective-permute-start.37 = (bf16[320,1920]{1,0:T(8,128)(2,1)}, bf16[320,1920]{1,0:T(8,128)(2,1)}, u32[]{:S(2)}, u32[]{:S(2)}) collective-permute-start(bf16[320,1920]{1,0:T(8,128)(2,1)} %slice.233), channel_id=1, source_target_pairs={{0,8},{8,0},{16,24},{24,16},{1,9},{9,1},{17,25},{25,17},{2,10},{10... | collective-permute-start | bytes 3686408 | tf_op jit(solution)/shard_map/ppermute | solution.py:18
  815.8 49.0 %collective-permute-start.34 = (bf16[256,2560]{1,0:T(8,128)(2,1)}, bf16[256,2560]{1,0:T(8,128)(2,1)}, u32[]{:S(2)}, u32[]{:S(2)}) collective-permute-start(bf16[256,2560]{1,0:T(8,128)(2,1)} %get-tuple-element.192), channel_id=1, source_target_pairs={{0,1},{1,0},{2,3},{3,2},{4,5},{5,4},{6,7},{7,6},{8,9},{9,8},{10,11... | collective-permute-start | bytes 3932168 | tf_op jit(solution)/shard_map/ppermute | solution.py:22
  (97 other events, 1355.2 us)
Sparse Core Ops, SparseCore 0:
  10.2 38.4 all-gather.6
  50.8 41.9 all-gather.4
  95.0 191.8 all-gather.8
  288.8 92.2 all-gather.10
  387.6 93.3 reduce-scatter.9
  483.8 174.2 reduce-scatter.7
  747.3 73.4 reduce-scatter.11

commit v6 on v5

--- a/solution.py
+++ b/solution.py
@@ -943,7 +943,10 @@
     ffn_part = jnp.dot(
         after(activation[:count], ffn_other), down_weight, preferred_element_type=F32
     )
-    ffn_part = (ffn_part + swap(ffn_other.astype(BF16)).astype(F32)).astype(BF16)
+    ffn_part, ffn_other = lax.optimization_barrier(
+        (ffn_part.astype(BF16), swap(ffn_other.astype(BF16)))
+    )
+    ffn_part = (ffn_part.astype(F32) + ffn_other.astype(F32)).astype(BF16)
     ffn_cores = [ffn_part[j * half : (j + 1) * half] for j in range(seqs)]
     ffn_near = scatter_near(ffn_cores)
     pair_keep, pair_sent, _ = lax.optimization_barrier((pair_keep, pair_sent, ffn_part))

time: 930 us -> 924 us (level)
    unnamed x148 -> x152, local copies, waits for them, and re-layouts: 54.4 us -> 56.6 us
  transfers between devices with their start and end apart: 54 -> 54, of which waited for: 17 -> 18; matrix products, arithmetic and copies ran while one was open for 28% -> 27% of each run, Pallas kernels for 42% -> 42%
where the time goes in v6:
time: 924 us; the launch traced here: 913 us
  Pallas kernels  408 us (44%)
  waiting for transfers between devices  141 us (15%)
  local copies, waits for them, and re-layouts  125 us (14%)
  matrix products  92.2 us (10%)
  other arithmetic  73.4 us (8%)
  starting transfers between devices  57.4 us (6%)
  between operations  15.8 us (2%)
    pallas_call x2, Pallas kernels, gather_rows(): pl.pallas_call(rows_kernel, out_shape=jax.ShapeDtypeStruct((8 * half, wid...  102 us
    ppermute x28, waiting for transfers between devices, exchange(): return lax.ppermute(value, 'seq', [(at, at ^ step) for at in range(count)])  88 us
    dot_general x4, matrix products, rows_product(): lax.dot_general(left, right, (((0,), (0,)), ((), ())), preferred_element_...  58.2 us
    unnamed x152, local copies, waits for them, and re-layouts  56.6 us
    pallas_call x1, Pallas kernels, return_pairs(): pl.pallas_call(functools.partial(return_kernel, steps), out_shape=[jax.Sh...  55.5 us
    pallas_call x2, Pallas kernels, trade(): pl.pallas_call(functools.partial(trade_kernel, to_rows), out_shape=jax.Sh...  55 us
    pallas_call x1, Pallas kernels, scatter_rows(): pl.pallas_call(sum_kernel, out_shape=jax.ShapeDtypeStruct((half, width),...  50.3 us
    pallas_call x1, Pallas kernels, ffn_back(): pl.pallas_call(ffn_back_kernel, out_shape=(jax.ShapeDtypeStruct((count, 2...  43.2 us
  transfers between devices with their start and end apart: 54, of which 18 were waited for; matrix products, arithmetic and copies ran while one was open for 27% of the time, Pallas kernels for 42%

profile of v6, /device:TPU:9, one launch (start us, length us, event | category | flops | bytes accessed | tf_op | source)
XLA Modules:
  0.0 913.1 jit_solution(12645684015543148424)
XLA Ops:
  32.7 51.9 %gather_rows.2 = bf16[2048,2560]{1,0:T(8,128)(2,1)} custom-call(bf16[256,2560]{1,0:T(8,128)(2,1)} %fusion.3.own_ref), custom_call_target="tpu_custom_call" | custom-call | flops 1000 | bytes 1000 | tf_op jit(solution)/shard_map/gather_rows/pallas_call | solution.py:178
  105.3 34.2 %trade.2 = bf16[512,1536]{1,0:T(8,128)(2,1)} custom-call(bf16[2048,384]{1,0:T(8,128)(2,1)} %copy.33.value_ref), custom_call_target="tpu_custom_call" | custom-call | flops 1000 | bytes 1000 | tf_op jit(solution)/shard_map/trade/pallas_call | solution.py:318
  169.3 15.2 %collective-permute-done.5 = bf16[512,256]{1,0:T(8,128)(2,1)} collective-permute-done((bf16[512,256]{1,0:T(8,128)(2,1)}, bf16[512,256]{1,0:T(8,128)(2,1)}, u32[]{:S(2)}, u32[]{:S(2)}) %collective-permute-start.5) | collective-permute-done | bytes 262176 | tf_op jit(solution)/shard_map/ppermute | solution.py:870
  185.5 16.8 %collective-permute-done.6 = bf16[512,256]{1,0:T(8,128)(2,1)} collective-permute-done((bf16[512,256]{1,0:T(8,128)(2,1)}, bf16[512,256]{1,0:T(8,128)(2,1)}, u32[]{:S(2)}, u32[]{:S(2)}) %collective-permute-start.6) | collective-permute-done | bytes 262176 | tf_op jit(solution)/shard_map/ppermute | solution.py:870
  205.6 8.6 collective-permute-start.11
  222.9 15.4 %attend.1 = (bf16[512,1280]{1,0:T(8,128)(2,1)S(1)}, f32[5,1,512]{2,1,0:T(1,128)S(1)}) custom-call(s32[1]{0:T(128)} %bitcast.pos_ref, bf16[512,1280]{1,0:T(8,128)(2,1)S(1)} %slice.194.q_ref, bf16[2560,256]{1,0:T(8,128)(2,1)S(1)} %get-tuple-element.198.k_ref, bf16[2560,256]{1,0:T(8,128)(2,1)S(1)} %get-tuple-element.197.v_ref), custom_call_target="tpu_custom_call" | custom-call | flops 1000 | bytes 1000 | tf_op jit(solution)/shard_map/attend/pallas_call | solution.py:485
  280.8 50.1 %gather_rows.3.x_ref = bf16[2048,2560]{1,0:T(8,128)(2,1)} custom-call(bf16[256,2560]{1,0:T(8,128)(2,1)} %multiply_convert_fusion.own_ref), custom_call_target="tpu_custom_call" | custom-call | flops 1000 | bytes 1000 | tf_op jit(solution)/shard_map/gather_rows/pallas_call | solution.py:178
  330.9 32.8 %ffn.1 = (bf16[2048,960]{1,0:T(8,128)(2,1)}, bf16[2048,960]{1,0:T(8,128)(2,1)}, bf16[2048,960]{1,0:T(8,128)(2,1)}) custom-call(bf16[2048,2560]{1,0:T(8,128)(2,1)} %gather_rows.3.x_ref, bf16[2560,1920]{1,0:T(8,128)(2,1)} %all-gather.9.cloned.1.call-done.w_ref), custom_call_target="tpu_custom_call" | custom-call | flops 1000 | bytes 1000 | tf_op jit(solution)/shard_map/ffn/pallas_call | solution.py:639
  363.8 15.9 %convolution_convert_fusion.3 = bf16[2560,960]{0,1:T(8,128)(2,1)} fusion(bf16[2048,2560]{1,0:T(8,128)(2,1)} %constant_dynamic-update-slice_fusion.5.c_ref, bf16[2048,960]{1,0:T(8,128)(2,1)} %get-tuple-element.114), kind=kOutput, calls=%fused_computation.4 | convolution fusion | flops 10068787200 | bytes 19333120 | tf_op jit(solution)/shard_map/dot_general | solution.py:80
  379.6 7.8 copy.42
  389.1 43.2 %ffn_back.1 = (bf16[2048,1920]{1,0:T(8,128)(2,1)}, bf16[2048,2560]{1,0:T(8,128)(2,1)}) custom-call(bf16[2048,2560]{1,0:T(8,128)(2,1)} %constant_dynamic-update-slice_fusion.5.c_ref, bf16[960,2560]{1,0:T(8,128)(2,1)} %all-gather.11.cloned.1.call-done.d_ref, bf16[2048,960]{1,0:T(8,128)(2,1)} %get-tuple-element.100.a_ref, ...), custom_call_target="tpu_custom_call" | custom-call | flops 1000 | bytes 1000 | tf_op jit(solution)/shard_map/ffn_back/pallas_call | solution.py:673
  436.9 28.0 %convolution_convert_fusion = bf16[2560,1920]{1,0:T(8,128)(2,1)} fusion(bf16[2048,2560]{1,0:T(8,128)(2,1)} %gather_rows.3.x_ref, bf16[2048,1920]{1,0:T(8,128)(2,1)} %get-tuple-element.107), kind=kOutput, calls=%fused_computation | convolution fusion | flops 20137574400 | bytes 28180480 | tf_op jit(solution)/shard_map/dot_general | solution.py:80
  471.9 50.3 %scatter_rows.1 = f32[256,2560]{1,0:T(8,128)S(1)} custom-call(bf16[2048,2560]{1,0:T(8,128)(2,1)S(1)} %copy-done.7), custom_call_target="tpu_custom_call" | custom-call | flops 1000 | bytes 1000 | tf_op jit(solution)/shard_map/scatter_rows/pallas_call | solution.py:409
  556.1 26.3 %attend_back.1 = (bf16[512,1280]{1,0:T(8,128)(2,1)S(1)}, f32[2560,256]{1,0:T(8,128)}, bf16[2560,256]{1,0:T(8,128)(2,1)S(1)}) custom-call(s32[2]{0:T(128)S(1)} %pad_add_fusion.pos_ref, bf16[512,1280]{1,0:T(8,128)(2,1)S(1)} %copy-done.4, bf16[512,1280]{1,0:T(8,128)(2,1)S(1)} %convolution_convert_fusion.5.g_ref, bf16[2560,256]{1,0:T(8,128)(2,1)} %copy-done.6, ...), custom_call_target="tpu_custom_call" | custom-call | flops 1000 | bytes 1000 | tf_op jit(solution)/shard_map/attend_back/pallas_call | solution.py:577
  582.5 8.4 fusion.10
  590.9 15.2 %collective-permute-done.28 = bf16[320,2560]{1,0:T(8,128)(2,1)} collective-permute-done((bf16[320,2560]{1,0:T(8,128)(2,1)}, bf16[320,2560]{1,0:T(8,128)(2,1)}, u32[]{:S(2)}, u32[]{:S(2)}) %collective-permute-start.28) | collective-permute-done | bytes 1638432 | tf_op jit(solution)/shard_map/ppermute | solution.py:18
  635.7 55.5 %return_pairs.1 = (f32[512,256]{1,0:T(8,128)S(1)}, bf16[160,2560]{1,0:T(8,128)(2,1)S(1)}, bf16[160,2560]{1,0:T(8,128)(2,1)S(1)}, bf16[480,640]{1,0:T(8,128)(2,1)S(1)}, bf16[480,640]{1,0:T(8,128)(2,1)S(1)}) custom-call(f32[2560,256]{1,0:T(8,128)S(1)} %copy-done.11, bf16[2560,256]{1,0:T(8,128)(2,1)S(1)} %copy-done.14, ...), custom_call_target="tpu_custom_call" | custom-call | flops 1000 | bytes 1000 | tf_op jit(solution)/shard_map/return_pairs/pallas_call | solution.py:269
  699.7 20.8 %trade.3 = bf16[2048,384]{1,0:T(8,128)(2,1)} custom-call(bf16[512,1536]{1,0:T(8,128)(2,1)} %constant_dynamic-update-slice_fusion.13.value_ref.grad_ref), custom_call_target="tpu_custom_call" | custom-call | flops 1000 | bytes 1000 | tf_op jit(solution)/shard_map/trade/pallas_call | solution.py:318
  720.5 8.8 convolution_convert_fusion.4
  747.8 10.1 %unit_grads.1 = f32[512,2560]{1,0:T(8,128)} custom-call(s32[1]{0:T(128)} %bitcast.19.seq_ref, bf16[512,1536]{1,0:T(8,128)(2,1)S(1)} %copy-done.2, bf16[2560,384]{1,0:T(8,128)(2,1)S(1)} %copy-done.12, bf16[2560,384]{1,0:T(8,128)(2,1)S(1)} %copy-done.10, bf16[2560,384]{1,0:T(8,128)(2,1)} %collective-permute-done.21.refs_2_, bf16[2560,384]{1,0:T(8,128)(2,1)S(1)} %copy-done.8), custom_call_target="tpu_custom_call" | custom-call | flops 1000 | bytes 1000 | tf_op jit(solution)/shard_map/unit_grads/pallas_call | solution.py:206
  763.2 20.9 %collective-permute-done.35.refs_1_ = bf16[640,1920]{1,0:T(8,128)(2,1)} collective-permute-done((bf16[640,1920]{1,0:T(8,128)(2,1)}, bf16[640,1920]{1,0:T(8,128)(2,1)}, u32[]{:S(2)}, u32[]{:S(2)}) %collective-permute-start.35) | collective-permute-done | bytes 2457632 | tf_op jit(solution)/shard_map/ppermute | solution.py:18
  819.1 11.9 %collective-permute-done.37 = bf16[320,1920]{1,0:T(8,128)(2,1)} collective-permute-done((bf16[320,1920]{1,0:T(8,128)(2,1)}, bf16[320,1920]{1,0:T(8,128)(2,1)}, u32[]{:S(2)}, u32[]{:S(2)}) %collective-permute-start.37) | collective-permute-done | bytes 1228832 | tf_op jit(solution)/shard_map/ppermute | solution.py:18
  832.9 17.5 %collective-permute-done.40 = bf16[640,704]{0,1:T(8,128)(2,1)} collective-permute-done((bf16[640,704]{0,1:T(8,128)(2,1)S(1)}, bf16[640,704]{0,1:T(8,128)(2,1)}, u32[]{:S(2)}, u32[]{:S(2)}) %collective-permute-start.40) | collective-permute-done | bytes 901152 | tf_op jit(solution)/shard_map/ppermute | solution.py:18
  862.9 17.4 %join_columns.1 = (f32[640,3840]{1,0:T(8,128)}, f32[640,3840]{1,0:T(8,128)}, f32[640,1]{1,0:T(8,128)S(1)}) custom-call(s32[1]{0:T(128)} %bitcast.19.seq_ref, bf16[640,1920]{1,0:T(8,128)(2,1)} %reduce-scatter.8.cloned.1.call-done.refs_0_, bf16[640,1920]{1,0:T(8,128)(2,1)} %collective-permute-done.35.refs_1_, ...), custom_call_target="tpu_custom_call" | custom-call | flops 1000 | bytes 1000 | tf_op jit(solution)/shard_map/join_columns/pallas_call | solution.py:719
  (402 shorter events, 314.2 us)
Async XLA Ops:
  7.2 77.5 %all-gather.7.cloned.1.call-start = ((), (), s32[]{:S(2)}) async-start(), calls=%async_computation.4 | async-start | bytes 2048000 | tf_op jit(solution)/shard_map/all_gather | solution.py:827
  9.4 83.4 %all-gather.5.cloned.1.call-start = ((), (), s32[]{:S(2)}) async-start(), calls=%async_computation.3 | async-start | bytes 2457600 | tf_op jit(solution)/shard_map/all_gather | solution.py:808
  12.2 318.7 %all-gather.9.cloned.1.call-start = ((), (), s32[]{:S(2)}) async-start(), calls=%async_computation.5 | async-start | bytes 12288000 | tf_op jit(solution)/shard_map/all_gather | solution.py:818
  22.9 366.2 %all-gather.11.cloned.1.call-start = ((), (), s32[]{:S(2)}) async-start(), calls=%async_computation.6 | async-start | bytes 6144000 | tf_op jit(solution)/shard_map/all_gather | solution.py:819
  84.7 65.4 %collective-permute-start.7 = (bf16[320,2560]{1,0:T(8,128)(2,1)}, bf16[320,2560]{1,0:T(8,128)(2,1)}, u32[]{:S(2)}, u32[]{:S(2)}) collective-permute-start(bf16[320,2560]{1,0:T(8,128)(2,1)} %all-gather.7.cloned.1.call-done), channel_id=1, source_target_pairs={{0,8},{8,0},{16,24},{24,16},{1,9},{9,1},{17,25},{25,17},{2,10},{10... | collective-permute-start | bytes 4915208 | tf_op jit(solution)/shard_map/ppermute | solution.py:18
  84.8 70.6 %collective-permute-start.8 = (bf16[320,2560]{1,0:T(8,128)(2,1)}, bf16[320,2560]{1,0:T(8,128)(2,1)}, u32[]{:S(2)}, u32[]{:S(2)}) collective-permute-start(bf16[320,2560]{1,0:T(8,128)(2,1)} %all-gather.7.cloned.1.call-done), channel_id=1, source_target_pairs={{0,16},{8,24},{16,0},{24,8},{1,17},{9,25},{17,1},{25,9},{2,18},{10... | collective-permute-start | bytes 4915208 | tf_op jit(solution)/shard_map/ppermute | solution.py:18
  152.2 52.1 %collective-permute-start.10 = (bf16[160,2560]{1,0:T(8,128)(2,1)}, bf16[160,2560]{1,0:T(8,128)(2,1)S(1)}, u32[]{:S(2)}, u32[]{:S(2)}) collective-permute-start(bf16[160,2560]{1,0:T(8,128)(2,1)} %slice.255), channel_id=1, source_target_pairs={{0,16},{8,24},{16,0},{24,8},{1,17},{9,25},{17,1},{25,9},{2,18},{10... | collective-permute-start | bytes 2457608 | tf_op jit(solution)/shard_map/ppermute | solution.py:18
  157.4 46.8 %collective-permute-start.9 = (bf16[160,2560]{1,0:T(8,128)(2,1)}, bf16[160,2560]{1,0:T(8,128)(2,1)}, u32[]{:S(2)}, u32[]{:S(2)}) collective-permute-start(bf16[160,2560]{1,0:T(8,128)(2,1)} %slice.254), channel_id=1, source_target_pairs={{0,8},{8,0},{16,24},{24,16},{1,9},{9,1},{17,25},{25,17},{2,10},{10... | collective-permute-start | bytes 2457608 | tf_op jit(solution)/shard_map/ppermute | solution.py:18
  158.3 44.0 %collective-permute-start.6 = (bf16[512,256]{1,0:T(8,128)(2,1)}, bf16[512,256]{1,0:T(8,128)(2,1)}, u32[]{:S(2)}, u32[]{:S(2)}) collective-permute-start(bf16[512,256]{1,0:T(8,128)(2,1)} %get-tuple-element.203), channel_id=1, source_target_pairs={{0,2},{2,4},{4,6},{6,0},{1,3},{3,5},{5,7},{7,1},{8,10},{10,12},{12... | collective-permute-start | bytes 786440 | tf_op jit(solution)/shard_map/ppermute | solution.py:870
  162.5 376.7 %reduce-scatter.10.cloned.1.call-start = ((), (), s32[]{:S(2)}) async-start(), calls=%async_computation.8 | async-start | bytes 6553600
  387.5 308.4 %reduce-scatter.8.cloned.1.call-start = ((), (), s32[]{:S(2)}) async-start(), calls=%async_computation.7 | async-start | bytes 12288000 | tf_op jit(solution)/shard_map/reduce_scatter | solution.py:924
  387.5 44.8 %collective-permute-start.20 = (bf16[2560,384]{1,0:T(8,128)(2,1)}, bf16[2560,384]{1,0:T(8,128)(2,1)S(1)}, u32[]{:S(2)}, u32[]{:S(2)}) collective-permute-start(bf16[2560,384]{1,0:T(8,128)(2,1)} %all-gather.5.cloned.1.call-done.refs_0_), channel_id=1, source_target_pairs={{0,8},{8,0},{16,24},{24,16},{1,9},{9,1},{17,25},{25,17},{2,10},{10... | collective-permute-start | bytes 5898248 | tf_op jit(solution)/shard_map/ppermute | solution.py:18
  388.8 44.3 %collective-permute-start.21 = (bf16[2560,384]{1,0:T(8,128)(2,1)}, bf16[2560,384]{1,0:T(8,128)(2,1)}, u32[]{:S(2)}, u32[]{:S(2)}) collective-permute-start(bf16[2560,384]{1,0:T(8,128)(2,1)} %all-gather.5.cloned.1.call-done.refs_0_), channel_id=1, source_target_pairs={{0,16},{8,24},{16,0},{24,8},{1,17},{9,25},{17,1},{25,9},{2,18},{10... | collective-permute-start | bytes 5898248 | tf_op jit(solution)/shard_map/ppermute | solution.py:18
  467.9 346.8 %reduce-scatter.12.cloned.1.call-start = ((), (), s32[]{:S(2)}) async-start(), calls=%async_computation.9 | async-start | bytes 4915200
  541.6 40.8 %collective-permute-start.25 = (bf16[960,640]{1,0:T(8,128)(2,1)}, bf16[960,640]{1,0:T(8,128)(2,1)}, u32[]{:S(2)}, u32[]{:S(2)}) collective-permute-start(bf16[960,640]{1,0:T(8,128)(2,1)} %bitcast.79), channel_id=1, source_target_pairs={{0,8},{8,0},{16,24},{24,16},{1,9},{9,1},{17,25},{25,17},{2,10},{10... | collective-permute-start | bytes 3686408 | tf_op jit(solution)/shard_map/ppermute | solution.py:18
  542.5 39.9 %collective-permute-start.26 = (bf16[960,640]{1,0:T(8,128)(2,1)}, bf16[960,640]{1,0:T(8,128)(2,1)}, u32[]{:S(2)}, u32[]{:S(2)}) collective-permute-start(bf16[960,640]{1,0:T(8,128)(2,1)} %bitcast.80), channel_id=1, source_target_pairs={{0,16},{8,24},{16,0},{24,8},{1,17},{9,25},{17,1},{25,9},{2,18},{10... | collective-permute-start | bytes 3686408 | tf_op jit(solution)/shard_map/ppermute | solution.py:18
  546.6 59.5 %collective-permute-start.28 = (bf16[320,2560]{1,0:T(8,128)(2,1)}, bf16[320,2560]{1,0:T(8,128)(2,1)}, u32[]{:S(2)}, u32[]{:S(2)}) collective-permute-start(bf16[320,2560]{1,0:T(8,128)(2,1)} %pad_maximum_fusion.7), channel_id=1, source_target_pairs={{0,16},{8,24},{16,0},{24,8},{1,17},{9,25},{17,1},{25,9},{2,18},{10... | collective-permute-start | bytes 4915208 | tf_op jit(solution)/shard_map/ppermute | solution.py:18
  548.8 57.3 %collective-permute-start.27 = (bf16[320,2560]{1,0:T(8,128)(2,1)}, bf16[320,2560]{1,0:T(8,128)(2,1)}, u32[]{:S(2)}, u32[]{:S(2)}) collective-permute-start(bf16[320,2560]{1,0:T(8,128)(2,1)} %pad_maximum_fusion.6), channel_id=1, source_target_pairs={{0,8},{8,0},{16,24},{24,16},{1,9},{9,1},{17,25},{25,17},{2,10},{10... | collective-permute-start | bytes 4915208 | tf_op jit(solution)/shard_map/ppermute | solution.py:18
  623.1 70.7 %collective-permute-start.31 = (bf16[256,2560]{1,0:T(8,128)(2,1)}, bf16[256,2560]{1,0:T(8,128)(2,1)}, u32[]{:S(2)}, u32[]{:S(2)}) collective-permute-start(bf16[256,2560]{1,0:T(8,128)(2,1)} %pad_maximum_fusion.11), channel_id=1, source_target_pairs={{0,16},{8,24},{16,0},{24,8},{1,17},{9,25},{17,1},{25,9},{2,18},{10... | collective-permute-start | bytes 3932168 | tf_op jit(solution)/shard_map/ppermute | solution.py:18
  624.8 69.0 %collective-permute-start.30 = (bf16[256,2560]{1,0:T(8,128)(2,1)}, bf16[256,2560]{1,0:T(8,128)(2,1)}, u32[]{:S(2)}, u32[]{:S(2)}) collective-permute-start(bf16[256,2560]{1,0:T(8,128)(2,1)} %pad_maximum_fusion.10), channel_id=1, source_target_pairs={{0,8},{8,0},{16,24},{24,16},{1,9},{9,1},{17,25},{25,17},{2,10},{10... | collective-permute-start | bytes 3932168 | tf_op jit(solution)/shard_map/ppermute | solution.py:18
  729.4 54.8 %collective-permute-start.35 = (bf16[640,1920]{1,0:T(8,128)(2,1)}, bf16[640,1920]{1,0:T(8,128)(2,1)}, u32[]{:S(2)}, u32[]{:S(2)}) collective-permute-start(bf16[640,1920]{1,0:T(8,128)(2,1)} %reduce-scatter.8.cloned.1.call-done.refs_0_), channel_id=1, source_target_pairs={{0,8},{8,0},{16,24},{24,16},{1,9},{9,1},{17,25},{25,17},{2,10},{10... | collective-permute-start | bytes 7372808 | tf_op jit(solution)/shard_map/ppermute | solution.py:18
  729.4 54.7 %collective-permute-start.36 = (bf16[640,1920]{1,0:T(8,128)(2,1)}, bf16[640,1920]{1,0:T(8,128)(2,1)}, u32[]{:S(2)}, u32[]{:S(2)}) collective-permute-start(bf16[640,1920]{1,0:T(8,128)(2,1)} %reduce-scatter.8.cloned.1.call-done.refs_0_), channel_id=1, source_target_pairs={{0,16},{8,24},{16,0},{24,8},{1,17},{9,25},{17,1},{25,9},{2,18},{10... | collective-permute-start | bytes 7372808 | tf_op jit(solution)/shard_map/ppermute | solution.py:18
  794.9 36.1 %collective-permute-start.37 = (bf16[320,1920]{1,0:T(8,128)(2,1)}, bf16[320,1920]{1,0:T(8,128)(2,1)}, u32[]{:S(2)}, u32[]{:S(2)}) collective-permute-start(bf16[320,1920]{1,0:T(8,128)(2,1)} %slice.233), channel_id=1, source_target_pairs={{0,8},{8,0},{16,24},{24,16},{1,9},{9,1},{17,25},{25,17},{2,10},{10... | collective-permute-start | bytes 3686408 | tf_op jit(solution)/shard_map/ppermute | solution.py:18
  809.5 49.0 %collective-permute-start.34 = (bf16[256,2560]{1,0:T(8,128)(2,1)}, bf16[256,2560]{1,0:T(8,128)(2,1)}, u32[]{:S(2)}, u32[]{:S(2)}) collective-permute-start(bf16[256,2560]{1,0:T(8,128)(2,1)} %get-tuple-element.196), channel_id=1, source_target_pairs={{0,1},{1,0},{2,3},{3,2},{4,5},{5,4},{6,7},{7,6},{8,9},{9,8},{10,11... | collective-permute-start | bytes 3932168 | tf_op jit(solution)/shard_map/ppermute | solution.py:22
  (98 other events, 1394.9 us)
Sparse Core Ops, SparseCore 0:
  10.2 38.4 all-gather.6
  50.8 41.9 all-gather.4
  95.0 191.8 all-gather.8
  288.8 92.2 all-gather.10
  387.6 93.3 reduce-scatter.9
  483.8 183.3 reduce-scatter.7
  741.0 73.6 reduce-scatter.11

commit v7 on v6

--- a/solution.py
+++ b/solution.py
@@ -1007,9 +1007,7 @@
     grad_unit_one = my_half(unit_part) + swap(other_half(unit_part))
     layer_half = (hidden_in + scatter_end(ffn_sum, ffn_far)).astype(BF16)
     grad_half = grad_hidden + norm_pull(source, inverse_one, grad_unit_one * gains[0])
-    in_parts, grad_half, last_near = lax.optimization_barrier(
-        (in_parts, grad_half, gather_near(last_sum))
-    )
+    in_parts, last_near = lax.optimization_barrier((in_parts, gather_near(last_sum)))
     last_parts = gather_far(last_sum, last_near)
     layer_out, grad_input = whole_rows(layer_half), whole_rows(grad_half)
     if kernels and square:

time: 924 us -> 923 us (level)
    unnamed x152 -> x154, local copies, waits for them, and re-layouts: 56.6 us -> 57.9 us
  transfers between devices with their start and end apart: 54 -> 54, of which waited for: 18 -> 20; matrix products, arithmetic and copies ran while one was open for 27% -> 27% of each run, Pallas kernels for 42% -> 42%
where the time goes in v7:
time: 923 us; the launch traced here: 912 us
  Pallas kernels  404 us (44%)
  waiting for transfers between devices  142 us (15%)
  local copies, waits for them, and re-layouts  124 us (13%)
  matrix products  92.1 us (10%)
  other arithmetic  76.6 us (8%)
  starting transfers between devices  58.3 us (6%)
  between operations  15.8 us (2%)
    pallas_call x2, Pallas kernels, gather_rows(): pl.pallas_call(rows_kernel, out_shape=jax.ShapeDtypeStruct((8 * half, wid...  102 us
    ppermute x28, waiting for transfers between devices, exchange(): return lax.ppermute(value, 'seq', [(at, at ^ step) for at in range(count)])  85.6 us
    dot_general x4, matrix products, rows_product(): lax.dot_general(left, right, (((0,), (0,)), ((), ())), preferred_element_...  58 us
    unnamed x154, local copies, waits for them, and re-layouts  57.9 us
    pallas_call x2, Pallas kernels, trade(): pl.pallas_call(functools.partial(trade_kernel, to_rows), out_shape=jax.Sh...  54.9 us
    pallas_call x1, Pallas kernels, return_pairs(): pl.pallas_call(functools.partial(return_kernel, steps), out_shape=[jax.Sh...  53.3 us
    pallas_call x1, Pallas kernels, scatter_rows(): pl.pallas_call(sum_kernel, out_shape=jax.ShapeDtypeStruct((half, width),...  50.3 us
    pallas_call x1, Pallas kernels, ffn_back(): pl.pallas_call(ffn_back_kernel, out_shape=(jax.ShapeDtypeStruct((count, 2...  43.2 us
  transfers between devices with their start and end apart: 54, of which 20 were waited for; matrix products, arithmetic and copies ran while one was open for 27% of the time, Pallas kernels for 42%

profile of v7, /device:TPU:9, one launch (start us, length us, event | category | flops | bytes accessed | tf_op | source)
XLA Modules:
  0.0 912.4 jit_solution(9796104136127483668)
XLA Ops:
  32.7 51.9 %gather_rows.2 = bf16[2048,2560]{1,0:T(8,128)(2,1)} custom-call(bf16[256,2560]{1,0:T(8,128)(2,1)} %fusion.3.own_ref), custom_call_target="tpu_custom_call" | custom-call | flops 1000 | bytes 1000 | tf_op jit(solution)/shard_map/gather_rows/pallas_call | solution.py:178
  105.3 34.1 %trade.2 = bf16[512,1536]{1,0:T(8,128)(2,1)} custom-call(bf16[2048,384]{1,0:T(8,128)(2,1)} %copy.33.value_ref), custom_call_target="tpu_custom_call" | custom-call | flops 1000 | bytes 1000 | tf_op jit(solution)/shard_map/trade/pallas_call | solution.py:318
  169.3 15.2 %collective-permute-done.5 = bf16[512,256]{1,0:T(8,128)(2,1)} collective-permute-done((bf16[512,256]{1,0:T(8,128)(2,1)}, bf16[512,256]{1,0:T(8,128)(2,1)}, u32[]{:S(2)}, u32[]{:S(2)}) %collective-permute-start.5) | collective-permute-done | bytes 262176 | tf_op jit(solution)/shard_map/ppermute | solution.py:870
  185.5 16.8 %collective-permute-done.6 = bf16[512,256]{1,0:T(8,128)(2,1)} collective-permute-done((bf16[512,256]{1,0:T(8,128)(2,1)}, bf16[512,256]{1,0:T(8,128)(2,1)}, u32[]{:S(2)}, u32[]{:S(2)}) %collective-permute-start.6) | collective-permute-done | bytes 262176 | tf_op jit(solution)/shard_map/ppermute | solution.py:870
  205.6 8.6 collective-permute-start.11
  222.9 15.4 %attend.1 = (bf16[512,1280]{1,0:T(8,128)(2,1)S(1)}, f32[5,1,512]{2,1,0:T(1,128)S(1)}) custom-call(s32[1]{0:T(128)} %bitcast.pos_ref, bf16[512,1280]{1,0:T(8,128)(2,1)S(1)} %slice.194.q_ref, bf16[2560,256]{1,0:T(8,128)(2,1)S(1)} %get-tuple-element.196.k_ref, bf16[2560,256]{1,0:T(8,128)(2,1)S(1)} %get-tuple-element.195.v_ref), custom_call_target="tpu_custom_call" | custom-call | flops 1000 | bytes 1000 | tf_op jit(solution)/shard_map/attend/pallas_call | solution.py:485
  280.8 50.1 %gather_rows.3.x_ref = bf16[2048,2560]{1,0:T(8,128)(2,1)} custom-call(bf16[256,2560]{1,0:T(8,128)(2,1)} %multiply_convert_fusion.own_ref), custom_call_target="tpu_custom_call" | custom-call | flops 1000 | bytes 1000 | tf_op jit(solution)/shard_map/gather_rows/pallas_call | solution.py:178
  330.9 32.8 %ffn.1 = (bf16[2048,960]{1,0:T(8,128)(2,1)}, bf16[2048,960]{1,0:T(8,128)(2,1)}, bf16[2048,960]{1,0:T(8,128)(2,1)}) custom-call(bf16[2048,2560]{1,0:T(8,128)(2,1)} %gather_rows.3.x_ref, bf16[2560,1920]{1,0:T(8,128)(2,1)} %all-gather.9.cloned.1.call-done.w_ref), custom_call_target="tpu_custom_call" | custom-call | flops 1000 | bytes 1000 | tf_op jit(solution)/shard_map/ffn/pallas_call | solution.py:639
  363.8 15.9 %convolution_convert_fusion.3 = bf16[2560,960]{0,1:T(8,128)(2,1)} fusion(bf16[2048,2560]{1,0:T(8,128)(2,1)} %constant_dynamic-update-slice_fusion.5.c_ref, bf16[2048,960]{1,0:T(8,128)(2,1)} %get-tuple-element.113), kind=kOutput, calls=%fused_computation.4 | convolution fusion | flops 10068787200 | bytes 19333120 | tf_op jit(solution)/shard_map/dot_general | solution.py:80
  389.1 43.2 %ffn_back.1 = (bf16[2048,1920]{1,0:T(8,128)(2,1)}, bf16[2048,2560]{1,0:T(8,128)(2,1)}) custom-call(bf16[2048,2560]{1,0:T(8,128)(2,1)} %constant_dynamic-update-slice_fusion.5.c_ref, bf16[960,2560]{1,0:T(8,128)(2,1)} %all-gather.11.cloned.1.call-done.d_ref, bf16[2048,960]{1,0:T(8,128)(2,1)} %get-tuple-element.99.a_ref, ...), custom_call_target="tpu_custom_call" | custom-call | flops 1000 | bytes 1000 | tf_op jit(solution)/shard_map/ffn_back/pallas_call | solution.py:673
  436.9 28.0 %convolution_convert_fusion = bf16[2560,1920]{1,0:T(8,128)(2,1)} fusion(bf16[2048,2560]{1,0:T(8,128)(2,1)} %gather_rows.3.x_ref, bf16[2048,1920]{1,0:T(8,128)(2,1)} %get-tuple-element.106), kind=kOutput, calls=%fused_computation | convolution fusion | flops 20137574400 | bytes 28180480 | tf_op jit(solution)/shard_map/dot_general | solution.py:80
  472.0 50.3 %scatter_rows.1 = f32[256,2560]{1,0:T(8,128)S(1)} custom-call(bf16[2048,2560]{1,0:T(8,128)(2,1)S(1)} %copy-done.7), custom_call_target="tpu_custom_call" | custom-call | flops 1000 | bytes 1000 | tf_op jit(solution)/shard_map/scatter_rows/pallas_call | solution.py:409
  556.2 26.3 %attend_back.1 = (bf16[512,1280]{1,0:T(8,128)(2,1)S(1)}, f32[2560,256]{1,0:T(8,128)}, bf16[2560,256]{1,0:T(8,128)(2,1)S(1)}) custom-call(s32[2]{0:T(128)S(1)} %pad_add_fusion.pos_ref, bf16[512,1280]{1,0:T(8,128)(2,1)S(1)} %copy-done.4, bf16[512,1280]{1,0:T(8,128)(2,1)S(1)} %convolution_convert_fusion.5.g_ref, bf16[2560,256]{1,0:T(8,128)(2,1)} %copy-done.6, ...), custom_call_target="tpu_custom_call" | custom-call | flops 1000 | bytes 1000 | tf_op jit(solution)/shard_map/attend_back/pallas_call | solution.py:577
  582.6 8.4 fusion.10
  591.0 15.2 %collective-permute-done.28 = bf16[320,2560]{1,0:T(8,128)(2,1)} collective-permute-done((bf16[320,2560]{1,0:T(8,128)(2,1)}, bf16[320,2560]{1,0:T(8,128)(2,1)}, u32[]{:S(2)}, u32[]{:S(2)}) %collective-permute-start.28) | collective-permute-done | bytes 1638432 | tf_op jit(solution)/shard_map/ppermute | solution.py:18
  637.9 53.3 %return_pairs.1 = (f32[512,256]{1,0:T(8,128)S(1)}, bf16[160,2560]{1,0:T(8,128)(2,1)S(1)}, bf16[160,2560]{1,0:T(8,128)(2,1)S(1)}, bf16[480,640]{1,0:T(8,128)(2,1)S(1)}, bf16[480,640]{1,0:T(8,128)(2,1)S(1)}) custom-call(f32[2560,256]{1,0:T(8,128)S(1)} %copy-done.11, bf16[2560,256]{1,0:T(8,128)(2,1)S(1)} %copy-done.15, ...), custom_call_target="tpu_custom_call" | custom-call | flops 1000 | bytes 1000 | tf_op jit(solution)/shard_map/return_pairs/pallas_call | solution.py:269
  700.1 20.8 %trade.3 = bf16[2048,384]{1,0:T(8,128)(2,1)} custom-call(bf16[512,1536]{1,0:T(8,128)(2,1)} %constant_dynamic-update-slice_fusion.13.value_ref.grad_ref), custom_call_target="tpu_custom_call" | custom-call | flops 1000 | bytes 1000 | tf_op jit(solution)/shard_map/trade/pallas_call | solution.py:318
  722.1 8.7 convolution_convert_fusion.4
  747.2 9.6 %unit_grads.1 = f32[512,2560]{1,0:T(8,128)} custom-call(s32[1]{0:T(128)} %bitcast.19.seq_ref, bf16[512,1536]{1,0:T(8,128)(2,1)S(1)} %copy-done.2, bf16[2560,384]{1,0:T(8,128)(2,1)S(1)} %copy-done.13, bf16[2560,384]{1,0:T(8,128)(2,1)S(1)} %copy-done.10, bf16[2560,384]{1,0:T(8,128)(2,1)} %collective-permute-done.21.refs_2_, bf16[2560,384]{1,0:T(8,128)(2,1)S(1)} %copy-done.8), custom_call_target="tpu_custom_call" | custom-call | flops 1000 | bytes 1000 | tf_op jit(solution)/shard_map/unit_grads/pallas_call | solution.py:206
  762.2 13.6 %collective-permute-done.35.refs_1_ = bf16[640,1920]{1,0:T(8,128)(2,1)} collective-permute-done((bf16[640,1920]{1,0:T(8,128)(2,1)}, bf16[640,1920]{1,0:T(8,128)(2,1)}, u32[]{:S(2)}, u32[]{:S(2)}) %collective-permute-start.35) | collective-permute-done | bytes 2457632 | tf_op jit(solution)/shard_map/ppermute | solution.py:18
  784.7 10.8 %collective-permute-done.32 = bf16[128,2560]{1,0:T(8,128)(2,1)S(1)} collective-permute-done((bf16[128,2560]{1,0:T(8,128)(2,1)S(1)}, bf16[128,2560]{1,0:T(8,128)(2,1)S(1)}, u32[]{:S(2)}, u32[]{:S(2)}) %collective-permute-start.32) | collective-permute-done | bytes 655392 | tf_op jit(solution)/shard_map/ppermute | solution.py:18
  818.1 15.4 %collective-permute-done.39 = bf16[320,1920]{1,0:T(8,128)(2,1)S(1)} collective-permute-done((bf16[320,1920]{1,0:T(8,128)(2,1)}, bf16[320,1920]{1,0:T(8,128)(2,1)S(1)}, u32[]{:S(2)}, u32[]{:S(2)}) %collective-permute-start.39) | collective-permute-done | bytes 1228832 | tf_op jit(solution)/shard_map/ppermute | solution.py:18
  842.2 10.6 %collective-permute-done.41 = bf16[640,704]{0,1:T(8,128)(2,1)} collective-permute-done((bf16[640,704]{0,1:T(8,128)(2,1)S(1)}, bf16[640,704]{0,1:T(8,128)(2,1)}, u32[]{:S(2)}, u32[]{:S(2)}) %collective-permute-start.41) | collective-permute-done | bytes 901152 | tf_op jit(solution)/shard_map/ppermute | solution.py:18
  867.2 16.2 %join_columns.1 = (f32[640,3840]{1,0:T(8,128)}, f32[640,3840]{1,0:T(8,128)}, f32[640,1]{1,0:T(8,128)S(1)}) custom-call(s32[1]{0:T(128)} %bitcast.19.seq_ref, bf16[640,1920]{1,0:T(8,128)(2,1)S(1)} %copy-done.12, bf16[640,1920]{1,0:T(8,128)(2,1)} %collective-permute-done.35.refs_1_, bf16[640,1920]{1,0:T(8,128)(2,1)} %collective-permute-done.36.refs_2_, ...), custom_call_target="tpu_custom_call" | custom-call | flops 1000 | bytes 1000 | tf_op jit(solution)/shard_map/join_columns/pallas_call | solution.py:719
  (404 shorter events, 325.3 us)
Async XLA Ops:
  7.2 77.5 %all-gather.7.cloned.1.call-start = ((), (), s32[]{:S(2)}) async-start(), calls=%async_computation.4 | async-start | bytes 2048000 | tf_op jit(solution)/shard_map/all_gather | solution.py:827
  9.4 83.4 %all-gather.5.cloned.1.call-start = ((), (), s32[]{:S(2)}) async-start(), calls=%async_computation.3 | async-start | bytes 2457600 | tf_op jit(solution)/shard_map/all_gather | solution.py:808
  12.2 318.7 %all-gather.9.cloned.1.call-start = ((), (), s32[]{:S(2)}) async-start(), calls=%async_computation.5 | async-start | bytes 12288000 | tf_op jit(solution)/shard_map/all_gather | solution.py:818
  22.9 366.2 %all-gather.11.cloned.1.call-start = ((), (), s32[]{:S(2)}) async-start(), calls=%async_computation.6 | async-start | bytes 6144000 | tf_op jit(solution)/shard_map/all_gather | solution.py:819
  84.7 65.4 %collective-permute-start.7 = (bf16[320,2560]{1,0:T(8,128)(2,1)}, bf16[320,2560]{1,0:T(8,128)(2,1)}, u32[]{:S(2)}, u32[]{:S(2)}) collective-permute-start(bf16[320,2560]{1,0:T(8,128)(2,1)} %all-gather.7.cloned.1.call-done), channel_id=1, source_target_pairs={{0,8},{8,0},{16,24},{24,16},{1,9},{9,1},{17,25},{25,17},{2,10},{10... | collective-permute-start | bytes 4915208 | tf_op jit(solution)/shard_map/ppermute | solution.py:18
  84.8 70.6 %collective-permute-start.8 = (bf16[320,2560]{1,0:T(8,128)(2,1)}, bf16[320,2560]{1,0:T(8,128)(2,1)}, u32[]{:S(2)}, u32[]{:S(2)}) collective-permute-start(bf16[320,2560]{1,0:T(8,128)(2,1)} %all-gather.7.cloned.1.call-done), channel_id=1, source_target_pairs={{0,16},{8,24},{16,0},{24,8},{1,17},{9,25},{17,1},{25,9},{2,18},{10... | collective-permute-start | bytes 4915208 | tf_op jit(solution)/shard_map/ppermute | solution.py:18
  152.2 52.1 %collective-permute-start.10 = (bf16[160,2560]{1,0:T(8,128)(2,1)}, bf16[160,2560]{1,0:T(8,128)(2,1)S(1)}, u32[]{:S(2)}, u32[]{:S(2)}) collective-permute-start(bf16[160,2560]{1,0:T(8,128)(2,1)} %slice.255), channel_id=1, source_target_pairs={{0,16},{8,24},{16,0},{24,8},{1,17},{9,25},{17,1},{25,9},{2,18},{10... | collective-permute-start | bytes 2457608 | tf_op jit(solution)/shard_map/ppermute | solution.py:18
  157.4 46.8 %collective-permute-start.9 = (bf16[160,2560]{1,0:T(8,128)(2,1)}, bf16[160,2560]{1,0:T(8,128)(2,1)}, u32[]{:S(2)}, u32[]{:S(2)}) collective-permute-start(bf16[160,2560]{1,0:T(8,128)(2,1)} %slice.254), channel_id=1, source_target_pairs={{0,8},{8,0},{16,24},{24,16},{1,9},{9,1},{17,25},{25,17},{2,10},{10... | collective-permute-start | bytes 2457608 | tf_op jit(solution)/shard_map/ppermute | solution.py:18
  158.3 44.0 %collective-permute-start.6 = (bf16[512,256]{1,0:T(8,128)(2,1)}, bf16[512,256]{1,0:T(8,128)(2,1)}, u32[]{:S(2)}, u32[]{:S(2)}) collective-permute-start(bf16[512,256]{1,0:T(8,128)(2,1)} %get-tuple-element.201), channel_id=1, source_target_pairs={{0,2},{2,4},{4,6},{6,0},{1,3},{3,5},{5,7},{7,1},{8,10},{10,12},{12... | collective-permute-start | bytes 786440 | tf_op jit(solution)/shard_map/ppermute | solution.py:870
  162.5 376.8 %reduce-scatter.10.cloned.1.call-start = ((), (), s32[]{:S(2)}) async-start(), calls=%async_computation.8 | async-start | bytes 6553600
  387.5 308.4 %reduce-scatter.8.cloned.1.call-start = ((), (), s32[]{:S(2)}) async-start(), calls=%async_computation.7 | async-start | bytes 12288000 | tf_op jit(solution)/shard_map/reduce_scatter | solution.py:924
  387.6 44.8 %collective-permute-start.20 = (bf16[2560,384]{1,0:T(8,128)(2,1)}, bf16[2560,384]{1,0:T(8,128)(2,1)S(1)}, u32[]{:S(2)}, u32[]{:S(2)}) collective-permute-start(bf16[2560,384]{1,0:T(8,128)(2,1)} %all-gather.5.cloned.1.call-done.refs_0_), channel_id=1, source_target_pairs={{0,8},{8,0},{16,24},{24,16},{1,9},{9,1},{17,25},{25,17},{2,10},{10... | collective-permute-start | bytes 5898248 | tf_op jit(solution)/shard_map/ppermute | solution.py:18
  388.8 44.3 %collective-permute-start.21 = (bf16[2560,384]{1,0:T(8,128)(2,1)}, bf16[2560,384]{1,0:T(8,128)(2,1)}, u32[]{:S(2)}, u32[]{:S(2)}) collective-permute-start(bf16[2560,384]{1,0:T(8,128)(2,1)} %all-gather.5.cloned.1.call-done.refs_0_), channel_id=1, source_target_pairs={{0,16},{8,24},{16,0},{24,8},{1,17},{9,25},{17,1},{25,9},{2,18},{10... | collective-permute-start | bytes 5898248 | tf_op jit(solution)/shard_map/ppermute | solution.py:18
  468.0 347.0 %reduce-scatter.12.cloned.1.call-start = ((), (), s32[]{:S(2)}) async-start(), calls=%async_computation.9 | async-start | bytes 4915200
  541.7 40.8 %collective-permute-start.25 = (bf16[960,640]{1,0:T(8,128)(2,1)}, bf16[960,640]{1,0:T(8,128)(2,1)}, u32[]{:S(2)}, u32[]{:S(2)}) collective-permute-start(bf16[960,640]{1,0:T(8,128)(2,1)} %bitcast.78), channel_id=1, source_target_pairs={{0,8},{8,0},{16,24},{24,16},{1,9},{9,1},{17,25},{25,17},{2,10},{10... | collective-permute-start | bytes 3686408 | tf_op jit(solution)/shard_map/ppermute | solution.py:18
  542.6 39.9 %collective-permute-start.26 = (bf16[960,640]{1,0:T(8,128)(2,1)}, bf16[960,640]{1,0:T(8,128)(2,1)}, u32[]{:S(2)}, u32[]{:S(2)}) collective-permute-start(bf16[960,640]{1,0:T(8,128)(2,1)} %bitcast.79), channel_id=1, source_target_pairs={{0,16},{8,24},{16,0},{24,8},{1,17},{9,25},{17,1},{25,9},{2,18},{10... | collective-permute-start | bytes 3686408 | tf_op jit(solution)/shard_map/ppermute | solution.py:18
  546.7 59.5 %collective-permute-start.28 = (bf16[320,2560]{1,0:T(8,128)(2,1)}, bf16[320,2560]{1,0:T(8,128)(2,1)}, u32[]{:S(2)}, u32[]{:S(2)}) collective-permute-start(bf16[320,2560]{1,0:T(8,128)(2,1)} %pad_maximum_fusion.7), channel_id=1, source_target_pairs={{0,16},{8,24},{16,0},{24,8},{1,17},{9,25},{17,1},{25,9},{2,18},{10... | collective-permute-start | bytes 4915208 | tf_op jit(solution)/shard_map/ppermute | solution.py:18
  548.8 57.4 %collective-permute-start.27 = (bf16[320,2560]{1,0:T(8,128)(2,1)}, bf16[320,2560]{1,0:T(8,128)(2,1)}, u32[]{:S(2)}, u32[]{:S(2)}) collective-permute-start(bf16[320,2560]{1,0:T(8,128)(2,1)} %pad_maximum_fusion.6), channel_id=1, source_target_pairs={{0,8},{8,0},{16,24},{24,16},{1,9},{9,1},{17,25},{25,17},{2,10},{10... | collective-permute-start | bytes 4915208 | tf_op jit(solution)/shard_map/ppermute | solution.py:18
  623.1 70.7 %collective-permute-start.31 = (bf16[256,2560]{1,0:T(8,128)(2,1)}, bf16[256,2560]{1,0:T(8,128)(2,1)}, u32[]{:S(2)}, u32[]{:S(2)}) collective-permute-start(bf16[256,2560]{1,0:T(8,128)(2,1)} %pad_maximum_fusion.11), channel_id=1, source_target_pairs={{0,16},{8,24},{16,0},{24,8},{1,17},{9,25},{17,1},{25,9},{2,18},{10... | collective-permute-start | bytes 3932168 | tf_op jit(solution)/shard_map/ppermute | solution.py:18
  624.9 68.9 %collective-permute-start.30 = (bf16[256,2560]{1,0:T(8,128)(2,1)}, bf16[256,2560]{1,0:T(8,128)(2,1)}, u32[]{:S(2)}, u32[]{:S(2)}) collective-permute-start(bf16[256,2560]{1,0:T(8,128)(2,1)} %pad_maximum_fusion.10), channel_id=1, source_target_pairs={{0,8},{8,0},{16,24},{24,16},{1,9},{9,1},{17,25},{25,17},{2,10},{10... | collective-permute-start | bytes 3932168 | tf_op jit(solution)/shard_map/ppermute | solution.py:18
  720.9 54.8 %collective-permute-start.35 = (bf16[640,1920]{1,0:T(8,128)(2,1)}, bf16[640,1920]{1,0:T(8,128)(2,1)}, u32[]{:S(2)}, u32[]{:S(2)}) collective-permute-start(bf16[640,1920]{1,0:T(8,128)(2,1)} %reduce-scatter.8.cloned.1.call-done.refs_0_), channel_id=1, source_target_pairs={{0,8},{8,0},{16,24},{24,16},{1,9},{9,1},{17,25},{25,17},{2,10},{10... | collective-permute-start | bytes 7372808 | tf_op jit(solution)/shard_map/ppermute | solution.py:18
  721.0 54.7 %collective-permute-start.36 = (bf16[640,1920]{1,0:T(8,128)(2,1)}, bf16[640,1920]{1,0:T(8,128)(2,1)}, u32[]{:S(2)}, u32[]{:S(2)}) collective-permute-start(bf16[640,1920]{1,0:T(8,128)(2,1)} %reduce-scatter.8.cloned.1.call-done.refs_0_), channel_id=1, source_target_pairs={{0,16},{8,24},{16,0},{24,8},{1,17},{9,25},{17,1},{25,9},{2,18},{10... | collective-permute-start | bytes 7372808 | tf_op jit(solution)/shard_map/ppermute | solution.py:18
  801.0 58.7 %collective-permute-start.38 = (f32[256,2560]{1,0:T(8,128)}, f32[256,2560]{1,0:T(8,128)}, u32[]{:S(2)}, u32[]{:S(2)}) collective-permute-start(f32[256,2560]{1,0:T(8,128)} %get-tuple-element.193), channel_id=1, source_target_pairs={{0,1},{1,0},{2,3},{3,2},{4,5},{5,4},{6,7},{7,6},{8,9},{9,8},{10,11... | collective-permute-start | bytes 7864328 | tf_op jit(solution)/shard_map/ppermute | solution.py:22
  816.9 36.0 %collective-permute-start.41 = (bf16[640,704]{0,1:T(8,128)(2,1)S(1)}, bf16[640,704]{0,1:T(8,128)(2,1)}, u32[]{:S(2)}, u32[]{:S(2)}) collective-permute-start(bf16[640,704]{0,1:T(8,128)(2,1)S(1)} %copy.45), channel_id=1, source_target_pairs={{0,8},{8,0},{16,24},{24,16},{1,9},{9,1},{17,25},{25,17},{2,10},{10... | collective-permute-start | bytes 2703368 | tf_op jit(solution)/shard_map/ppermute | solution.py:18
  (99 other events, 1353.0 us)
Sparse Core Ops, SparseCore 0:
  10.2 38.4 all-gather.6
  50.8 41.9 all-gather.4
  95.0 191.8 all-gather.8
  288.8 92.2 all-gather.10
  387.6 93.3 reduce-scatter.9
  483.9 181.2 reduce-scatter.7
  741.3 73.6 reduce-scatter.11
